TPU v7x, 32 devices: a whole 2x2x4 slice. The times are simulated.
32 devices in a mesh: clip: 2 (over y), frame: 4 (over z), track: 4 (over x, core).
Axes of the slice: x: 2, y: 2, z: 4, core: 2. Of those that a mesh axis runs over, the one named last changes fastest.
Arguments:
- feature_maps: bfloat16 [8, 4096, 256], P(('clip', 'frame')), parts along dimension 0, may hold values from -6 to 6
- query_frame: int32 [1024], P('clip'), parts along dimension 0, may hold values from 0 to 3
- query_row: int32 [1024], P('clip'), parts along dimension 0, may hold values from 0 to 63
- query_col: int32 [1024], P('clip'), parts along dimension 0, may hold values from 0 to 63
- track_order: int32 [1024], P('clip'), parts along dimension 0, may hold values from 0 to 511, each once
- conv_weight: float32 [16, 9], replicated, may hold values from -2 to 2
- conv_bias: float32 [16], replicated, may hold values from -2 to 2
- head_weight: float32 [16], replicated, may hold values from -2 to 2
- mix_in: bfloat16 [256, 1024], replicated, may hold values from -0.375 to 0.375
- temporal_taps: float32 [3, 1024], replicated, may hold values from -2.5 to 2.5
- mix_gain: float32 [1024], replicated, may hold values from 0.25 to 1.75
- mix_out: bfloat16 [1024, 3], replicated, may hold values from -0.1875 to 0.1875
Outputs:
- estimates: float32 [1024, 3, 4], P(('clip', 'frame', 'track')), parts along dimension 0
There are 2 independent parts, one for each index of `clip`. A program takes and returns all parts, laid end to end along the dimension named above; an argument that names none is the same for every part. Nothing has to cross between parts.
Inputs may be any that keep to these rules, and one draw needn't show every extreme that they name: `track_order`: each track appears in exactly one slot.
All inputs are finite; a program needn't handle non-finite values.
Results may differ from a plain program's by a relative error of at most 0.0053.
Values may be sent and summed in bfloat16 or wider, within the bound.
No kernel may reach another device: no remote copies, remote signals or barrier semaphores. Data moves between devices by JAX's collectives and lax.ppermute only.
A program may use at most 64 MiB of HBM per device.

v0:
```python
import math

import jax
import jax.numpy as jnp
from jax import lax
from jax.sharding import PartitionSpec as P

GRID_H = 64
GRID_W = 64


def padded_2(block, sides, width):
    for axis, dim in sides:
        count = lax.axis_size(axis)
        forward = [(i, i + 1) for i in range(count - 1)]
        backward = [(target, source) for source, target in forward]
        low = lax.ppermute(
            lax.slice_in_dim(block, block.shape[dim] - width, None, axis=dim), axis, forward
        )
        high = lax.ppermute(lax.slice_in_dim(block, 0, width, axis=dim), axis, backward)
        block = jnp.concatenate([low, block, high], axis=dim)
    return block


def conv_logits(cost, conv_weight, conv_bias, head_weight):
    height, width = (cost.shape[1], cost.shape[2])
    padded = jnp.pad(cost, ((0, 0), (1, 1), (1, 1)))
    logit = jnp.zeros(cost.shape, jnp.float32)
    for channel in range(conv_weight.shape[0]):
        acc = jnp.zeros(cost.shape, jnp.float32) + conv_bias[channel]
        for tap in range(9):
            acc = (
                acc
                + conv_weight[channel, tap]
                * padded[:, tap // 3 : tap // 3 + height, tap % 3 : tap % 3 + width]
            )
        logit = logit + head_weight[channel] * jax.nn.relu(acc)
    return logit


def block_terms(qblock, maps, conv_weight, conv_bias, head_weight, row_pos, col_pos):
    cost = lax.dot_general(
        qblock, maps, (((1,), (1,)), ((), ())), preferred_element_type=jnp.float32
    )
    cost = cost * (1.0 / math.sqrt(maps.shape[1]))
    logit = conv_logits(
        cost.reshape(cost.shape[0], GRID_H, GRID_W), conv_weight, conv_bias, head_weight
    )
    heat = jax.nn.softmax(logit.reshape(cost.shape), axis=-1)
    row_est = jnp.sum(heat * row_pos, axis=-1).astype(jnp.bfloat16)
    col_est = jnp.sum(heat * col_pos, axis=-1).astype(jnp.bfloat16)
    sampled = jnp.dot(heat.astype(jnp.bfloat16), maps, preferred_element_type=jnp.float32).astype(
        jnp.bfloat16
    )
    return (sampled, row_est, col_est)


def temporal_mix(extended, temporal_taps, mix_gain, mix_out):
    mixed = (
        temporal_taps[0] * extended[:, :-2]
        + temporal_taps[1] * extended[:, 1:-1]
        + temporal_taps[2] * extended[:, 2:]
    )
    normed = mixed * lax.rsqrt(jnp.mean(mixed * mixed, axis=-1, keepdims=True) + 1e-06) * mix_gain
    hidden = jax.nn.gelu(normed).astype(jnp.bfloat16)
    rows, frames_here = (hidden.shape[0], hidden.shape[1])
    delta = jnp.dot(
        hidden.reshape(rows * frames_here, hidden.shape[2]),
        mix_out,
        preferred_element_type=jnp.float32,
    )
    return delta.reshape(rows, frames_here, 3)


def assemble(row_est, col_est, delta):
    return jnp.stack(
        [
            row_est.astype(jnp.float32) + delta[:, :, 0],
            col_est.astype(jnp.float32) + delta[:, :, 1],
            delta[:, :, 2],
        ],
        axis=1,
    )


def project(sampled, mix_in):
    rows, frames_here, chan = sampled.shape
    projected = jnp.dot(
        sampled.reshape(rows * frames_here, chan), mix_in, preferred_element_type=jnp.float32
    )
    return projected.reshape(rows, frames_here, mix_in.shape[1])


def on_device(
    feature_maps,
    query_frame,
    query_row,
    query_col,
    track_order,
    conv_weight,
    conv_bias,
    head_weight,
    mix_in,
    temporal_taps,
    mix_gain,
    mix_out,
):
    frame_count = lax.axis_size("frame")
    track_count = lax.axis_size("track")
    frame_here = lax.axis_index("frame")
    track_here = lax.axis_index("track")
    f_dev, pixels, chan = feature_maps.shape
    total = track_order.shape[0]
    tr_dev = total // track_count
    sub_rows = tr_dev // frame_count
    slots = (
        jnp.arange(frame_count, dtype=jnp.int32)[:, None] * track_count + track_here
    ) * sub_rows
    slots = (slots + jnp.arange(sub_rows, dtype=jnp.int32)[None, :]).reshape(tr_dev)
    tracks = track_order[slots]
    local_frame = query_frame[tracks] - frame_here * f_dev
    owned = (local_frame >= 0) & (local_frame < f_dev)
    pixel_ids = query_row[tracks] * GRID_W + query_col[tracks]
    flat = jnp.clip(local_frame, 0, f_dev - 1) * pixels + pixel_ids
    picks = feature_maps.reshape(f_dev * pixels, chan)[flat]
    partial_value = jnp.where(owned[:, None], picks, jnp.zeros((), picks.dtype))
    queries = lax.psum(partial_value, "frame").astype(jnp.float32).astype(jnp.bfloat16)
    positions = jnp.arange(pixels, dtype=jnp.int32)
    row_pos = (positions // GRID_W).astype(jnp.float32) / (GRID_H - 1)
    col_pos = (positions % GRID_W).astype(jnp.float32) / (GRID_W - 1)
    blk = min(tr_dev, 64)
    blocks = tr_dev // blk
    grouped = queries.reshape(blocks, blk, chan)
    sampled_list, row_list, col_list = ([], [], [])
    maps = feature_maps[0]

    def per_block(qblock):
        return block_terms(qblock, maps, conv_weight, conv_bias, head_weight, row_pos, col_pos)

    sampled_f, row_f, col_f = lax.map(per_block, grouped)
    sampled_list.append(sampled_f.reshape(tr_dev, chan))
    row_list.append(row_f.reshape(tr_dev))
    col_list.append(col_f.reshape(tr_dev))
    sampled = jnp.stack(sampled_list, axis=1)
    row_est = jnp.stack(row_list, axis=1)
    col_est = jnp.stack(col_list, axis=1)
    rims = padded_2(sampled, (("frame", 1),), 1)
    projected = project(rims, mix_in)
    global_frame = frame_here * f_dev - 1 + jnp.arange(f_dev + 2, dtype=jnp.int32)
    valid = (global_frame >= 0) & (global_frame < frame_count * f_dev)
    extended = jnp.where(valid[None, :, None], projected, 0.0)
    delta = temporal_mix(extended, temporal_taps, mix_gain, mix_out)
    local_est = assemble(row_est, col_est, delta).reshape(frame_count, sub_rows, 3, f_dev)
    gathered = lax.all_to_all(local_est, "frame", split_axis=0, concat_axis=3, tiled=True)
    return gathered.reshape(sub_rows, 3, frame_count * f_dev)


def solution(mesh):
    placed = (
        P(("clip", "frame"), None, None),
        P("clip"),
        P("clip"),
        P("clip"),
        P("clip"),
        P(),
        P(),
        P(),
        P(),
        P(),
        P(),
        P(),
    )
    return jax.shard_map(
        on_device,
        mesh=mesh,
        in_specs=placed,
        out_specs=P(("clip", "frame", "track"), None, None),
        check_vma=False,
    )
```

profile of v0, /device:TPU:0, one launch (start us, length us, event | category | flops | bytes accessed | tf_op | source)
XLA Modules:
  0.0 403.0 jit_solution(6857952410239867091)
XLA Ops:
  6.8 1.6 gather_fusion
  8.4 1.6 gather_fusion.1
  10.1 1.6 gather_fusion.2
  11.7 1.6 gather_fusion.3
  13.4 2.6 gather_fusion.4
  16.0 0.7 broadcast_select_fusion
  16.8 37.1 %all-reduce.3.cloned.1.call-done = bf16[2,64,256]{2,1,0:T(8,128)(2,1)} async-done(((bf16[2,64,256]{2,1,0:T(8,128)(2,1)}), bf16[2,64,256]{2,1,0:T(8,128)(2,1)}) %all-reduce.3.cloned.1.call-update) | async-done | bytes 65552 | tf_op jit(solution)/shard_map/psum | solution.py:127
  53.9 322.9 %while.17 = (s32[]{:T(128)}, bf16[2,64,256]{2,1,0:T(8,128)(2,1)S(1)}, bf16[2,64]{1,0:T(2,128)(2,1)S(1)}, bf16[2,64]{1,0:T(2,128)(2,1)S(1)}, f32[16]{0:T(128)S(1)...) while((s32[]{:T(128)}, ...), condition=%wide.region_6.7_spmd.clone, body=%wide.region_1.6_spmd.clone.sunk | while | flops 359751424 | bytes 14882489 | solution.py:140
  53.9 0.7 fusion.90
  54.7 0.7 fusion.91
  55.4 0.7 fusion.92
  56.1 0.7 fusion.93
  56.9 0.7 fusion.94
  57.6 0.7 fusion.95
  58.3 0.7 fusion.87
  59.0 0.7 fusion.96
  59.7 0.7 fusion.88
  60.4 0.7 fusion.89
  61.1 2.4 convolution_multiply_fusion.2
  63.5 2.2 reshape.346
  65.7 142.6 %fusion.97 = (f32[64]{0:T(128)S(1)}, f32[64,64,64]{2,1,0:T(8,128)S(1)}) fusion(f32[]{:T(128)} %bitcast.408, f32[]{:T(128)} %bitcast.409, f32[]{:T(128)} %bitcast.410, f32[]{:T(128)} %bitcast.411, f32[64,64,64]{2,1,0:T(8,128)} %reshape.346, f32[]{:T(128)} %bitcast.412, f32[]{:T(128)} %bitcast.413, f32[]{:T(128)} %bitcast.414, f32[]{:T(128)} %bitcast.415, ...), kind=kLoop, calls=%fused_computation.97.clone.1 | loop fusion | flops 88080320 | bytes 2098112 | tf_op jit(solution)/shard_map/while/body/eval_jaxpr/reduce_max | solution.py:49
  208.3 1.0 fusion.98
  209.5 1.8 multiply_reduce_fusion.4
  211.3 1.6 reshape.347
  212.9 2.4 fusion.99
  215.4 0.7 fusion.90
  216.1 0.7 fusion.91
  216.9 0.7 fusion.92
  217.6 0.7 fusion.93
  218.3 0.7 fusion.94
  219.0 0.7 fusion.95
  219.7 0.7 fusion.87
  220.5 0.7 fusion.96
  221.2 0.7 fusion.88
  221.9 0.7 fusion.89
  222.6 2.4 convolution_multiply_fusion.2
  225.0 2.2 reshape.346
  227.2 142.6 %fusion.97 = (f32[64]{0:T(128)S(1)}, f32[64,64,64]{2,1,0:T(8,128)S(1)}) fusion(f32[]{:T(128)} %bitcast.408, f32[]{:T(128)} %bitcast.409, f32[]{:T(128)} %bitcast.410, f32[]{:T(128)} %bitcast.411, f32[64,64,64]{2,1,0:T(8,128)} %reshape.346, f32[]{:T(128)} %bitcast.412, f32[]{:T(128)} %bitcast.413, f32[]{:T(128)} %bitcast.414, f32[]{:T(128)} %bitcast.415, ...), kind=kLoop, calls=%fused_computation.97.clone.1 | loop fusion | flops 88080320 | bytes 2098112 | tf_op jit(solution)/shard_map/while/body/eval_jaxpr/reduce_max | solution.py:49
  369.7 1.0 fusion.98
  370.9 1.8 multiply_reduce_fusion.4
  372.8 1.6 reshape.347
  374.4 2.4 fusion.99
  376.8 3.3 collective-permute-start
  380.2 1.3 collective-permute-start.1
  381.7 0.4 collective-permute-done
  382.1 4.3 %collective-permute-done.1 = bf16[128,1,256]{2,0,1:T(8,128)(2,1)S(1)} collective-permute-done((bf16[128,1,256]{2,0,1:T(8,128)(2,1)S(1)}, bf16[128,1,256]{2,0,1:T(8,128)(2,1)S(1)}, u32[]{:S(2)}, u32[]{:S(2)}) %collective-permute-start.1) | collective-permute-done | bytes 65568 | tf_op jit(solution)/shard_map/ppermute | solution.py:20
  387.6 7.9 %all_to_all.15 = f32[4,32,3,1]{1,3,2,0:T(1,128)S(1)} all-to-all(f32[4,32,3,1]{1,3,2,0:T(1,128)S(1)} %copy.15), channel_id=1, replica_groups=mesh['clip'=2,'frame'=4,'track'=4] {'frame'}, dimensions={0} | all-to-all | bytes 3072 | tf_op jit(solution)/shard_map/all_to_all | solution.py:154
  395.6 0.6 copy.18
  (55 shorter events, 2.2 us)
Async XLA Ops:
  6.5 379.8 %copy-start = (bf16[256,1024]{1,0:T(8,128)(2,1)S(1)}, bf16[256,1024]{1,0:T(8,128)(2,1)}, u32[]{:S(2)}) copy-start(bf16[256,1024]{1,0:T(8,128)(2,1)} %param.22) | copy-start | bytes 1572868
  6.5 10.2 %copy-start.4 = (f32[3,1024]{1,0:T(4,128)S(1)}, f32[3,1024]{1,0:T(4,128)}, u32[]{:S(2)}) copy-start(f32[3,1024]{1,0:T(4,128)} %param.23) | copy-start | bytes 36868
  6.5 47.4 %copy-start.1 = (f32[16,9]{1,0:T(8,128)S(1)}, f32[16,9]{1,0:T(8,128)}, u32[]{:S(2)}) copy-start(f32[16,9]{1,0:T(8,128)} %param.19) | copy-start | bytes 1732
  6.5 47.4 %copy-start.3 = (f32[16]{0:T(128)S(1)}, f32[16]{0:T(128)}, u32[]{:S(2)}) copy-start(f32[16]{0:T(128)} %param.20) | copy-start | bytes 196
  6.5 47.4 %copy-start.2 = (f32[16]{0:T(128)S(1)}, f32[16]{0:T(128)}, u32[]{:S(2)}) copy-start(f32[16]{0:T(128)} %param.21) | copy-start | bytes 196
  6.5 47.4 %all-reduce.3.cloned.1.call-start = ((), (), s32[]{:S(2)}) async-start(), calls=%async_computation.1 | async-start | bytes 131072 | tf_op jit(solution)/shard_map/psum | solution.py:127
  376.8 5.2 %collective-permute-start = (bf16[128,1,256]{2,0,1:T(8,128)(2,1)S(1)}, bf16[128,1,256]{2,0,1:T(8,128)(2,1)S(1)}, u32[]{:S(2)}, u32[]{:S(2)}) collective-permute-start(bf16[128,1,256]{2,0,1:T(8,128)(2,1)S(1)} %bitcast.589), channel_id=1, source_target_pairs={{0,4},{4,8},{8,12},{1,5},{5,9},{9,13},{2,6},{6,10},{10,14},{3,7},{... | collective-permute-start | bytes 196616 | tf_op jit(solution)/shard_map/ppermute | solution.py:17
  380.2 6.2 %collective-permute-start.1 = (bf16[128,1,256]{2,0,1:T(8,128)(2,1)S(1)}, bf16[128,1,256]{2,0,1:T(8,128)(2,1)S(1)}, u32[]{:S(2)}, u32[]{:S(2)}) collective-permute-start(bf16[128,1,256]{2,0,1:T(8,128)(2,1)S(1)} %bitcast.590), channel_id=1, source_target_pairs={{4,0},{8,4},{12,8},{5,1},{9,5},{13,9},{6,2},{10,6},{14,10},{7,3},{... | collective-permute-start | bytes 196616 | tf_op jit(solution)/shard_map/ppermute | solution.py:20
  381.7 5.3 %copy-start.5 = (bf16[1024,3]{0,1:T(4,128)(2,1)S(1)}, bf16[1024,3]{0,1:T(4,128)(2,1)}, u32[]{:S(2)}) copy-start(bf16[1024,3]{0,1:T(4,128)(2,1)} %param.25) | copy-start | bytes 18436
  381.7 5.3 %copy-start.6 = (f32[1024]{0:T(1024)S(1)}, f32[1024]{0:T(1024)}, u32[]{:S(2)}) copy-start(f32[1024]{0:T(1024)} %param.24) | copy-start | bytes 12292
Sparse Core Ops, SparseCore 0:
  16.9 37.0 all-reduce.2
where the time goes:
time: 406 us; the launch traced here: 403 us
  other arithmetic  292 us (72%)
  waiting for transfers between devices  41.8 us (10%)
  local copies, waits for them, and re-layouts  32.8 us (8%)
  between operations  13.5 us (3%)
  matrix products  10.4 us (3%)
  blocking collectives  7.93 us (2%)
  starting transfers between devices  4.66 us (1%)
    reduce_max x2, other arithmetic, block_terms(): heat = jax.nn.softmax(logit.reshape(cost.shape), axis=-1)  285 us
    psum x1, waiting for transfers between devices, on_device(): lax.psum(partial_value, 'frame').astype(jnp.float32).astype(jnp.bfloat16)  37.1 us
    slice x16, local copies, waits for them, and re-layouts, conv_logits(): conv_weight[channel, tap]  11.5 us
  transfers between devices with their start and end apart: 3, of which 3 were waited for; matrix products, arithmetic and copies ran while one was open for 0% of the time, Pallas kernels for 0%

commit v1 on v0

v1 whole, which is shorter than its diff:
```python
import functools
import math

import jax
import jax.numpy as jnp
from jax import lax
from jax.experimental import pallas as pl
from jax.experimental.pallas import tpu as pltpu
from jax.sharding import PartitionSpec as P

GRID_H = 64
GRID_W = 64
TILE = 16
KDIM = 256
ROWS_PAD = GRID_H + 4
LANES = 128

VMEM_SPEC = pl.BlockSpec(memory_space=pltpu.VMEM)
SMEM_SPEC = pl.BlockSpec(memory_space=pltpu.SMEM)
F32 = jnp.float32
BF16 = jnp.bfloat16


def iota(shape, dim):
    return lax.broadcasted_iota(jnp.int32, shape, dim)


def pick_kernel(frame_ref, tracks_ref, qf_ref, qr_ref, qc_ref, maps_ref, out_ref):
    total = qf_ref.shape[1]
    slots = tracks_ref.shape[1]
    pixels = maps_ref.shape[0]
    hot = jnp.where(iota((total, slots), 0) == tracks_ref[...], 1.0, 0.0).astype(BF16)
    table = jnp.concatenate(
        [qf_ref[...], qr_ref[...], qc_ref[...], jnp.zeros((5, total), jnp.int32)], axis=0
    ).astype(F32).astype(BF16)
    found = jnp.dot(table, hot, preferred_element_type=F32)
    local = found[0:1] - frame_ref[0].astype(F32)
    flat = jnp.where(local == 0.0, found[1:2] * GRID_W + found[2:3], -1.0)
    column = jnp.broadcast_to(flat, (slots, slots)).T[:, 0:1].astype(jnp.int32)
    step = 512
    acc = jnp.zeros((slots, maps_ref.shape[1]), F32)
    for base in range(0, pixels, step):
        sel = jnp.where(iota((slots, step), 1) + base == column, 1.0, 0.0).astype(BF16)
        acc = acc + jnp.dot(sel, maps_ref[base : base + step, :], preferred_element_type=F32)
    out_ref[...] = acc.astype(BF16)


def prep_kernel(weight_ref, maps_ref, out_ref, turned_ref):
    hid = weight_ref.shape[0]
    part = 2 * TILE
    row = iota((part, KDIM), 0)
    kk = iota((part, KDIM), 1)
    row_out, col_out = row // TILE, row % TILE
    mid = kk < 12 * TILE
    within = kk % (4 * TILE)
    seg = kk // (4 * TILE)
    edge = kk - 12 * TILE
    edge_seg = edge // TILE
    edge_at = edge % TILE
    use_low = jnp.where(mid, seg, edge_seg) == 2
    for parity in range(2):
        row_in = jnp.where(mid, within // TILE, edge_at % 8 - 2 * parity)
        col_in = jnp.where(mid, within % TILE, jnp.where(edge_at < 8, -1, TILE))
        down, across = row_in - row_out, col_in - col_out + 1
        good = (row_in >= 0) & (row_in < 4) & (down >= 0) & (down < 3)
        good = good & (across >= 0) & (across < 3) & (mid | (edge_seg < 3))
        tap = jnp.where(good, down * 3 + across, -1)
        masks = [tap == t for t in range(9)]
        for h in range(hid):
            full = jnp.zeros((part, KDIM), F32)
            for t in range(9):
                full = jnp.where(masks[t], weight_ref[h, t], full)
            high = full.astype(BF16).astype(F32)
            value = jnp.where(use_low, full - high, high)
            out_ref[parity, h * part : (h + 1) * part, :] = value.astype(BF16)
    step = 512
    for base in range(0, maps_ref.shape[0], step):
        turned_ref[:, base : base + step] = maps_ref[base : base + step, :].T


def heat_kernel(
    pieces,
    bias_ref,
    head_ref,
    *refs,
):
    q_refs = refs[:pieces]
    maps_ref, turned_ref, weight_ref, out_ref = refs[pieces : pieces + 4]
    cost_ref, high_ref, low_ref, edge_high, edge_low, logit_ref, heat_ref = refs[pieces + 4 :]
    pixels, chan = maps_ref.shape
    slots = q_refs[0].shape[0]
    hid = bias_ref.shape[0]
    part = 2 * TILE
    query = q_refs[0][...].astype(F32)
    for ref in q_refs[1:]:
        query = query + ref[...].astype(F32)
    turned_q = query.T.astype(BF16)
    scale = 1.0 / math.sqrt(chan)

    for lo, hi in ((0, GRID_W), (GRID_W + pixels, ROWS_PAD * GRID_W)):
        cost_ref[lo:hi, :] = jnp.zeros((hi - lo, slots), F32)
        high_ref[lo:hi, :] = jnp.zeros((hi - lo, slots), BF16)
        low_ref[lo:hi, :] = jnp.zeros((hi - lo, slots), BF16)

    step = 256

    def cost_step(n, carry):
        at = pl.multiple_of(n * step, step)
        cost = jnp.dot(maps_ref[pl.ds(at, step), :], turned_q, preferred_element_type=F32) * scale
        to = pl.multiple_of(at + GRID_W, GRID_W)
        high = cost.astype(BF16)
        cost_ref[pl.ds(to, step), :] = cost
        high_ref[pl.ds(to, step), :] = high
        low_ref[pl.ds(to, step), :] = (cost - high.astype(F32)).astype(BF16)
        return carry

    lax.fori_loop(0, pixels // step, cost_step, 0)

    cols = GRID_W // TILE
    const = 0.0
    for h in range(hid):
        const = const + head_ref[h] * bias_ref[h]

    def window_step(j, best):
        for k in range(cols):
            base = j * 4 * GRID_W + k * TILE
            left = (
                jnp.zeros((8, slots), F32)
                if k == 0
                else cost_ref[pl.ds(base - 1, 8, stride=GRID_W), :]
            )
            right = (
                jnp.zeros((8, slots), F32)
                if k == cols - 1
                else cost_ref[pl.ds(base + TILE, 8, stride=GRID_W), :]
            )
            both = jnp.concatenate([left, right], axis=0)
            high = both.astype(BF16)
            edge_high[k] = high
            edge_low[k] = (both - high.astype(F32)).astype(BF16)
        for parity in range(2):
            top = (4 * j + 2 * parity) * GRID_W
            for pair in range(cols // 2):
                sides = []
                for k in (2 * pair, 2 * pair + 1):
                    at = [pl.multiple_of(top + rr * GRID_W + k * TILE, TILE) for rr in range(4)]
                    mid_high = [high_ref[pl.ds(a, TILE), :] for a in at]
                    mid_low = [low_ref[pl.ds(a, TILE), :] for a in at]
                    eh, el = edge_high[k], edge_low[k]
                    sides.append(
                        jnp.concatenate(mid_high + mid_low + mid_high + [eh, el, eh, eh], axis=0)
                    )
                window = jnp.concatenate(sides, axis=1)
                act = jnp.dot(weight_ref[parity], window, preferred_element_type=F32)
                acc = jnp.full((part, 2 * slots), const, F32)
                for h in range(hid):
                    acc = acc + head_ref[h] * jnp.maximum(
                        act[h * part : (h + 1) * part], -bias_ref[h]
                    )
                for side in range(2):
                    k = 2 * pair + side
                    for rr in range(2):
                        piece = acc[rr * TILE : (rr + 1) * TILE, side * slots : (side + 1) * slots]
                        to = pl.multiple_of(top + rr * GRID_W + k * TILE, TILE)
                        logit_ref[pl.ds(to, TILE), :] = piece
                        best = jnp.maximum(best, jnp.maximum(piece[:8], piece[8:]))
        return best

    best = lax.fori_loop(0, GRID_H // 4, window_step, jnp.full((8, slots), -jnp.inf, F32))
    top_value = jnp.max(best, axis=0, keepdims=True)

    def exp_step(r, carry):
        row_acc, col_acc = carry
        at = pl.multiple_of(r * GRID_W, GRID_W)
        value = jnp.exp(logit_ref[pl.ds(at, GRID_W), :] - top_value)
        logit_ref[pl.ds(at, GRID_W), :] = value
        col_acc = col_acc + value
        folded = value[0:8]
        for n in range(1, GRID_W // 8):
            folded = folded + value[8 * n : 8 * n + 8]
        row_acc = row_acc + folded * (r.astype(F32) * (1.0 / (GRID_H - 1)))
        return row_acc, col_acc

    row_acc, col_acc = lax.fori_loop(
        0, GRID_H, exp_step, (jnp.zeros((8, slots), F32), jnp.zeros((GRID_W, slots), F32))
    )
    total = jnp.sum(col_acc, axis=0, keepdims=True)
    inverse = 1.0 / total
    row_est = jnp.sum(row_acc, axis=0, keepdims=True) * inverse
    col_pos = iota((GRID_W, slots), 0).astype(F32) * (1.0 / (GRID_W - 1))
    col_est = jnp.sum(col_acc * col_pos, axis=0, keepdims=True) * inverse

    def norm_step(n, carry):
        at = pl.multiple_of(n * step, step)
        heat_ref[pl.ds(at, step), :] = (logit_ref[pl.ds(at, step), :] * inverse).astype(BF16)
        return carry

    lax.fori_loop(0, pixels // step, norm_step, 0)
    sampled = jnp.dot(turned_ref[...], heat_ref[...], preferred_element_type=F32)
    rest = jnp.concatenate([row_est, col_est, jnp.zeros((LANES - 2, slots), F32)], axis=0)
    out_ref[:, :chan] = sampled.T.astype(BF16)
    out_ref[:, chan:] = rest.T.astype(BF16)


def mix_kernel(got_ref, mix_in_ref, taps_ref, gain_ref, mix_out_ref, out_ref, z_ref):
    frames, rows, width = got_ref.shape
    chan = mix_in_ref.shape[0]
    for t in range(frames):
        z_ref[t] = jnp.dot(got_ref[t, :, :chan], mix_in_ref[...], preferred_element_type=F32)
    for t in range(frames):
        mixed = taps_ref[1:2, :] * z_ref[t]
        if t > 0:
            mixed = taps_ref[0:1, :] * z_ref[t - 1] + mixed
        if t < frames - 1:
            mixed = mixed + taps_ref[2:3, :] * z_ref[t + 1]
        power = jnp.mean(mixed * mixed, axis=-1, keepdims=True)
        normed = mixed * lax.rsqrt(power + 1e-06) * gain_ref[...]
        hidden = jax.nn.gelu(normed).astype(BF16)
        delta = jnp.dot(hidden, mix_out_ref[...], preferred_element_type=F32)
        place = got_ref[t, :, chan:].astype(F32)
        out_ref[t] = delta + place


def on_device(
    feature_maps,
    query_frame,
    query_row,
    query_col,
    track_order,
    conv_weight,
    conv_bias,
    head_weight,
    mix_in,
    temporal_taps,
    mix_gain,
    mix_out,
):
    frame_count = lax.axis_size("frame")
    track_count = lax.axis_size("track")
    frame_here = lax.axis_index("frame").astype(jnp.int32)
    track_here = lax.axis_index("track")
    f_dev, pixels, chan = feature_maps.shape
    total = track_order.shape[0]
    tr_dev = total // track_count
    sub_rows = tr_dev // frame_count
    hid = conv_weight.shape[0]
    mixw = mix_in.shape[1]
    maps = feature_maps.reshape(f_dev * pixels, chan)

    tracks = lax.dynamic_index_in_dim(
        track_order.reshape(frame_count, track_count, sub_rows), track_here, 1, keepdims=False
    ).reshape(1, tr_dev)

    picks = pl.pallas_call(
        pick_kernel,
        name="pick",
        out_shape=jax.ShapeDtypeStruct((tr_dev, chan), BF16),
        in_specs=[SMEM_SPEC] + [VMEM_SPEC] * 5,
        out_specs=VMEM_SPEC,
    )(
        frame_here.reshape(1),
        tracks,
        query_frame.reshape(1, total),
        query_row.reshape(1, total),
        query_col.reshape(1, total),
        maps,
    )
    pieces = [picks]
    for shift in range(1, frame_count):
        pieces.append(
            lax.ppermute(picks, "frame", [(i, (i + shift) % frame_count) for i in range(frame_count)])
        )

    part = 2 * TILE
    weight, turned = pl.pallas_call(
        prep_kernel,
        name="prep",
        out_shape=(
            jax.ShapeDtypeStruct((2, hid * part, KDIM), BF16),
            jax.ShapeDtypeStruct((chan, pixels), BF16),
        ),
        in_specs=[SMEM_SPEC, VMEM_SPEC],
        out_specs=(VMEM_SPEC, VMEM_SPEC),
    )(conv_weight, maps)

    padded = ROWS_PAD * GRID_W
    packed = pl.pallas_call(
        functools.partial(heat_kernel, frame_count),
        name="heat",
        out_shape=jax.ShapeDtypeStruct((tr_dev, chan + LANES), BF16),
        in_specs=[SMEM_SPEC] * 2 + [VMEM_SPEC] * (frame_count + 3),
        out_specs=VMEM_SPEC,
        scratch_shapes=[
            pltpu.VMEM((padded, tr_dev), F32),
            pltpu.VMEM((padded, tr_dev), BF16),
            pltpu.VMEM((padded, tr_dev), BF16),
            pltpu.VMEM((GRID_W // TILE, TILE, tr_dev), BF16),
            pltpu.VMEM((GRID_W // TILE, TILE, tr_dev), BF16),
            pltpu.VMEM((pixels, tr_dev), F32),
            pltpu.VMEM((pixels, tr_dev), BF16),
        ],
    )(conv_bias, head_weight, *pieces, maps, turned, weight)

    got = lax.all_to_all(
        packed.reshape(frame_count, sub_rows, chan + LANES),
        "frame",
        split_axis=0,
        concat_axis=0,
        tiled=True,
    )
    wide_out = jnp.pad(mix_out, ((0, 0), (0, LANES - mix_out.shape[1])))
    mixed = pl.pallas_call(
        mix_kernel,
        name="mix",
        out_shape=jax.ShapeDtypeStruct((frame_count, sub_rows, LANES), F32),
        in_specs=[VMEM_SPEC] * 5,
        out_specs=VMEM_SPEC,
        scratch_shapes=[pltpu.VMEM((frame_count, sub_rows, mixw), F32)],
    )(got, mix_in, temporal_taps, mix_gain.reshape(1, mixw), wide_out)
    return jnp.transpose(mixed[:, :, :3], (1, 2, 0))


def solution(mesh):
    placed = (
        P(("clip", "frame"), None, None),
        P("clip"),
        P("clip"),
        P("clip"),
        P("clip"),
        P(),
        P(),
        P(),
        P(),
        P(),
        P(),
        P(),
    )
    return jax.shard_map(
        on_device,
        mesh=mesh,
        in_specs=placed,
        out_specs=P(("clip", "frame", "track"), None, None),
        check_vma=False,
    )
```

time: 406 us -> 46.7 us (0.12)
  other arithmetic: 292 us -> 0 us
  waiting for transfers between devices: 41.8 us -> 4.88 us
  local copies, waits for them, and re-layouts: 32.8 us -> 5.23 us
  Pallas kernels: 0 us -> 25.7 us
  between operations: 13.5 us -> 0.04 us
  matrix products: 10.4 us -> 0 us
  blocking collectives: 7.93 us -> 0 us
  starting transfers between devices: 4.66 us -> 10.5 us
    reduce_max x2 -> x0, other arithmetic: 285 us -> none  [block_terms(): heat = jax.nn.softmax(logit.reshape(cost.shape), axis=-1)]
    psum x1 -> x0, waiting for transfers between devices: 37.1 us -> none  [on_device(): lax.psum(partial_value, 'frame').astype(jnp.float32).astype(jnp.bfloat16)]
    pallas_call x0 -> x4, Pallas kernels: none -> 25.7 us  [the longest x1 15.8 us: on_device(): pl.pallas_call(functools.partial(heat_kernel, frame_count), name='heat',...]
    slice x21 -> x0, local copies, waits for them, and re-layouts: 14.4 us -> none  [the longest x16 11.5 us: conv_logits(): conv_weight[channel, tap]]
    dot_general x6 -> x0, matrix products: 10.4 us -> none  [the longest x2 4.86 us: block_terms(): jnp.dot(heat.astype(jnp.bfloat16), maps, preferred_element_type=jnp.float32)]
    gather x5 -> x0, local copies, waits for them, and re-layouts: 9.19 us -> none  [the longest x2 3.29 us: on_device(): pixel_ids = query_row[tracks] * GRID_W + query_col[tracks]]
    all_to_all x1 -> x0, blocking collectives: 7.93 us -> none  [on_device(): lax.all_to_all(local_est, 'frame', split_axis=0, concat_axis=3, tiled=True)]
    reshape x4 -> x2, local copies, waits for them, and re-layouts: 7.63 us -> 1.43 us  [the longest x1 0.76 us: on_device(): track_order.reshape(frame_count, track_count, sub_rows)]
  transfers between devices with their start and end apart: 3 -> 4, of which waited for: 3 -> 1; matrix products, arithmetic and copies ran while one was open for 0% -> 2% of each run, Pallas kernels for 0% -> 9%
where the time goes in v1:
time: 46.7 us; the launch traced here: 46.3 us
  Pallas kernels  25.7 us (55%)
  starting transfers between devices  10.5 us (22%)
  local copies, waits for them, and re-layouts  5.23 us (11%)
  waiting for transfers between devices  4.88 us (10%)
    pallas_call x1, Pallas kernels, on_device(): pl.pallas_call(functools.partial(heat_kernel, frame_count), name='heat',...  15.8 us
    ppermute x3, starting transfers between devices, on_device(): lax.ppermute(picks, 'frame', [(i, (i + shift) % frame_count) for i in ran...  6.99 us
    all_to_all x1, waiting for transfers between devices, on_device(): lax.all_to_all(packed.reshape(frame_count, sub_rows, chan + LANES), 'fram...  4.87 us
    pallas_call x1, Pallas kernels, on_device(): pl.pallas_call(prep_kernel, name='prep', out_shape=(jax.ShapeDtypeStruct(...  4.3 us
    all_to_all x1, starting transfers between devices, on_device(): lax.all_to_all(packed.reshape(frame_count, sub_rows, chan + LANES), 'fram...  3.48 us
    pallas_call x1, Pallas kernels, on_device(): pl.pallas_call(pick_kernel, name='pick', out_shape=jax.ShapeDtypeStruct((...  2.96 us
    pallas_call x1, Pallas kernels, on_device(): pl.pallas_call(mix_kernel, name='mix', out_shape=jax.ShapeDtypeStruct((fr...  2.63 us
    transpose x2, local copies, waits for them, and re-layouts, on_device(): return jnp.transpose(mixed[:, :, :3], (1, 2, 0))  1.53 us
  transfers between devices with their start and end apart: 4, of which 1 were waited for; matrix products, arithmetic and copies ran while one was open for 2% of the time, Pallas kernels for 9%

profile of v1, /device:TPU:0, one launch (start us, length us, event | category | flops | bytes accessed | tf_op | source)
XLA Modules:
  0.0 46.3 jit_solution(9170891855301227945)
XLA Ops:
  0.0 0.8 %reshape.29 = s32[4,4,32]{2,1,0:T(4,128)S(1)} reshape(s32[512]{0:T(512)} %param.16) | data formatting | bytes 4096 | tf_op jit(solution)/shard_map/reshape | solution.py:251
  0.8 0.7 %reshape.30.tracks_ref = s32[1,128]{1,0:T(1,128)} reshape(s32[4,32]{1,0:T(4,128)S(1)} %dynamic-slice_reduce_fusion) | data formatting | bytes 1024 | tf_op jit(solution)/shard_map/reshape | solution.py:252
  1.5 3.0 %pick.1.refs_0_ = bf16[128,256]{1,0:T(8,128)(2,1)} custom-call(s32[1]{0:T(128)} %bitcast.frame_ref, s32[1,128]{1,0:T(1,128)} %reshape.30.tracks_ref, s32[1,512]{1,0:T(1,128)} %bitcast.14, s32[1,512]{1,0:T(1,128)} %bitcast.15, s32[1,512]{1,0:T(1,128)} %bitcast.16, bf16[4096,256]{1,0:T(8,128)(2,1)} %bitcast.9), custom_call_target="tpu_custom_call" | custom-call | tf_op jit(solution)/shard_map/pick/pallas_call | solution.py:254
  4.4 3.1 %collective-permute-start = (bf16[128,256]{1,0:T(8,128)(2,1)}, bf16[128,256]{1,0:T(8,128)(2,1)S(1)}, u32[]{:S(2)}, u32[]{:S(2)}) collective-permute-start(bf16[128,256]{1,0:T(8,128)(2,1)} %pick.1.refs_0_), channel_id=1, source_target_pairs={{0,4},{4,8},{8,12},{12,0},{1,5},{5,9},{9,13},{13,1},{2,6},{6,10},{... | collective-permute-start | bytes 196616 | tf_op jit(solution)/shard_map/ppermute | solution.py:271
  7.5 2.6 %collective-permute-start.1 = (bf16[128,256]{1,0:T(8,128)(2,1)}, bf16[128,256]{1,0:T(8,128)(2,1)S(1)}, u32[]{:S(2)}, u32[]{:S(2)}) collective-permute-start(bf16[128,256]{1,0:T(8,128)(2,1)} %pick.1.refs_0_), channel_id=1, source_target_pairs={{0,8},{4,12},{8,0},{12,4},{1,9},{5,13},{9,1},{13,5},{2,10},{6,14},... | collective-permute-start | bytes 196616 | tf_op jit(solution)/shard_map/ppermute | solution.py:271
  10.1 1.4 %collective-permute-start.2 = (bf16[128,256]{1,0:T(8,128)(2,1)}, bf16[128,256]{1,0:T(8,128)(2,1)S(1)}, u32[]{:S(2)}, u32[]{:S(2)}) collective-permute-start(bf16[128,256]{1,0:T(8,128)(2,1)} %pick.1.refs_0_), channel_id=1, source_target_pairs={{0,12},{4,0},{8,4},{12,8},{1,13},{5,1},{9,5},{13,9},{2,14},{6,2},{... | collective-permute-start | bytes 196616 | tf_op jit(solution)/shard_map/ppermute | solution.py:271
  11.4 4.3 %prep.1 = (bf16[2,512,256]{2,1,0:T(8,128)(2,1)}, bf16[256,4096]{1,0:T(8,128)(2,1)}) custom-call(f32[16,9]{1,0:T(8,128)} %weight_ref.1, bf16[4096,256]{1,0:T(8,128)(2,1)} %bitcast.10), custom_call_target="tpu_custom_call" | custom-call | tf_op jit(solution)/shard_map/prep/pallas_call | solution.py:275
  15.7 0.0 collective-permute-done.refs_1_
  15.7 0.0 copy-start.1
  15.7 0.0 collective-permute-done.1.refs_2_
  15.7 0.0 copy-start.2
  15.7 0.0 collective-permute-done.2.refs_3_
  15.7 0.0 copy-start.3
  15.7 0.6 %copy-done.1 = bf16[128,256]{1,0:T(8,128)(2,1)} copy-done((bf16[128,256]{1,0:T(8,128)(2,1)}, bf16[128,256]{1,0:T(8,128)(2,1)S(1)}, u32[]{:S(2)}) %copy-start.1) | copy-done | bytes 65560
  16.3 0.0 copy-done.2
  16.4 0.0 copy-done.3
  16.4 0.0 copy-start.4
  16.4 15.8 %heat.1 = bf16[128,384]{1,0:T(8,128)(2,1)} custom-call(f32[16]{0:T(128)} %bias_ref.1, f32[16]{0:T(128)} %head_ref.1, bf16[128,256]{1,0:T(8,128)(2,1)} %pick.1.refs_0_, bf16[128,256]{1,0:T(8,128)(2,1)} %copy-done.1, bf16[128,256]{1,0:T(8,128)(2,1)} %copy-done.2, bf16[128,256]{1,0:T(8,128)(2,1)} %copy-done.3, bf16[4096,256]{1,0:T(8,128)(2,1)} %bitcast.11, ...), custom_call_target="tpu_custom_call" | custom-call | tf_op jit(solution)/shard_map/heat/pallas_call | solution.py:287
  32.2 3.5 %all-to-all-start = ((bf16[4,32,384]{2,1,0:T(8,128)(2,1)}), bf16[4,32,384]{2,1,0:T(8,128)(2,1)S(1)}, u32[]{:S(2)}, u32[]{:S(2)}) async-start(bf16[4,32,384]{2,1,0:T(8,128)(2,1)} %bitcast.12), calls=%async_computation | async-start | bytes 196608 | tf_op jit(solution)/shard_map/all_to_all | solution.py:304
  35.7 0.0 copy-done.4
  35.7 0.2 copy.15
  35.9 0.8 %pad.4.mix_out_ref = bf16[1024,128]{1,0:T(8,128)(2,1)} pad(bf16[1024,3]{1,0:T(8,128)(2,1)S(1)} %copy.15, bf16[]{:T(256)} %constant.15.clone.1), padding=0_0x0_125 | pad | bytes 268290 | tf_op jit(solution)/shard_map/jit(_pad)/pad | solution.py:311
  36.6 4.9 %all-to-all-done.got_ref = bf16[4,32,384]{2,1,0:T(8,128)(2,1)S(1)} async-done(((bf16[4,32,384]{2,1,0:T(8,128)(2,1)}), bf16[4,32,384]{2,1,0:T(8,128)(2,1)S(1)}, u32[]{:S(2)}, u32[]{:S(2)}) %all-to-all-start) | async-done | bytes 98336 | tf_op jit(solution)/shard_map/all_to_all | solution.py:304
  41.5 0.0 copy-start
  41.5 0.6 %copy-done = bf16[4,32,384]{2,1,0:T(8,128)(2,1)} copy-done((bf16[4,32,384]{2,1,0:T(8,128)(2,1)}, bf16[4,32,384]{2,1,0:T(8,128)(2,1)S(1)}, u32[]{:S(2)}) %copy-start) | copy-done | bytes 98328
  42.1 2.6 %mix.1 = f32[4,32,128]{2,1,0:T(8,128)} custom-call(bf16[4,32,384]{2,1,0:T(8,128)(2,1)} %copy-done, bf16[256,1024]{1,0:T(8,128)(2,1)} %mix_in_ref.1, f32[3,1024]{1,0:T(4,128)} %taps_ref.1, f32[1,1024]{1,0:T(1,128)} %bitcast.13, bf16[1024,128]{1,0:T(8,128)(2,1)} %pad.4.mix_out_ref), custom_call_target="tpu_custom_call" | custom-call | tf_op jit(solution)/shard_map/mix/pallas_call | solution.py:312
  44.8 0.8 %slice_bitcast_fusion = f32[32,3,4]{1,0,2:T(8,128)S(1)} fusion(f32[4,32,128]{2,1,0:T(8,128)} %mix.1), kind=kLoop, calls=%fused_computation | loop fusion | bytes 3072 | tf_op jit(solution)/shard_map/transpose | solution.py:320
  45.6 0.7 %copy.16 = f32[32,3,4]{0,2,1:T(4,128)} copy(f32[32,3,4]{1,0,2:T(8,128)S(1)} %slice_bitcast_fusion) | data formatting | bytes 3072 | tf_op jit(solution)/shard_map/transpose | solution.py:320
  (1 shorter events, 0.0 us)
Async XLA Ops:
  4.4 11.3 %collective-permute-start = (bf16[128,256]{1,0:T(8,128)(2,1)}, bf16[128,256]{1,0:T(8,128)(2,1)S(1)}, u32[]{:S(2)}, u32[]{:S(2)}) collective-permute-start(bf16[128,256]{1,0:T(8,128)(2,1)} %pick.1.refs_0_), channel_id=1, source_target_pairs={{0,4},{4,8},{8,12},{12,0},{1,5},{5,9},{9,13},{13,1},{2,6},{6,10},{... | collective-permute-start | bytes 196616 | tf_op jit(solution)/shard_map/ppermute | solution.py:271
  7.5 8.2 %collective-permute-start.1 = (bf16[128,256]{1,0:T(8,128)(2,1)}, bf16[128,256]{1,0:T(8,128)(2,1)S(1)}, u32[]{:S(2)}, u32[]{:S(2)}) collective-permute-start(bf16[128,256]{1,0:T(8,128)(2,1)} %pick.1.refs_0_), channel_id=1, source_target_pairs={{0,8},{4,12},{8,0},{12,4},{1,9},{5,13},{9,1},{13,5},{2,10},{6,14},... | collective-permute-start | bytes 196616 | tf_op jit(solution)/shard_map/ppermute | solution.py:271
  10.1 5.7 %collective-permute-start.2 = (bf16[128,256]{1,0:T(8,128)(2,1)}, bf16[128,256]{1,0:T(8,128)(2,1)S(1)}, u32[]{:S(2)}, u32[]{:S(2)}) collective-permute-start(bf16[128,256]{1,0:T(8,128)(2,1)} %pick.1.refs_0_), channel_id=1, source_target_pairs={{0,12},{4,0},{8,4},{12,8},{1,13},{5,1},{9,5},{13,9},{2,14},{6,2},{... | collective-permute-start | bytes 196616 | tf_op jit(solution)/shard_map/ppermute | solution.py:271
  15.7 0.6 %copy-start.1 = (bf16[128,256]{1,0:T(8,128)(2,1)}, bf16[128,256]{1,0:T(8,128)(2,1)S(1)}, u32[]{:S(2)}) copy-start(bf16[128,256]{1,0:T(8,128)(2,1)S(1)} %collective-permute-done.refs_1_) | copy-start | bytes 196612
  15.7 0.6 %copy-start.2 = (bf16[128,256]{1,0:T(8,128)(2,1)}, bf16[128,256]{1,0:T(8,128)(2,1)S(1)}, u32[]{:S(2)}) copy-start(bf16[128,256]{1,0:T(8,128)(2,1)S(1)} %collective-permute-done.1.refs_2_) | copy-start | bytes 196612
  15.7 0.7 %copy-start.3 = (bf16[128,256]{1,0:T(8,128)(2,1)}, bf16[128,256]{1,0:T(8,128)(2,1)S(1)}, u32[]{:S(2)}) copy-start(bf16[128,256]{1,0:T(8,128)(2,1)S(1)} %collective-permute-done.2.refs_3_) | copy-start | bytes 196612
  16.4 19.3 %copy-start.4 = (bf16[1024,3]{0,1:T(4,128)(2,1)S(1)}, bf16[1024,3]{0,1:T(4,128)(2,1)}, u32[]{:S(2)}) copy-start(bf16[1024,3]{0,1:T(4,128)(2,1)} %param.23) | copy-start | bytes 18436
  32.2 9.3 %all-to-all-start = ((bf16[4,32,384]{2,1,0:T(8,128)(2,1)}), bf16[4,32,384]{2,1,0:T(8,128)(2,1)S(1)}, u32[]{:S(2)}, u32[]{:S(2)}) async-start(bf16[4,32,384]{2,1,0:T(8,128)(2,1)} %bitcast.12), calls=%async_computation | async-start | bytes 196608 | tf_op jit(solution)/shard_map/all_to_all | solution.py:304
  41.5 0.6 %copy-start = (bf16[4,32,384]{2,1,0:T(8,128)(2,1)}, bf16[4,32,384]{2,1,0:T(8,128)(2,1)S(1)}, u32[]{:S(2)}) copy-start(bf16[4,32,384]{2,1,0:T(8,128)(2,1)S(1)} %all-to-all-done.got_ref) | copy-start | bytes 294916

commit v2 on v1

--- a/solution.py
+++ b/solution.py
@@ -25,27 +25,60 @@
     return lax.broadcasted_iota(jnp.int32, shape, dim)
 
 
-def pick_kernel(frame_ref, tracks_ref, qf_ref, qr_ref, qc_ref, maps_ref, out_ref):
-    total = qf_ref.shape[1]
-    slots = tracks_ref.shape[1]
-    pixels = maps_ref.shape[0]
-    hot = jnp.where(iota((total, slots), 0) == tracks_ref[...], 1.0, 0.0).astype(BF16)
-    table = jnp.concatenate(
-        [qf_ref[...], qr_ref[...], qc_ref[...], jnp.zeros((5, total), jnp.int32)], axis=0
-    ).astype(F32).astype(BF16)
-    found = jnp.dot(table, hot, preferred_element_type=F32)
-    local = found[0:1] - frame_ref[0].astype(F32)
-    flat = jnp.where(local == 0.0, found[1:2] * GRID_W + found[2:3], -1.0)
+def pick_kernel(
+    frame_count,
+    track_count,
+    place_ref,
+    order_ref,
+    qf_ref,
+    qr_ref,
+    qc_ref,
+    maps_ref,
+    out_ref,
+    held_ref,
+    sem,
+):
+    total = order_ref.shape[1]
+    slots = out_ref.shape[0]
+    pixels, chan = held_ref.shape
+    chunks = sem.shape[0]
+    step = pixels // chunks
+    copies = [
+        pltpu.make_async_copy(
+            maps_ref.at[pl.ds(n * step, step)], held_ref.at[pl.ds(n * step, step)], sem.at[n]
+        )
+        for n in range(chunks)
+    ]
+    for copy in copies:
+        copy.start()
+    frame_here, track_here = place_ref[0], place_ref[1]
+    sub = slots // frame_count
+    at = iota((1, slots), 1)
+    slot = (at // sub * track_count + track_here) * sub + at % sub
+    row = iota((total, slots), 0)
+    hot = jnp.where(row == slot, 1.0, 0.0).astype(BF16)
+    order = order_ref[...]
+    blank = jnp.zeros((5, total), jnp.int32)
+    table = jnp.concatenate([order // 256, order % 256, blank, blank[:1]], axis=0)
+    found = jnp.dot(table.astype(F32).astype(BF16), hot, preferred_element_type=F32)
+    track = (found[0:1] * 256.0 + found[1:2]).astype(jnp.int32)
+    hot = jnp.where(row == track, 1.0, 0.0).astype(BF16)
+    table = jnp.concatenate([qf_ref[...], qr_ref[...], qc_ref[...], blank], axis=0)
+    found = jnp.dot(table.astype(F32).astype(BF16), hot, preferred_element_type=F32)
+    flat = found[1:2] * GRID_W + found[2:3]
+    flat = jnp.where(found[0:1] == frame_here.astype(F32), flat, -1.0)
     column = jnp.broadcast_to(flat, (slots, slots)).T[:, 0:1].astype(jnp.int32)
-    step = 512
-    acc = jnp.zeros((slots, maps_ref.shape[1]), F32)
-    for base in range(0, pixels, step):
-        sel = jnp.where(iota((slots, step), 1) + base == column, 1.0, 0.0).astype(BF16)
-        acc = acc + jnp.dot(sel, maps_ref[base : base + step, :], preferred_element_type=F32)
+    acc = jnp.zeros((slots, chan), F32)
+    for n in range(chunks):
+        sel = jnp.where(iota((slots, step), 1) + n * step == column, 1.0, 0.0).astype(BF16)
+        copies[n].wait()
+        acc = acc + jnp.dot(
+            sel, held_ref[n * step : (n + 1) * step, :], preferred_element_type=F32
+        )
     out_ref[...] = acc.astype(BF16)
 
 
-def prep_kernel(weight_ref, maps_ref, out_ref, turned_ref):
+def prep_kernel(weight_ref, out_ref):
     hid = weight_ref.shape[0]
     part = 2 * TILE
     row = iota((part, KDIM), 0)
@@ -73,20 +106,20 @@
             high = full.astype(BF16).astype(F32)
             value = jnp.where(use_low, full - high, high)
             out_ref[parity, h * part : (h + 1) * part, :] = value.astype(BF16)
-    step = 512
-    for base in range(0, maps_ref.shape[0], step):
-        turned_ref[:, base : base + step] = maps_ref[base : base + step, :].T
 
 
 def heat_kernel(
     pieces,
+    order,
+    frame_ref,
     bias_ref,
     head_ref,
     *refs,
 ):
     q_refs = refs[:pieces]
-    maps_ref, turned_ref, weight_ref, out_ref = refs[pieces : pieces + 4]
-    cost_ref, high_ref, low_ref, edge_high, edge_low, logit_ref, heat_ref = refs[pieces + 4 :]
+    maps_ref, weight_ref = refs[pieces : pieces + 2]
+    out_refs = refs[pieces + 2 : 2 * pieces + 2]
+    cost_ref, high_ref, low_ref, edge_high, edge_low, logit_ref, full_ref = refs[2 * pieces + 2 :]
     pixels, chan = maps_ref.shape
     slots = q_refs[0].shape[0]
     hid = bias_ref.shape[0]
@@ -102,7 +135,7 @@
         high_ref[lo:hi, :] = jnp.zeros((hi - lo, slots), BF16)
         low_ref[lo:hi, :] = jnp.zeros((hi - lo, slots), BF16)
 
-    step = 256
+    step = 512
 
     def cost_step(n, carry):
         at = pl.multiple_of(n * step, step)
@@ -169,20 +202,22 @@
     best = lax.fori_loop(0, GRID_H // 4, window_step, jnp.full((8, slots), -jnp.inf, F32))
     top_value = jnp.max(best, axis=0, keepdims=True)
 
-    def exp_step(r, carry):
+    def exp_step(n, carry):
         row_acc, col_acc = carry
-        at = pl.multiple_of(r * GRID_W, GRID_W)
-        value = jnp.exp(logit_ref[pl.ds(at, GRID_W), :] - top_value)
-        logit_ref[pl.ds(at, GRID_W), :] = value
-        col_acc = col_acc + value
-        folded = value[0:8]
-        for n in range(1, GRID_W // 8):
-            folded = folded + value[8 * n : 8 * n + 8]
-        row_acc = row_acc + folded * (r.astype(F32) * (1.0 / (GRID_H - 1)))
+        for m in range(4):
+            r = n * 4 + m
+            at = pl.multiple_of(r * GRID_W, GRID_W)
+            value = jnp.exp(logit_ref[pl.ds(at, GRID_W), :] - top_value)
+            logit_ref[pl.ds(at, GRID_W), :] = value
+            col_acc = col_acc + value
+            parts = [value[8 * n : 8 * n + 8] for n in range(GRID_W // 8)]
+            while len(parts) > 1:
+                parts = [a + b for a, b in zip(parts[::2], parts[1::2])]
+            row_acc = row_acc + parts[0] * (r.astype(F32) * (1.0 / (GRID_H - 1)))
         return row_acc, col_acc
 
     row_acc, col_acc = lax.fori_loop(
-        0, GRID_H, exp_step, (jnp.zeros((8, slots), F32), jnp.zeros((GRID_W, slots), F32))
+        0, GRID_H // 4, exp_step, (jnp.zeros((8, slots), F32), jnp.zeros((GRID_W, slots), F32))
     )
     total = jnp.sum(col_acc, axis=0, keepdims=True)
     inverse = 1.0 / total
@@ -190,23 +225,33 @@
     col_pos = iota((GRID_W, slots), 0).astype(F32) * (1.0 / (GRID_W - 1))
     col_est = jnp.sum(col_acc * col_pos, axis=0, keepdims=True) * inverse
 
-    def norm_step(n, carry):
+    def sample_step(n, acc):
         at = pl.multiple_of(n * step, step)
-        heat_ref[pl.ds(at, step), :] = (logit_ref[pl.ds(at, step), :] * inverse).astype(BF16)
-        return carry
-
-    lax.fori_loop(0, pixels // step, norm_step, 0)
-    sampled = jnp.dot(turned_ref[...], heat_ref[...], preferred_element_type=F32)
+        heat = (logit_ref[pl.ds(at, step), :] * inverse).astype(BF16)
+        return acc + jnp.dot(heat.T, maps_ref[pl.ds(at, step), :], preferred_element_type=F32)
+
+    sampled = lax.fori_loop(0, pixels // step, sample_step, jnp.zeros((slots, chan), F32))
     rest = jnp.concatenate([row_est, col_est, jnp.zeros((LANES - 2, slots), F32)], axis=0)
-    out_ref[:, :chan] = sampled.T.astype(BF16)
-    out_ref[:, chan:] = rest.T.astype(BF16)
-
-
-def mix_kernel(got_ref, mix_in_ref, taps_ref, gain_ref, mix_out_ref, out_ref, z_ref):
-    frames, rows, width = got_ref.shape
+    sub = slots // pieces
+    full_ref[:, :, :chan] = sampled.astype(BF16).reshape(pieces, sub, chan)
+    full_ref[:, :, chan:] = rest.T.astype(BF16).reshape(pieces, sub, LANES)
+    for m in range(pieces):
+        out_refs[m][...] = full_ref[peer(order, frame_ref[0], m, pieces)]
+
+
+def mix_kernel(order, frames, frame_ref, *refs):
+    got_refs = refs[:frames]
+    mix_in_ref, taps_ref, gain_ref, mix_out_ref, out_ref, z_ref, place_ref = refs[frames:]
     chan = mix_in_ref.shape[0]
-    for t in range(frames):
-        z_ref[t] = jnp.dot(got_ref[t, :, :chan], mix_in_ref[...], preferred_element_type=F32)
+    rows = got_refs[0].shape[0]
+    joined = jnp.concatenate([ref[...] for ref in got_refs], axis=0)
+    z = jnp.dot(joined[:, :chan], mix_in_ref[...], preferred_element_type=F32)
+    for m in range(frames):
+        source = peer(order, frame_ref[0], -m, frames)
+        z_ref[source] = z[m * rows : (m + 1) * rows]
+        place_ref[source] = got_refs[m][:, chan:]
+    place = place_ref[...].astype(F32).reshape(frames * rows, LANES).T[:8]
+    hidden = []
     for t in range(frames):
         mixed = taps_ref[1:2, :] * z_ref[t]
         if t > 0:
@@ -215,10 +260,29 @@
             mixed = mixed + taps_ref[2:3, :] * z_ref[t + 1]
         power = jnp.mean(mixed * mixed, axis=-1, keepdims=True)
         normed = mixed * lax.rsqrt(power + 1e-06) * gain_ref[...]
-        hidden = jax.nn.gelu(normed).astype(BF16)
-        delta = jnp.dot(hidden, mix_out_ref[...], preferred_element_type=F32)
-        place = got_ref[t, :, chan:].astype(F32)
-        out_ref[t] = delta + place
+        hidden.append(jax.nn.gelu(normed).astype(BF16))
+    delta = lax.dot_general(
+        mix_out_ref[...],
+        jnp.concatenate(hidden, axis=0),
+        (((1,), (1,)), ((), ())),
+        preferred_element_type=F32,
+    )
+    count = mix_out_ref.shape[0]
+    result = delta + place[:count]
+    for t in range(frames):
+        out_ref[:, t, :] = result[:, t * rows : (t + 1) * rows]
+
+
+def peer(order, here, m, count):
+    if order == "xor":
+        return here ^ abs(m)
+    if isinstance(here, int):
+        return (here + m) % count
+    return lax.rem(here + m + count, count)
+
+
+def in_vmem(x):
+    return pltpu.with_memory_space_constraint(x, pltpu.MemorySpace.VMEM)
 
 
 def on_device(
@@ -238,7 +302,7 @@
     frame_count = lax.axis_size("frame")
     track_count = lax.axis_size("track")
     frame_here = lax.axis_index("frame").astype(jnp.int32)
-    track_here = lax.axis_index("track")
+    track_here = lax.axis_index("track").astype(jnp.int32)
     f_dev, pixels, chan = feature_maps.shape
     total = track_order.shape[0]
     tr_dev = total // track_count
@@ -247,49 +311,51 @@
     mixw = mix_in.shape[1]
     maps = feature_maps.reshape(f_dev * pixels, chan)
 
-    tracks = lax.dynamic_index_in_dim(
-        track_order.reshape(frame_count, track_count, sub_rows), track_here, 1, keepdims=False
-    ).reshape(1, tr_dev)
-
-    picks = pl.pallas_call(
-        pick_kernel,
+    order = "xor" if frame_count & (frame_count - 1) == 0 else "ring"
+
+    def send(x, m):
+        pairs = [(i, peer(order, i, m, frame_count)) for i in range(frame_count)]
+        return lax.ppermute(x, "frame", pairs)
+
+    limits = pltpu.CompilerParams(vmem_limit_bytes=24 << 20)
+    place = jnp.stack([frame_here, track_here])
+    picks, held = pl.pallas_call(
+        functools.partial(pick_kernel, frame_count, track_count),
         name="pick",
-        out_shape=jax.ShapeDtypeStruct((tr_dev, chan), BF16),
-        in_specs=[SMEM_SPEC] + [VMEM_SPEC] * 5,
-        out_specs=VMEM_SPEC,
+        out_shape=(pltpu.VMEM((tr_dev, chan), BF16), pltpu.VMEM((pixels, chan), BF16)),
+        in_specs=[SMEM_SPEC] + [VMEM_SPEC] * 4 + [pl.BlockSpec(memory_space=pl.ANY)],
+        out_specs=(VMEM_SPEC, VMEM_SPEC),
+        scratch_shapes=[pltpu.SemaphoreType.DMA((4,))],
+        compiler_params=limits,
     )(
-        frame_here.reshape(1),
-        tracks,
+        place,
+        track_order.reshape(1, total),
         query_frame.reshape(1, total),
         query_row.reshape(1, total),
         query_col.reshape(1, total),
         maps,
     )
-    pieces = [picks]
-    for shift in range(1, frame_count):
-        pieces.append(
-            lax.ppermute(picks, "frame", [(i, (i + shift) % frame_count) for i in range(frame_count)])
-        )
+    queries = [picks] + [send(picks, m) for m in range(1, frame_count)]
 
     part = 2 * TILE
-    weight, turned = pl.pallas_call(
+    weight = pl.pallas_call(
         prep_kernel,
         name="prep",
-        out_shape=(
-            jax.ShapeDtypeStruct((2, hid * part, KDIM), BF16),
-            jax.ShapeDtypeStruct((chan, pixels), BF16),
+        out_shape=pltpu.VMEM((2, hid * part, KDIM), BF16),
+        in_specs=[SMEM_SPEC],
+        out_specs=VMEM_SPEC,
+        compiler_params=limits,
+    )(conv_weight)
+
+    padded = ROWS_PAD * GRID_W
+    pieces = pl.pallas_call(
+        functools.partial(heat_kernel, frame_count, order),
+        name="heat",
+        out_shape=tuple(
+            pltpu.VMEM((sub_rows, chan + LANES), BF16) for _ in range(frame_count)
         ),
-        in_specs=[SMEM_SPEC, VMEM_SPEC],
-        out_specs=(VMEM_SPEC, VMEM_SPEC),
-    )(conv_weight, maps)
-
-    padded = ROWS_PAD * GRID_W
-    packed = pl.pallas_call(
-        functools.partial(heat_kernel, frame_count),
-        name="heat",
-        out_shape=jax.ShapeDtypeStruct((tr_dev, chan + LANES), BF16),
-        in_specs=[SMEM_SPEC] * 2 + [VMEM_SPEC] * (frame_count + 3),
-        out_specs=VMEM_SPEC,
+        in_specs=[SMEM_SPEC] * 3 + [VMEM_SPEC] * (frame_count + 2),
+        out_specs=tuple(VMEM_SPEC for _ in range(frame_count)),
         scratch_shapes=[
             pltpu.VMEM((padded, tr_dev), F32),
             pltpu.VMEM((padded, tr_dev), BF16),
@@ -297,27 +363,38 @@
             pltpu.VMEM((GRID_W // TILE, TILE, tr_dev), BF16),
             pltpu.VMEM((GRID_W // TILE, TILE, tr_dev), BF16),
             pltpu.VMEM((pixels, tr_dev), F32),
-            pltpu.VMEM((pixels, tr_dev), BF16),
+            pltpu.VMEM((frame_count, sub_rows, chan + LANES), BF16),
         ],
-    )(conv_bias, head_weight, *pieces, maps, turned, weight)
-
-    got = lax.all_to_all(
-        packed.reshape(frame_count, sub_rows, chan + LANES),
-        "frame",
-        split_axis=0,
-        concat_axis=0,
-        tiled=True,
-    )
-    wide_out = jnp.pad(mix_out, ((0, 0), (0, LANES - mix_out.shape[1])))
+        compiler_params=limits,
+    )(
+        frame_here.reshape(1),
+        conv_bias,
+        head_weight,
+        *[in_vmem(q) for q in queries],
+        in_vmem(held),
+        in_vmem(weight),
+    )
+    got = [pieces[0]] + [send(pieces[m], m) for m in range(1, frame_count)]
     mixed = pl.pallas_call(
-        mix_kernel,
+        functools.partial(mix_kernel, order, frame_count),
         name="mix",
-        out_shape=jax.ShapeDtypeStruct((frame_count, sub_rows, LANES), F32),
-        in_specs=[VMEM_SPEC] * 5,
+        out_shape=jax.ShapeDtypeStruct((mix_out.shape[1], frame_count, sub_rows), F32),
+        in_specs=[SMEM_SPEC] + [VMEM_SPEC] * (frame_count + 4),
         out_specs=VMEM_SPEC,
-        scratch_shapes=[pltpu.VMEM((frame_count, sub_rows, mixw), F32)],
-    )(got, mix_in, temporal_taps, mix_gain.reshape(1, mixw), wide_out)
-    return jnp.transpose(mixed[:, :, :3], (1, 2, 0))
+        scratch_shapes=[
+            pltpu.VMEM((frame_count, sub_rows, mixw), F32),
+            pltpu.VMEM((frame_count, sub_rows, LANES), BF16),
+        ],
+        compiler_params=limits,
+    )(
+        frame_here.reshape(1),
+        *[in_vmem(g) for g in got],
+        in_vmem(mix_in),
+        in_vmem(temporal_taps),
+        in_vmem(mix_gain.reshape(1, mixw)),
+        in_vmem(mix_out.T),
+    )
+    return jnp.transpose(mixed, (2, 0, 1))
 
 
 def solution(mesh):

time: 46.7 us -> 40.5 us (0.87)
  Pallas kernels: 25.7 us -> 17.5 us
  waiting for transfers between devices: 4.88 us -> 8 us
  local copies, waits for them, and re-layouts: 5.23 us -> 4.35 us
    pallas_call x4, Pallas kernels: 25.7 us -> 17.5 us  [the longest x1 12.6 us: on_device(): pl.pallas_call(functools.partial(heat_kernel, frame_count, order), name='...]
    ppermute x3 -> x6, waiting for transfers between devices: 0.01 us -> 8 us  [send(): return lax.ppermute(x, 'frame', pairs)]
    all_to_all x1 -> x0, waiting for transfers between devices: 4.87 us -> none  [on_device(): lax.all_to_all(packed.reshape(frame_count, sub_rows, chan + LANES), 'fram...]
    all_to_all x1 -> x0, starting transfers between devices: 3.48 us -> none  [on_device(): lax.all_to_all(packed.reshape(frame_count, sub_rows, chan + LANES), 'fram...]
    ppermute x3 -> x6, starting transfers between devices: 6.99 us -> 10.2 us  [send(): return lax.ppermute(x, 'frame', pairs)]
    unnamed x11 -> x24, local copies, waits for them, and re-layouts: 1.5 us -> 4.35 us
    transpose x2 -> x0, local copies, waits for them, and re-layouts: 1.53 us -> none  [on_device(): return jnp.transpose(mixed[:, :, :3], (1, 2, 0))]
    reshape x2 -> x0, local copies, waits for them, and re-layouts: 1.43 us -> none  [the longest x1 0.76 us: on_device(): track_order.reshape(frame_count, track_count, sub_rows)]
  transfers between devices with their start and end apart: 4 -> 6, of which waited for: 1 -> 4; matrix products, arithmetic and copies ran while one was open for 2% -> 0% of each run, Pallas kernels for 9% -> 4%
where the time goes in v2:
time: 40.5 us; the launch traced here: 40.3 us
  Pallas kernels  17.5 us (43%)
  starting transfers between devices  10.2 us (25%)
  waiting for transfers between devices  8 us (20%)
  local copies, waits for them, and re-layouts  4.35 us (11%)
    pallas_call x1, Pallas kernels, on_device(): pl.pallas_call(functools.partial(heat_kernel, frame_count, order), name='...  12.6 us
    ppermute x6, starting transfers between devices, send(): return lax.ppermute(x, 'frame', pairs)  10.2 us
    ppermute x6, waiting for transfers between devices, send(): return lax.ppermute(x, 'frame', pairs)  8 us
    unnamed x24, local copies, waits for them, and re-layouts  4.35 us
    pallas_call x1, Pallas kernels, on_device(): pl.pallas_call(functools.partial(pick_kernel, frame_count, track_count),...  2.11 us
    pallas_call x1, Pallas kernels, on_device(): pl.pallas_call(prep_kernel, name='prep', out_shape=pltpu.VMEM((2, hid * p...  1.46 us
    pallas_call x1, Pallas kernels, on_device(): pl.pallas_call(functools.partial(mix_kernel, order, frame_count), name='m...  1.4 us
  transfers between devices with their start and end apart: 6, of which 4 were waited for; matrix products, arithmetic and copies ran while one was open for 0% of the time, Pallas kernels for 4%

profile of v2, /device:TPU:0, one launch (start us, length us, event | category | flops | bytes accessed | tf_op | source)
XLA Modules:
  0.0 40.3 jit_solution(8648057562458318416)
XLA Ops:
  0.0 0.0 copy-start.3
  0.0 0.0 copy-start.11
  0.0 0.0 copy-start.10
  0.0 0.1 pad_add_fusion.place_ref
  0.1 0.0 copy-start
  0.1 1.6 %copy-done = bf16[1,4096,256]{2,1,0:T(8,128)(2,1)S(1)} copy-done((bf16[1,4096,256]{2,1,0:T(8,128)(2,1)S(1)}, bf16[1,4096,256]{2,1,0:T(8,128)(2,1)}, u32[]{:S(2)}) %copy-start) | copy-done | bytes 2097176
  1.7 0.0 copy-start.6
  1.7 0.7 %copy-done.6 = s32[512]{0:T(512)S(1)} copy-done((s32[512]{0:T(512)S(1)}, s32[512]{0:T(512)}, u32[]{:S(2)}) %copy-start.6) | copy-done | bytes 2072
  2.4 0.0 copy-start.7
  2.4 0.7 %copy-done.7 = s32[512]{0:T(512)S(1)} copy-done((s32[512]{0:T(512)S(1)}, s32[512]{0:T(512)}, u32[]{:S(2)}) %copy-start.7) | copy-done | bytes 2072
  3.0 0.0 copy-start.8
  3.0 0.7 %copy-done.8 = s32[512]{0:T(512)S(1)} copy-done((s32[512]{0:T(512)S(1)}, s32[512]{0:T(512)}, u32[]{:S(2)}) %copy-start.8) | copy-done | bytes 2072
  3.7 0.0 copy-start.9
  3.7 0.7 %copy-done.9 = s32[512]{0:T(512)S(1)} copy-done((s32[512]{0:T(512)S(1)}, s32[512]{0:T(512)}, u32[]{:S(2)}) %copy-start.9) | copy-done | bytes 2072
  4.4 2.1 %pick.1 = (bf16[128,256]{1,0:T(8,128)(2,1)S(1)}, bf16[4096,256]{1,0:T(8,128)(2,1)S(1)}) custom-call(s32[2]{0:T(128)S(1)} %pad_add_fusion.place_ref, s32[1,512]{1,0:T(1,128)S(1)} %bitcast.13, s32[1,512]{1,0:T(1,128)S(1)} %bitcast.14, s32[1,512]{1,0:T(1,128)S(1)} %bitcast.15, s32[1,512]{1,0:T(1,128)S(1)} %bitcast.16, bf16[4096,256]{1,0:T(8,128)(2,1)S(1)} %bitcast.10), custom_call_target="tpu_custom_call" | custom-call | tf_op jit(solution)/shard_map/pick/pallas_call | solution.py:322
  6.5 0.0 copy-start.1
  6.5 0.0 copy-start.2
  6.5 0.0 copy-start.4
  6.6 0.0 copy-start.5
  6.6 5.2 %collective-permute-start.2 = (bf16[128,256]{1,0:T(8,128)(2,1)S(1)}, bf16[128,256]{1,0:T(8,128)(2,1)S(1)}, u32[]{:S(2)}, u32[]{:S(2)}) collective-permute-start(bf16[128,256]{1,0:T(8,128)(2,1)S(1)} %get-tuple-element.11.refs_0_), channel_id=1, source_target_pairs={{0,12},{4,8},{8,4},{12,0},{1,13},{5,9},{9,5},{13,1},{2,14},{6,10},... | collective-permute-start | bytes 196616 | tf_op jit(solution)/shard_map/ppermute | solution.py:318
  11.7 0.0 collective-permute-start.1
  11.7 0.6 %collective-permute-start = (bf16[128,256]{1,0:T(8,128)(2,1)S(1)}, bf16[128,256]{1,0:T(8,128)(2,1)S(1)}, u32[]{:S(2)}, u32[]{:S(2)}) collective-permute-start(bf16[128,256]{1,0:T(8,128)(2,1)S(1)} %get-tuple-element.11.refs_0_), channel_id=1, source_target_pairs={{0,4},{4,0},{8,12},{12,8},{1,5},{5,1},{9,13},{13,9},{2,6},{6,2},{1... | collective-permute-start | bytes 196616 | tf_op jit(solution)/shard_map/ppermute | solution.py:318
  12.4 0.0 copy-done.3
  12.4 1.5 %prep.1.refs_5_ = bf16[2,512,256]{2,1,0:T(8,128)(2,1)S(1)} custom-call(f32[16,9]{1,0:T(8,128)S(1)} %copy-done.3), custom_call_target="tpu_custom_call" | custom-call | tf_op jit(solution)/shard_map/prep/pallas_call | solution.py:341
  13.8 0.4 collective-permute-done.2.refs_3_
  14.2 3.1 %collective-permute-done.1.refs_2_ = bf16[128,256]{1,0:T(8,128)(2,1)S(1)} collective-permute-done((bf16[128,256]{1,0:T(8,128)(2,1)S(1)}, bf16[128,256]{1,0:T(8,128)(2,1)S(1)}, u32[]{:S(2)}, u32[]{:S(2)}) %collective-permute-start.1) | collective-permute-done | bytes 65568 | tf_op jit(solution)/shard_map/ppermute | solution.py:318
  17.3 0.0 collective-permute-done.refs_1_
  17.3 0.0 copy-done.11
  17.3 0.0 copy-done.10
  17.3 12.6 %heat.1 = (bf16[32,384]{1,0:T(8,128)(2,1)S(1)}, bf16[32,384]{1,0:T(8,128)(2,1)S(1)}, bf16[32,384]{1,0:T(8,128)(2,1)S(1)}, bf16[32,384]{1,0:T(8,128)(2,1)S(1)}) custom-call(s32[1]{0:T(128)} %bitcast.frame_ref, f32[16]{0:T(128)S(1)} %copy-done.10, f32[16]{0:T(128)S(1)} %copy-done.11, bf16[128,256]{1,0:T(8,128)(2,1)S(1)} %get-tuple-element.11.refs_0_, ...), custom_call_target="tpu_custom_call" | custom-call | tf_op jit(solution)/shard_map/heat/pallas_call | solution.py:351
  29.9 1.1 %collective-permute-start.3 = (bf16[32,384]{1,0:T(8,128)(2,1)S(1)}, bf16[32,384]{1,0:T(8,128)(2,1)S(1)}, u32[]{:S(2)}, u32[]{:S(2)}) collective-permute-start(bf16[32,384]{1,0:T(8,128)(2,1)S(1)} %get-tuple-element.14), channel_id=1, source_target_pairs={{0,4},{4,0},{8,12},{12,8},{1,5},{5,1},{9,13},{13,9},{2,6},{6,2},{1... | collective-permute-start | bytes 73736 | tf_op jit(solution)/shard_map/ppermute | solution.py:318
  31.0 2.2 %collective-permute-start.4 = (bf16[32,384]{1,0:T(8,128)(2,1)S(1)}, bf16[32,384]{1,0:T(8,128)(2,1)S(1)}, u32[]{:S(2)}, u32[]{:S(2)}) collective-permute-start(bf16[32,384]{1,0:T(8,128)(2,1)S(1)} %get-tuple-element.15), channel_id=1, source_target_pairs={{0,8},{4,12},{8,0},{12,4},{1,9},{5,13},{9,1},{13,5},{2,10},{6,14},... | collective-permute-start | bytes 73736 | tf_op jit(solution)/shard_map/ppermute | solution.py:318
  33.2 1.1 %collective-permute-start.5 = (bf16[32,384]{1,0:T(8,128)(2,1)S(1)}, bf16[32,384]{1,0:T(8,128)(2,1)S(1)}, u32[]{:S(2)}, u32[]{:S(2)}) collective-permute-start(bf16[32,384]{1,0:T(8,128)(2,1)S(1)} %get-tuple-element.16), channel_id=1, source_target_pairs={{0,12},{4,8},{8,4},{12,0},{1,13},{5,9},{9,5},{13,1},{2,14},{6,10},... | collective-permute-start | bytes 73736 | tf_op jit(solution)/shard_map/ppermute | solution.py:318
  34.4 0.0 collective-permute-done.3.refs_1_
  34.4 1.9 %collective-permute-done.4.refs_2_ = bf16[32,384]{1,0:T(8,128)(2,1)S(1)} collective-permute-done((bf16[32,384]{1,0:T(8,128)(2,1)S(1)}, bf16[32,384]{1,0:T(8,128)(2,1)S(1)}, u32[]{:S(2)}, u32[]{:S(2)}) %collective-permute-start.4) | collective-permute-done | bytes 24608 | tf_op jit(solution)/shard_map/ppermute | solution.py:318
  36.3 2.6 %collective-permute-done.5.refs_3_ = bf16[32,384]{1,0:T(8,128)(2,1)S(1)} collective-permute-done((bf16[32,384]{1,0:T(8,128)(2,1)S(1)}, bf16[32,384]{1,0:T(8,128)(2,1)S(1)}, u32[]{:S(2)}, u32[]{:S(2)}) %collective-permute-start.5) | collective-permute-done | bytes 24608 | tf_op jit(solution)/shard_map/ppermute | solution.py:318
  38.9 0.0 copy-done.1
  38.9 0.0 copy-done.2
  38.9 0.0 copy-done.4
  38.9 0.0 copy-done.5
  38.9 1.4 %mix.1 = f32[3,4,32]{2,1,0:T(4,128)} custom-call(s32[1]{0:T(128)} %bitcast.frame_ref, bf16[32,384]{1,0:T(8,128)(2,1)S(1)} %get-tuple-element.13.refs_0_, bf16[32,384]{1,0:T(8,128)(2,1)S(1)} %collective-permute-done.3.refs_1_, bf16[32,384]{1,0:T(8,128)(2,1)S(1)} %collective-permute-done.4.refs_2_, bf16[32,384]{1,0:T(8,128)(2,1)S(1)} %collective-permute-done.5.refs_3_, ...), custom_call_target="tpu_custom_call" | custom-call | tf_op jit(solution)/shard_map/mix/pallas_call | solution.py:378
Async XLA Ops:
  0.0 12.4 %copy-start.3 = (f32[16,9]{1,0:T(8,128)S(1)}, f32[16,9]{1,0:T(8,128)}, u32[]{:S(2)}) copy-start(f32[16,9]{1,0:T(8,128)} %weight_ref.1) | copy-start | bytes 1732
  0.0 17.3 %copy-start.11 = (f32[16]{0:T(128)S(1)}, f32[16]{0:T(128)}, u32[]{:S(2)}) copy-start(f32[16]{0:T(128)} %head_ref.1) | copy-start | bytes 196
  0.0 17.3 %copy-start.10 = (f32[16]{0:T(128)S(1)}, f32[16]{0:T(128)}, u32[]{:S(2)}) copy-start(f32[16]{0:T(128)} %bias_ref.1) | copy-start | bytes 196
  0.1 1.6 %copy-start = (bf16[1,4096,256]{2,1,0:T(8,128)(2,1)S(1)}, bf16[1,4096,256]{2,1,0:T(8,128)(2,1)}, u32[]{:S(2)}) copy-start(bf16[1,4096,256]{2,1,0:T(8,128)(2,1)} %param.12) | copy-start | bytes 6291460
  1.7 0.7 %copy-start.6 = (s32[512]{0:T(512)S(1)}, s32[512]{0:T(512)}, u32[]{:S(2)}) copy-start(s32[512]{0:T(512)} %param.16) | copy-start | bytes 6148
  2.4 0.7 %copy-start.7 = (s32[512]{0:T(512)S(1)}, s32[512]{0:T(512)}, u32[]{:S(2)}) copy-start(s32[512]{0:T(512)} %param.13) | copy-start | bytes 6148
  3.0 0.7 %copy-start.8 = (s32[512]{0:T(512)S(1)}, s32[512]{0:T(512)}, u32[]{:S(2)}) copy-start(s32[512]{0:T(512)} %param.14) | copy-start | bytes 6148
  3.7 0.7 %copy-start.9 = (s32[512]{0:T(512)S(1)}, s32[512]{0:T(512)}, u32[]{:S(2)}) copy-start(s32[512]{0:T(512)} %param.15) | copy-start | bytes 6148
  6.5 32.4 %copy-start.1 = (bf16[256,1024]{1,0:T(8,128)(2,1)S(1)}, bf16[256,1024]{1,0:T(8,128)(2,1)}, u32[]{:S(2)}) copy-start(bf16[256,1024]{1,0:T(8,128)(2,1)} %refs_4_.1) | copy-start | bytes 1572868
  6.5 32.3 %copy-start.2 = (f32[3,1024]{1,0:T(4,128)S(1)}, f32[3,1024]{1,0:T(4,128)}, u32[]{:S(2)}) copy-start(f32[3,1024]{1,0:T(4,128)} %refs_5_.1) | copy-start | bytes 36868
  6.5 32.3 %copy-start.4 = (bf16[1024,3]{0,1:T(4,128)(2,1)S(1)}, bf16[1024,3]{0,1:T(4,128)(2,1)}, u32[]{:S(2)}) copy-start(bf16[1024,3]{0,1:T(4,128)(2,1)} %param.23) | copy-start | bytes 18436
  6.6 32.3 %copy-start.5 = (f32[1024]{0:T(1024)S(1)}, f32[1024]{0:T(1024)}, u32[]{:S(2)}) copy-start(f32[1024]{0:T(1024)} %param.22) | copy-start | bytes 12292
  6.6 7.6 %collective-permute-start.2 = (bf16[128,256]{1,0:T(8,128)(2,1)S(1)}, bf16[128,256]{1,0:T(8,128)(2,1)S(1)}, u32[]{:S(2)}, u32[]{:S(2)}) collective-permute-start(bf16[128,256]{1,0:T(8,128)(2,1)S(1)} %get-tuple-element.11.refs_0_), channel_id=1, source_target_pairs={{0,12},{4,8},{8,4},{12,0},{1,13},{5,9},{9,5},{13,1},{2,14},{6,10},... | collective-permute-start | bytes 196616 | tf_op jit(solution)/shard_map/ppermute | solution.py:318
  11.7 5.6 %collective-permute-start.1 = (bf16[128,256]{1,0:T(8,128)(2,1)S(1)}, bf16[128,256]{1,0:T(8,128)(2,1)S(1)}, u32[]{:S(2)}, u32[]{:S(2)}) collective-permute-start(bf16[128,256]{1,0:T(8,128)(2,1)S(1)} %get-tuple-element.11.refs_0_), channel_id=1, source_target_pairs={{0,8},{4,12},{8,0},{12,4},{1,9},{5,13},{9,1},{13,5},{2,10},{6,14},... | collective-permute-start | bytes 196616 | tf_op jit(solution)/shard_map/ppermute | solution.py:318
  11.7 5.6 %collective-permute-start = (bf16[128,256]{1,0:T(8,128)(2,1)S(1)}, bf16[128,256]{1,0:T(8,128)(2,1)S(1)}, u32[]{:S(2)}, u32[]{:S(2)}) collective-permute-start(bf16[128,256]{1,0:T(8,128)(2,1)S(1)} %get-tuple-element.11.refs_0_), channel_id=1, source_target_pairs={{0,4},{4,0},{8,12},{12,8},{1,5},{5,1},{9,13},{13,9},{2,6},{6,2},{1... | collective-permute-start | bytes 196616 | tf_op jit(solution)/shard_map/ppermute | solution.py:318
  29.9 4.5 %collective-permute-start.3 = (bf16[32,384]{1,0:T(8,128)(2,1)S(1)}, bf16[32,384]{1,0:T(8,128)(2,1)S(1)}, u32[]{:S(2)}, u32[]{:S(2)}) collective-permute-start(bf16[32,384]{1,0:T(8,128)(2,1)S(1)} %get-tuple-element.14), channel_id=1, source_target_pairs={{0,4},{4,0},{8,12},{12,8},{1,5},{5,1},{9,13},{13,9},{2,6},{6,2},{1... | collective-permute-start | bytes 73736 | tf_op jit(solution)/shard_map/ppermute | solution.py:318
  31.0 5.3 %collective-permute-start.4 = (bf16[32,384]{1,0:T(8,128)(2,1)S(1)}, bf16[32,384]{1,0:T(8,128)(2,1)S(1)}, u32[]{:S(2)}, u32[]{:S(2)}) collective-permute-start(bf16[32,384]{1,0:T(8,128)(2,1)S(1)} %get-tuple-element.15), channel_id=1, source_target_pairs={{0,8},{4,12},{8,0},{12,4},{1,9},{5,13},{9,1},{13,5},{2,10},{6,14},... | collective-permute-start | bytes 73736 | tf_op jit(solution)/shard_map/ppermute | solution.py:318
  33.2 5.6 %collective-permute-start.5 = (bf16[32,384]{1,0:T(8,128)(2,1)S(1)}, bf16[32,384]{1,0:T(8,128)(2,1)S(1)}, u32[]{:S(2)}, u32[]{:S(2)}) collective-permute-start(bf16[32,384]{1,0:T(8,128)(2,1)S(1)} %get-tuple-element.16), channel_id=1, source_target_pairs={{0,12},{4,8},{8,4},{12,0},{1,13},{5,9},{9,5},{13,1},{2,14},{6,10},... | collective-permute-start | bytes 73736 | tf_op jit(solution)/shard_map/ppermute | solution.py:318

commit v3 on v2

--- a/solution.py
+++ b/solution.py
@@ -28,42 +28,50 @@
 def pick_kernel(
     frame_count,
     track_count,
-    place_ref,
-    order_ref,
-    qf_ref,
-    qr_ref,
-    qc_ref,
-    maps_ref,
+    order_hbm,
+    qf_hbm,
+    qr_hbm,
+    qc_hbm,
+    maps_hbm,
     out_ref,
     held_ref,
+    index_ref,
+    index_sem,
     sem,
 ):
-    total = order_ref.shape[1]
+    total = order_hbm.shape[1]
     slots = out_ref.shape[0]
     pixels, chan = held_ref.shape
     chunks = sem.shape[0]
     step = pixels // chunks
+    small = [
+        pltpu.make_async_copy(src, index_ref.at[n], index_sem.at[n])
+        for n, src in enumerate((order_hbm, qf_hbm, qr_hbm, qc_hbm))
+    ]
     copies = [
         pltpu.make_async_copy(
-            maps_ref.at[pl.ds(n * step, step)], held_ref.at[pl.ds(n * step, step)], sem.at[n]
+            maps_hbm.at[pl.ds(n * step, step)], held_ref.at[pl.ds(n * step, step)], sem.at[n]
         )
         for n in range(chunks)
     ]
-    for copy in copies:
+    for copy in small + copies:
         copy.start()
-    frame_here, track_here = place_ref[0], place_ref[1]
+    frame_here = lax.axis_index("frame").astype(jnp.int32)
+    track_here = lax.axis_index("track").astype(jnp.int32)
     sub = slots // frame_count
     at = iota((1, slots), 1)
     slot = (at // sub * track_count + track_here) * sub + at % sub
     row = iota((total, slots), 0)
     hot = jnp.where(row == slot, 1.0, 0.0).astype(BF16)
-    order = order_ref[...]
+    for copy in small:
+        copy.wait()
+    order = index_ref[0]
     blank = jnp.zeros((5, total), jnp.int32)
     table = jnp.concatenate([order // 256, order % 256, blank, blank[:1]], axis=0)
     found = jnp.dot(table.astype(F32).astype(BF16), hot, preferred_element_type=F32)
     track = (found[0:1] * 256.0 + found[1:2]).astype(jnp.int32)
     hot = jnp.where(row == track, 1.0, 0.0).astype(BF16)
-    table = jnp.concatenate([qf_ref[...], qr_ref[...], qc_ref[...], blank], axis=0)
+    table = jnp.concatenate([index_ref[1], index_ref[2], index_ref[3], blank], axis=0)
     found = jnp.dot(table.astype(F32).astype(BF16), hot, preferred_element_type=F32)
     flat = found[1:2] * GRID_W + found[2:3]
     flat = jnp.where(found[0:1] == frame_here.astype(F32), flat, -1.0)
@@ -78,7 +86,7 @@
     out_ref[...] = acc.astype(BF16)
 
 
-def prep_kernel(weight_ref, out_ref):
+def prep_kernel(weight_ref, bias_ref, head_ref, out_ref, coef_ref):
     hid = weight_ref.shape[0]
     part = 2 * TILE
     row = iota((part, KDIM), 0)
@@ -106,24 +114,30 @@
             high = full.astype(BF16).astype(F32)
             value = jnp.where(use_low, full - high, high)
             out_ref[parity, h * part : (h + 1) * part, :] = value.astype(BF16)
+    const = 0.0
+    for h in range(hid):
+        coef_ref[h] = jnp.full(coef_ref.shape[1:], -bias_ref[h], F32)
+        coef_ref[hid + h] = jnp.full(coef_ref.shape[1:], head_ref[h], F32)
+        const = const + head_ref[h] * bias_ref[h]
+    coef_ref[2 * hid] = jnp.full(coef_ref.shape[1:], const, F32)
 
 
 def heat_kernel(
     pieces,
+    queries,
     order,
-    frame_ref,
-    bias_ref,
-    head_ref,
     *refs,
 ):
-    q_refs = refs[:pieces]
-    maps_ref, weight_ref = refs[pieces : pieces + 2]
-    out_refs = refs[pieces + 2 : 2 * pieces + 2]
-    cost_ref, high_ref, low_ref, edge_high, edge_low, logit_ref, full_ref = refs[2 * pieces + 2 :]
+    q_refs = refs[:queries]
+    maps_ref, weight_ref, coef_ref = refs[queries : queries + 3]
+    rest = refs[queries + 3 :]
+    out_refs = rest[:pieces]
+    cost_ref, high_ref, low_ref, edge_high, edge_low, logit_ref, full_ref = rest[pieces:]
     pixels, chan = maps_ref.shape
     slots = q_refs[0].shape[0]
-    hid = bias_ref.shape[0]
+    hid = coef_ref.shape[0] // 2
     part = 2 * TILE
+    here = lax.axis_index("frame").astype(jnp.int32)
     query = q_refs[0][...].astype(F32)
     for ref in q_refs[1:]:
         query = query + ref[...].astype(F32)
@@ -147,13 +161,9 @@
         low_ref[pl.ds(to, step), :] = (cost - high.astype(F32)).astype(BF16)
         return carry
 
-    lax.fori_loop(0, pixels // step, cost_step, 0)
+    lax.fori_loop(0, pixels // step, cost_step, 0, unroll=4)
 
     cols = GRID_W // TILE
-    const = 0.0
-    for h in range(hid):
-        const = const + head_ref[h] * bias_ref[h]
-
     def window_step(j, best):
         for k in range(cols):
             base = j * 4 * GRID_W + k * TILE
@@ -185,21 +195,22 @@
                     )
                 window = jnp.concatenate(sides, axis=1)
                 act = jnp.dot(weight_ref[parity], window, preferred_element_type=F32)
-                acc = jnp.full((part, 2 * slots), const, F32)
-                for h in range(hid):
-                    acc = acc + head_ref[h] * jnp.maximum(
-                        act[h * part : (h + 1) * part], -bias_ref[h]
-                    )
                 for side in range(2):
                     k = 2 * pair + side
-                    for rr in range(2):
-                        piece = acc[rr * TILE : (rr + 1) * TILE, side * slots : (side + 1) * slots]
-                        to = pl.multiple_of(top + rr * GRID_W + k * TILE, TILE)
-                        logit_ref[pl.ds(to, TILE), :] = piece
-                        best = jnp.maximum(best, jnp.maximum(piece[:8], piece[8:]))
+                    lanes = slice(side * slots, (side + 1) * slots)
+                    for q in range(part // 8):
+                        acc = coef_ref[2 * hid]
+                        for h in range(hid):
+                            at = h * part + 8 * q
+                            acc = acc + coef_ref[hid + h] * jnp.maximum(
+                                act[at : at + 8, lanes], coef_ref[h]
+                            )
+                        to = top + (8 * q // TILE) * GRID_W + k * TILE + 8 * q % TILE
+                        logit_ref[pl.ds(pl.multiple_of(to, 8), 8), :] = acc
+                        best = jnp.maximum(best, acc)
         return best
 
-    best = lax.fori_loop(0, GRID_H // 4, window_step, jnp.full((8, slots), -jnp.inf, F32))
+    best = lax.fori_loop(0, GRID_H // 4, window_step, jnp.full((8, slots), -jnp.inf, F32), unroll=8)
     top_value = jnp.max(best, axis=0, keepdims=True)
 
     def exp_step(n, carry):
@@ -217,7 +228,7 @@
         return row_acc, col_acc
 
     row_acc, col_acc = lax.fori_loop(
-        0, GRID_H // 4, exp_step, (jnp.zeros((8, slots), F32), jnp.zeros((GRID_W, slots), F32))
+        0, GRID_H // 4, exp_step, (jnp.zeros((8, slots), F32), jnp.zeros((GRID_W, slots), F32)), unroll=4
     )
     total = jnp.sum(col_acc, axis=0, keepdims=True)
     inverse = 1.0 / total
@@ -230,24 +241,25 @@
         heat = (logit_ref[pl.ds(at, step), :] * inverse).astype(BF16)
         return acc + jnp.dot(heat.T, maps_ref[pl.ds(at, step), :], preferred_element_type=F32)
 
-    sampled = lax.fori_loop(0, pixels // step, sample_step, jnp.zeros((slots, chan), F32))
+    sampled = lax.fori_loop(0, pixels // step, sample_step, jnp.zeros((slots, chan), F32), unroll=4)
     rest = jnp.concatenate([row_est, col_est, jnp.zeros((LANES - 2, slots), F32)], axis=0)
     sub = slots // pieces
     full_ref[:, :, :chan] = sampled.astype(BF16).reshape(pieces, sub, chan)
     full_ref[:, :, chan:] = rest.T.astype(BF16).reshape(pieces, sub, LANES)
     for m in range(pieces):
-        out_refs[m][...] = full_ref[peer(order, frame_ref[0], m, pieces)]
-
-
-def mix_kernel(order, frames, frame_ref, *refs):
+        out_refs[m][...] = full_ref[peer(order, here, m, pieces)]
+
+
+def mix_kernel(order, frames, *refs):
     got_refs = refs[:frames]
     mix_in_ref, taps_ref, gain_ref, mix_out_ref, out_ref, z_ref, place_ref = refs[frames:]
     chan = mix_in_ref.shape[0]
     rows = got_refs[0].shape[0]
+    here = lax.axis_index("frame").astype(jnp.int32)
     joined = jnp.concatenate([ref[...] for ref in got_refs], axis=0)
     z = jnp.dot(joined[:, :chan], mix_in_ref[...], preferred_element_type=F32)
     for m in range(frames):
-        source = peer(order, frame_ref[0], -m, frames)
+        source = peer(order, here, -m, frames)
         z_ref[source] = z[m * rows : (m + 1) * rows]
         place_ref[source] = got_refs[m][:, chan:]
     place = place_ref[...].astype(F32).reshape(frames * rows, LANES).T[:8]
@@ -281,6 +293,10 @@
     return lax.rem(here + m + count, count)
 
 
+def in_hbm(x):
+    return pltpu.with_memory_space_constraint(x, pltpu.MemorySpace.HBM)
+
+
 def in_vmem(x):
     return pltpu.with_memory_space_constraint(x, pltpu.MemorySpace.VMEM)
 
@@ -301,8 +317,6 @@
 ):
     frame_count = lax.axis_size("frame")
     track_count = lax.axis_size("track")
-    frame_here = lax.axis_index("frame").astype(jnp.int32)
-    track_here = lax.axis_index("track").astype(jnp.int32)
     f_dev, pixels, chan = feature_maps.shape
     total = track_order.shape[0]
     tr_dev = total // track_count
@@ -318,43 +332,56 @@
         return lax.ppermute(x, "frame", pairs)
 
     limits = pltpu.CompilerParams(vmem_limit_bytes=24 << 20)
-    place = jnp.stack([frame_here, track_here])
+    any_spec = pl.BlockSpec(memory_space=pl.ANY)
     picks, held = pl.pallas_call(
         functools.partial(pick_kernel, frame_count, track_count),
         name="pick",
         out_shape=(pltpu.VMEM((tr_dev, chan), BF16), pltpu.VMEM((pixels, chan), BF16)),
-        in_specs=[SMEM_SPEC] + [VMEM_SPEC] * 4 + [pl.BlockSpec(memory_space=pl.ANY)],
+        in_specs=[any_spec] * 5,
         out_specs=(VMEM_SPEC, VMEM_SPEC),
-        scratch_shapes=[pltpu.SemaphoreType.DMA((4,))],
+        scratch_shapes=[
+            pltpu.VMEM((4, 1, total), jnp.int32),
+            pltpu.SemaphoreType.DMA((4,)),
+            pltpu.SemaphoreType.DMA((4,)),
+        ],
         compiler_params=limits,
     )(
-        place,
-        track_order.reshape(1, total),
-        query_frame.reshape(1, total),
-        query_row.reshape(1, total),
-        query_col.reshape(1, total),
-        maps,
-    )
-    queries = [picks] + [send(picks, m) for m in range(1, frame_count)]
+        in_hbm(track_order.reshape(1, total)),
+        in_hbm(query_frame.reshape(1, total)),
+        in_hbm(query_row.reshape(1, total)),
+        in_hbm(query_col.reshape(1, total)),
+        in_hbm(maps),
+    )
+    if order == "xor":
+        queries, reach = [picks], 1
+        while reach < frame_count:
+            mine = queries[0] if len(queries) == 1 else queries[0] + queries[1]
+            queries = [mine, send(mine, reach)]
+            reach *= 2
+    else:
+        queries = [picks] + [send(picks, m) for m in range(1, frame_count)]
 
     part = 2 * TILE
-    weight = pl.pallas_call(
+    weight, coef = pl.pallas_call(
         prep_kernel,
         name="prep",
-        out_shape=pltpu.VMEM((2, hid * part, KDIM), BF16),
-        in_specs=[SMEM_SPEC],
-        out_specs=VMEM_SPEC,
+        out_shape=(
+            pltpu.VMEM((2, hid * part, KDIM), BF16),
+            pltpu.VMEM((2 * hid + 1, 8, tr_dev), F32),
+        ),
+        in_specs=[SMEM_SPEC] * 3,
+        out_specs=(VMEM_SPEC, VMEM_SPEC),
         compiler_params=limits,
-    )(conv_weight)
+    )(conv_weight, conv_bias, head_weight)
 
     padded = ROWS_PAD * GRID_W
     pieces = pl.pallas_call(
-        functools.partial(heat_kernel, frame_count, order),
+        functools.partial(heat_kernel, frame_count, len(queries), order),
         name="heat",
         out_shape=tuple(
             pltpu.VMEM((sub_rows, chan + LANES), BF16) for _ in range(frame_count)
         ),
-        in_specs=[SMEM_SPEC] * 3 + [VMEM_SPEC] * (frame_count + 2),
+        in_specs=[VMEM_SPEC] * (len(queries) + 3),
         out_specs=tuple(VMEM_SPEC for _ in range(frame_count)),
         scratch_shapes=[
             pltpu.VMEM((padded, tr_dev), F32),
@@ -367,19 +394,17 @@
         ],
         compiler_params=limits,
     )(
-        frame_here.reshape(1),
-        conv_bias,
-        head_weight,
         *[in_vmem(q) for q in queries],
         in_vmem(held),
         in_vmem(weight),
+        in_vmem(coef),
     )
     got = [pieces[0]] + [send(pieces[m], m) for m in range(1, frame_count)]
     mixed = pl.pallas_call(
         functools.partial(mix_kernel, order, frame_count),
         name="mix",
         out_shape=jax.ShapeDtypeStruct((mix_out.shape[1], frame_count, sub_rows), F32),
-        in_specs=[SMEM_SPEC] + [VMEM_SPEC] * (frame_count + 4),
+        in_specs=[VMEM_SPEC] * (frame_count + 4),
         out_specs=VMEM_SPEC,
         scratch_shapes=[
             pltpu.VMEM((frame_count, sub_rows, mixw), F32),
@@ -387,7 +412,6 @@
         ],
         compiler_params=limits,
     )(
-        frame_here.reshape(1),
         *[in_vmem(g) for g in got],
         in_vmem(mix_in),
         in_vmem(temporal_taps),

time: 40.5 us -> 32.9 us (0.81)
  Pallas kernels: 17.5 us -> 12.7 us
  local copies, waits for them, and re-layouts: 4.35 us -> 0.03 us
  starting transfers between devices: 10.2 us -> 11.4 us
  waiting for transfers between devices: 8 us -> 8.62 us
    pallas_call x2, Pallas kernels: 14 us -> 8.58 us  [the longest x1 7.1 us: on_device(): pl.pallas_call(functools.partial(heat_kernel, frame_count, len(queries),...]
    unnamed x24 -> x14, local copies, waits for them, and re-layouts: 4.35 us -> 0.03 us
    ppermute x6 -> x5, starting transfers between devices: 10.2 us -> 11.4 us  [send(): return lax.ppermute(x, 'frame', pairs)]
    ppermute x6 -> x5, waiting for transfers between devices: 8 us -> 8.62 us  [send(): return lax.ppermute(x, 'frame', pairs)]
    pallas_call x1, Pallas kernels: 2.11 us -> 2.69 us  [on_device(): pl.pallas_call(functools.partial(pick_kernel, frame_count, track_count),...]
  transfers between devices with their start and end apart: 6 -> 5, of which waited for: 4 -> 4; matrix products, arithmetic and copies ran while one was open for 0% -> 0% of each run, Pallas kernels for 4% -> 5%
where the time goes in v3:
time: 32.9 us; the launch traced here: 32.8 us
  Pallas kernels  12.7 us (39%)
  starting transfers between devices  11.4 us (35%)
  waiting for transfers between devices  8.62 us (26%)
    ppermute x5, starting transfers between devices, send(): return lax.ppermute(x, 'frame', pairs)  11.4 us
    ppermute x5, waiting for transfers between devices, send(): return lax.ppermute(x, 'frame', pairs)  8.62 us
    pallas_call x1, Pallas kernels, on_device(): pl.pallas_call(functools.partial(heat_kernel, frame_count, len(queries),...  7.1 us
    pallas_call x1, Pallas kernels, on_device(): pl.pallas_call(functools.partial(pick_kernel, frame_count, track_count),...  2.69 us
    pallas_call x1, Pallas kernels, on_device(): pl.pallas_call(prep_kernel, name='prep', out_shape=(pltpu.VMEM((2, hid *...  1.48 us
    pallas_call x1, Pallas kernels, on_device(): pl.pallas_call(functools.partial(mix_kernel, order, frame_count), name='m...  1.39 us
  transfers between devices with their start and end apart: 5, of which 4 were waited for; matrix products, arithmetic and copies ran while one was open for 0% of the time, Pallas kernels for 5%

profile of v3, /device:TPU:0, one launch (start us, length us, event | category | flops | bytes accessed | tf_op | source)
XLA Modules:
  0.0 32.8 jit_solution(3771748791412698329)
XLA Ops:
  0.0 0.0 copy-start.6
  0.0 0.0 copy-start.5
  0.0 0.0 copy-start.3
  0.0 0.0 copy-start
  0.0 0.0 copy-start.1
  0.0 0.0 copy-start.2
  0.0 0.0 copy-start.4
  0.0 2.7 %pick.1 = (bf16[128,256]{1,0:T(8,128)(2,1)S(1)}, bf16[4096,256]{1,0:T(8,128)(2,1)S(1)}) custom-call(s32[1,512]{1,0:T(1,128)} %bitcast.11, s32[1,512]{1,0:T(1,128)} %bitcast.12, s32[1,512]{1,0:T(1,128)} %bitcast.13, s32[1,512]{1,0:T(1,128)} %bitcast.14, bf16[4096,256]{1,0:T(8,128)(2,1)} %bitcast.10), custom_call_target="tpu_custom_call" | custom-call | tf_op jit(solution)/shard_map/pick/pallas_call | solution.py:336
  2.7 3.1 %collective-permute-start = (bf16[128,256]{1,0:T(8,128)(2,1)S(1)}, bf16[128,256]{1,0:T(8,128)(2,1)S(1)}, u32[]{:S(2)}, u32[]{:S(2)}) collective-permute-start(bf16[128,256]{1,0:T(8,128)(2,1)S(1)} %get-tuple-element.13), channel_id=1, source_target_pairs={{0,4},{4,0},{8,12},{12,8},{1,5},{5,1},{9,13},{13,9},{2,6},{6,2},{1... | collective-permute-start | bytes 196616 | tf_op jit(solution)/shard_map/ppermute | solution.py:332
  5.9 2.2 %collective-permute-done = bf16[128,256]{1,0:T(8,128)(2,1)S(1)} collective-permute-done((bf16[128,256]{1,0:T(8,128)(2,1)S(1)}, bf16[128,256]{1,0:T(8,128)(2,1)S(1)}, u32[]{:S(2)}, u32[]{:S(2)}) %collective-permute-start) | collective-permute-done | bytes 65568 | tf_op jit(solution)/shard_map/ppermute | solution.py:332
  8.1 3.1 %collective-permute-start.1 = (bf16[128,256]{1,0:T(8,128)(2,1)S(1)}, bf16[128,256]{1,0:T(8,128)(2,1)S(1)}, u32[]{:S(2)}, u32[]{:S(2)}) collective-permute-start(bf16[128,256]{1,0:T(8,128)(2,1)S(1)} %add.3.refs_0_), channel_id=1, source_target_pairs={{0,8},{4,12},{8,0},{12,4},{1,9},{5,13},{9,1},{13,5},{2,10},{6,14},... | collective-permute-start | bytes 196616 | tf_op jit(solution)/shard_map/ppermute | solution.py:332
  11.2 0.0 copy-done.6
  11.2 0.0 copy-done.5
  11.2 0.0 copy-done.3
  11.2 1.5 %prep.1 = (bf16[2,512,256]{2,1,0:T(8,128)(2,1)S(1)}, f32[33,8,128]{2,1,0:T(8,128)S(1)}) custom-call(f32[16,9]{1,0:T(8,128)S(1)} %copy-done.3, f32[16]{0:T(128)S(1)} %copy-done.5, f32[16]{0:T(128)S(1)} %copy-done.6), custom_call_target="tpu_custom_call" | custom-call | tf_op jit(solution)/shard_map/prep/pallas_call | solution.py:365
  12.7 0.8 %collective-permute-done.1.refs_1_ = bf16[128,256]{1,0:T(8,128)(2,1)S(1)} collective-permute-done((bf16[128,256]{1,0:T(8,128)(2,1)S(1)}, bf16[128,256]{1,0:T(8,128)(2,1)S(1)}, u32[]{:S(2)}, u32[]{:S(2)}) %collective-permute-start.1) | collective-permute-done | bytes 65568 | tf_op jit(solution)/shard_map/ppermute | solution.py:332
  13.5 7.1 %heat.1 = (bf16[32,384]{1,0:T(8,128)(2,1)S(1)}, bf16[32,384]{1,0:T(8,128)(2,1)S(1)}, bf16[32,384]{1,0:T(8,128)(2,1)S(1)}, bf16[32,384]{1,0:T(8,128)(2,1)S(1)}) custom-call(bf16[128,256]{1,0:T(8,128)(2,1)S(1)} %add.3.refs_0_, bf16[128,256]{1,0:T(8,128)(2,1)S(1)} %collective-permute-done.1.refs_1_, bf16[4096,256]{1,0:T(8,128)(2,1)S(1)} %get-tuple-element.14.refs_2_, ...), custom_call_target="tpu_custom_call" | custom-call | tf_op jit(solution)/shard_map/heat/pallas_call | solution.py:378
  20.6 2.0 %collective-permute-start.2 = (bf16[32,384]{1,0:T(8,128)(2,1)S(1)}, bf16[32,384]{1,0:T(8,128)(2,1)S(1)}, u32[]{:S(2)}, u32[]{:S(2)}) collective-permute-start(bf16[32,384]{1,0:T(8,128)(2,1)S(1)} %get-tuple-element.18), channel_id=1, source_target_pairs={{0,4},{4,0},{8,12},{12,8},{1,5},{5,1},{9,13},{13,9},{2,6},{6,2},{1... | collective-permute-start | bytes 73736 | tf_op jit(solution)/shard_map/ppermute | solution.py:332
  22.6 3.2 %collective-permute-start.3 = (bf16[32,384]{1,0:T(8,128)(2,1)S(1)}, bf16[32,384]{1,0:T(8,128)(2,1)S(1)}, u32[]{:S(2)}, u32[]{:S(2)}) collective-permute-start(bf16[32,384]{1,0:T(8,128)(2,1)S(1)} %get-tuple-element.19), channel_id=1, source_target_pairs={{0,8},{4,12},{8,0},{12,4},{1,9},{5,13},{9,1},{13,5},{2,10},{6,14},... | collective-permute-start | bytes 73736 | tf_op jit(solution)/shard_map/ppermute | solution.py:332
  25.7 0.0 collective-permute-start.4
  25.7 0.0 collective-permute-done.2.refs_1_
  25.7 2.0 %collective-permute-done.3.refs_2_ = bf16[32,384]{1,0:T(8,128)(2,1)S(1)} collective-permute-done((bf16[32,384]{1,0:T(8,128)(2,1)S(1)}, bf16[32,384]{1,0:T(8,128)(2,1)S(1)}, u32[]{:S(2)}, u32[]{:S(2)}) %collective-permute-start.3) | collective-permute-done | bytes 24608 | tf_op jit(solution)/shard_map/ppermute | solution.py:332
  27.8 3.6 %collective-permute-done.4.refs_3_ = bf16[32,384]{1,0:T(8,128)(2,1)S(1)} collective-permute-done((bf16[32,384]{1,0:T(8,128)(2,1)S(1)}, bf16[32,384]{1,0:T(8,128)(2,1)S(1)}, u32[]{:S(2)}, u32[]{:S(2)}) %collective-permute-start.4) | collective-permute-done | bytes 24608 | tf_op jit(solution)/shard_map/ppermute | solution.py:332
  31.4 0.0 copy-done
  31.4 0.0 copy-done.1
  31.4 0.0 copy-done.2
  31.4 0.0 copy-done.4
  31.4 1.4 %mix.1 = f32[3,4,32]{2,1,0:T(4,128)} custom-call(bf16[32,384]{1,0:T(8,128)(2,1)S(1)} %get-tuple-element.17.refs_0_, bf16[32,384]{1,0:T(8,128)(2,1)S(1)} %collective-permute-done.2.refs_1_, bf16[32,384]{1,0:T(8,128)(2,1)S(1)} %collective-permute-done.3.refs_2_, bf16[32,384]{1,0:T(8,128)(2,1)S(1)} %collective-permute-done.4.refs_3_, ...), custom_call_target="tpu_custom_call" | custom-call | tf_op jit(solution)/shard_map/mix/pallas_call | solution.py:403
  (1 shorter events, 0.0 us)
Async XLA Ops:
  0.0 11.2 %copy-start.6 = (f32[16]{0:T(128)S(1)}, f32[16]{0:T(128)}, u32[]{:S(2)}) copy-start(f32[16]{0:T(128)} %head_ref.1) | copy-start | bytes 196
  0.0 11.2 %copy-start.5 = (f32[16]{0:T(128)S(1)}, f32[16]{0:T(128)}, u32[]{:S(2)}) copy-start(f32[16]{0:T(128)} %bias_ref.1) | copy-start | bytes 196
  0.0 11.2 %copy-start.3 = (f32[16,9]{1,0:T(8,128)S(1)}, f32[16,9]{1,0:T(8,128)}, u32[]{:S(2)}) copy-start(f32[16,9]{1,0:T(8,128)} %weight_ref.1) | copy-start | bytes 1732
  0.0 31.4 %copy-start = (bf16[256,1024]{1,0:T(8,128)(2,1)S(1)}, bf16[256,1024]{1,0:T(8,128)(2,1)}, u32[]{:S(2)}) copy-start(bf16[256,1024]{1,0:T(8,128)(2,1)} %refs_4_.1) | copy-start | bytes 1572868
  0.0 31.4 %copy-start.1 = (f32[3,1024]{1,0:T(4,128)S(1)}, f32[3,1024]{1,0:T(4,128)}, u32[]{:S(2)}) copy-start(f32[3,1024]{1,0:T(4,128)} %refs_5_.1) | copy-start | bytes 36868
  0.0 31.4 %copy-start.2 = (bf16[1024,3]{0,1:T(4,128)(2,1)S(1)}, bf16[1024,3]{0,1:T(4,128)(2,1)}, u32[]{:S(2)}) copy-start(bf16[1024,3]{0,1:T(4,128)(2,1)} %param.23) | copy-start | bytes 18436
  0.0 31.3 %copy-start.4 = (f32[1024]{0:T(1024)S(1)}, f32[1024]{0:T(1024)}, u32[]{:S(2)}) copy-start(f32[1024]{0:T(1024)} %param.22) | copy-start | bytes 12292
  2.7 5.4 %collective-permute-start = (bf16[128,256]{1,0:T(8,128)(2,1)S(1)}, bf16[128,256]{1,0:T(8,128)(2,1)S(1)}, u32[]{:S(2)}, u32[]{:S(2)}) collective-permute-start(bf16[128,256]{1,0:T(8,128)(2,1)S(1)} %get-tuple-element.13), channel_id=1, source_target_pairs={{0,4},{4,0},{8,12},{12,8},{1,5},{5,1},{9,13},{13,9},{2,6},{6,2},{1... | collective-permute-start | bytes 196616 | tf_op jit(solution)/shard_map/ppermute | solution.py:332
  8.1 5.3 %collective-permute-start.1 = (bf16[128,256]{1,0:T(8,128)(2,1)S(1)}, bf16[128,256]{1,0:T(8,128)(2,1)S(1)}, u32[]{:S(2)}, u32[]{:S(2)}) collective-permute-start(bf16[128,256]{1,0:T(8,128)(2,1)S(1)} %add.3.refs_0_), channel_id=1, source_target_pairs={{0,8},{4,12},{8,0},{12,4},{1,9},{5,13},{9,1},{13,5},{2,10},{6,14},... | collective-permute-start | bytes 196616 | tf_op jit(solution)/shard_map/ppermute | solution.py:332
  20.6 5.2 %collective-permute-start.2 = (bf16[32,384]{1,0:T(8,128)(2,1)S(1)}, bf16[32,384]{1,0:T(8,128)(2,1)S(1)}, u32[]{:S(2)}, u32[]{:S(2)}) collective-permute-start(bf16[32,384]{1,0:T(8,128)(2,1)S(1)} %get-tuple-element.18), channel_id=1, source_target_pairs={{0,4},{4,0},{8,12},{12,8},{1,5},{5,1},{9,13},{13,9},{2,6},{6,2},{1... | collective-permute-start | bytes 73736 | tf_op jit(solution)/shard_map/ppermute | solution.py:332
  22.6 5.2 %collective-permute-start.3 = (bf16[32,384]{1,0:T(8,128)(2,1)S(1)}, bf16[32,384]{1,0:T(8,128)(2,1)S(1)}, u32[]{:S(2)}, u32[]{:S(2)}) collective-permute-start(bf16[32,384]{1,0:T(8,128)(2,1)S(1)} %get-tuple-element.19), channel_id=1, source_target_pairs={{0,8},{4,12},{8,0},{12,4},{1,9},{5,13},{9,1},{13,5},{2,10},{6,14},... | collective-permute-start | bytes 73736 | tf_op jit(solution)/shard_map/ppermute | solution.py:332
  25.7 5.6 %collective-permute-start.4 = (bf16[32,384]{1,0:T(8,128)(2,1)S(1)}, bf16[32,384]{1,0:T(8,128)(2,1)S(1)}, u32[]{:S(2)}, u32[]{:S(2)}) collective-permute-start(bf16[32,384]{1,0:T(8,128)(2,1)S(1)} %get-tuple-element.20), channel_id=1, source_target_pairs={{0,12},{4,8},{8,4},{12,0},{1,13},{5,9},{9,5},{13,1},{2,14},{6,10},... | collective-permute-start | bytes 73736 | tf_op jit(solution)/shard_map/ppermute | solution.py:332

commit v4 on v3

--- a/solution.py
+++ b/solution.py
@@ -125,7 +125,6 @@
 def heat_kernel(
     pieces,
     queries,
-    order,
     *refs,
 ):
     q_refs = refs[:queries]
@@ -247,10 +246,10 @@
     full_ref[:, :, :chan] = sampled.astype(BF16).reshape(pieces, sub, chan)
     full_ref[:, :, chan:] = rest.T.astype(BF16).reshape(pieces, sub, LANES)
     for m in range(pieces):
-        out_refs[m][...] = full_ref[peer(order, here, m, pieces)]
-
-
-def mix_kernel(order, frames, *refs):
+        out_refs[m][...] = full_ref[ahead(here, m, pieces)]
+
+
+def mix_kernel(frames, *refs):
     got_refs = refs[:frames]
     mix_in_ref, taps_ref, gain_ref, mix_out_ref, out_ref, z_ref, place_ref = refs[frames:]
     chan = mix_in_ref.shape[0]
@@ -259,7 +258,7 @@
     joined = jnp.concatenate([ref[...] for ref in got_refs], axis=0)
     z = jnp.dot(joined[:, :chan], mix_in_ref[...], preferred_element_type=F32)
     for m in range(frames):
-        source = peer(order, here, -m, frames)
+        source = ahead(here, -m, frames)
         z_ref[source] = z[m * rows : (m + 1) * rows]
         place_ref[source] = got_refs[m][:, chan:]
     place = place_ref[...].astype(F32).reshape(frames * rows, LANES).T[:8]
@@ -285,9 +284,7 @@
         out_ref[:, t, :] = result[:, t * rows : (t + 1) * rows]
 
 
-def peer(order, here, m, count):
-    if order == "xor":
-        return here ^ abs(m)
+def ahead(here, m, count):
     if isinstance(here, int):
         return (here + m) % count
     return lax.rem(here + m + count, count)
@@ -325,11 +322,12 @@
     mixw = mix_in.shape[1]
     maps = feature_maps.reshape(f_dev * pixels, chan)
 
-    order = "xor" if frame_count & (frame_count - 1) == 0 else "ring"
-
     def send(x, m):
-        pairs = [(i, peer(order, i, m, frame_count)) for i in range(frame_count)]
+        pairs = [(i, ahead(i, m, frame_count)) for i in range(frame_count)]
         return lax.ppermute(x, "frame", pairs)
+
+    def swap(x, m):
+        return lax.ppermute(x, "frame", [(i, i ^ m) for i in range(frame_count)])
 
     limits = pltpu.CompilerParams(vmem_limit_bytes=24 << 20)
     any_spec = pl.BlockSpec(memory_space=pl.ANY)
@@ -352,12 +350,9 @@
         in_hbm(query_col.reshape(1, total)),
         in_hbm(maps),
     )
-    if order == "xor":
-        queries, reach = [picks], 1
-        while reach < frame_count:
-            mine = queries[0] if len(queries) == 1 else queries[0] + queries[1]
-            queries = [mine, send(mine, reach)]
-            reach *= 2
+    if frame_count & (frame_count - 1) == 0:
+        others = [1, *range(frame_count - 1, 1, -1)]
+        queries = [picks] + [swap(picks, m) for m in others]
     else:
         queries = [picks] + [send(picks, m) for m in range(1, frame_count)]
 
@@ -376,7 +371,7 @@
 
     padded = ROWS_PAD * GRID_W
     pieces = pl.pallas_call(
-        functools.partial(heat_kernel, frame_count, len(queries), order),
+        functools.partial(heat_kernel, frame_count, len(queries)),
         name="heat",
         out_shape=tuple(
             pltpu.VMEM((sub_rows, chan + LANES), BF16) for _ in range(frame_count)
@@ -401,7 +396,7 @@
     )
     got = [pieces[0]] + [send(pieces[m], m) for m in range(1, frame_count)]
     mixed = pl.pallas_call(
-        functools.partial(mix_kernel, order, frame_count),
+        functools.partial(mix_kernel, frame_count),
         name="mix",
         out_shape=jax.ShapeDtypeStruct((mix_out.shape[1], frame_count, sub_rows), F32),
         in_specs=[VMEM_SPEC] * (frame_count + 4),

time: 32.9 us -> 29.4 us (0.89)
  waiting for transfers between devices: 8.62 us -> 5.02 us
    ppermute x5 -> x3, waiting for transfers between devices: 8.62 us -> 1.78 us  [send(): return lax.ppermute(x, 'frame', pairs)]
    ppermute x0 -> x3, starting transfers between devices: none -> 5.73 us  [swap(): return lax.ppermute(x, 'frame', [(i, i ^ m) for i in range(frame_count)])]
    ppermute x5 -> x3, starting transfers between devices: 11.4 us -> 5.65 us  [send(): return lax.ppermute(x, 'frame', pairs)]
    ppermute x0 -> x3, waiting for transfers between devices: none -> 3.24 us  [swap(): return lax.ppermute(x, 'frame', [(i, i ^ m) for i in range(frame_count)])]
  transfers between devices with their start and end apart: 5 -> 6, of which waited for: 4 -> 6; matrix products, arithmetic and copies ran while one was open for 0% -> 0% of each run, Pallas kernels for 5% -> 5%
where the time goes in v4:
time: 29.4 us; the launch traced here: 29.3 us
  Pallas kernels  12.8 us (44%)
  starting transfers between devices  11.4 us (39%)
  waiting for transfers between devices  5.02 us (17%)
    pallas_call x1, Pallas kernels, on_device(): pl.pallas_call(functools.partial(heat_kernel, frame_count, len(queries)),...  7.16 us
    ppermute x3, starting transfers between devices, swap(): return lax.ppermute(x, 'frame', [(i, i ^ m) for i in range(frame_count)])  5.73 us
    ppermute x3, starting transfers between devices, send(): return lax.ppermute(x, 'frame', pairs)  5.65 us
    ppermute x3, waiting for transfers between devices, swap(): return lax.ppermute(x, 'frame', [(i, i ^ m) for i in range(frame_count)])  3.24 us
    pallas_call x1, Pallas kernels, on_device(): pl.pallas_call(functools.partial(pick_kernel, frame_count, track_count),...  2.69 us
    ppermute x3, waiting for transfers between devices, send(): return lax.ppermute(x, 'frame', pairs)  1.78 us
    pallas_call x1, Pallas kernels, on_device(): pl.pallas_call(functools.partial(mix_kernel, frame_count), name='mix', ou...  1.49 us
    pallas_call x1, Pallas kernels, on_device(): pl.pallas_call(prep_kernel, name='prep', out_shape=(pltpu.VMEM((2, hid *...  1.48 us
  transfers between devices with their start and end apart: 6, of which 6 were waited for; matrix products, arithmetic and copies ran while one was open for 0% of the time, Pallas kernels for 5%

profile of v4, /device:TPU:0, one launch (start us, length us, event | category | flops | bytes accessed | tf_op | source)
XLA Modules:
  0.0 29.3 jit_solution(1520962863464950415)
XLA Ops:
  0.0 0.0 copy-start.6
  0.0 0.0 copy-start.5
  0.0 0.0 copy-start.3
  0.0 0.0 copy-start
  0.0 0.0 copy-start.1
  0.0 0.0 copy-start.2
  0.0 0.0 copy-start.4
  0.0 2.7 %pick.1 = (bf16[128,256]{1,0:T(8,128)(2,1)S(1)}, bf16[4096,256]{1,0:T(8,128)(2,1)S(1)}) custom-call(s32[1,512]{1,0:T(1,128)} %bitcast.11, s32[1,512]{1,0:T(1,128)} %bitcast.12, s32[1,512]{1,0:T(1,128)} %bitcast.13, s32[1,512]{1,0:T(1,128)} %bitcast.14, bf16[4096,256]{1,0:T(8,128)(2,1)} %bitcast.10), custom_call_target="tpu_custom_call" | custom-call | tf_op jit(solution)/shard_map/pick/pallas_call | solution.py:334
  2.7 4.1 %collective-permute-start.2 = (bf16[128,256]{1,0:T(8,128)(2,1)S(1)}, bf16[128,256]{1,0:T(8,128)(2,1)S(1)}, u32[]{:S(2)}, u32[]{:S(2)}) collective-permute-start(bf16[128,256]{1,0:T(8,128)(2,1)S(1)} %get-tuple-element.13.refs_0_), channel_id=1, source_target_pairs={{0,8},{4,12},{8,0},{12,4},{1,9},{5,13},{9,1},{13,5},{2,10},{6,14},... | collective-permute-start | bytes 196616 | tf_op jit(solution)/shard_map/ppermute | solution.py:330
  6.9 1.3 %collective-permute-start.1 = (bf16[128,256]{1,0:T(8,128)(2,1)S(1)}, bf16[128,256]{1,0:T(8,128)(2,1)S(1)}, u32[]{:S(2)}, u32[]{:S(2)}) collective-permute-start(bf16[128,256]{1,0:T(8,128)(2,1)S(1)} %get-tuple-element.13.refs_0_), channel_id=1, source_target_pairs={{0,12},{4,8},{8,4},{12,0},{1,13},{5,9},{9,5},{13,1},{2,14},{6,10},... | collective-permute-start | bytes 196616 | tf_op jit(solution)/shard_map/ppermute | solution.py:330
  8.2 0.2 collective-permute-start
  8.5 0.0 copy-done.6
  8.5 0.0 copy-done.5
  8.5 0.0 copy-done.3
  8.5 1.5 %prep.1 = (bf16[2,512,256]{2,1,0:T(8,128)(2,1)S(1)}, f32[33,8,128]{2,1,0:T(8,128)S(1)}) custom-call(f32[16,9]{1,0:T(8,128)S(1)} %copy-done.3, f32[16]{0:T(128)S(1)} %copy-done.5, f32[16]{0:T(128)S(1)} %copy-done.6), custom_call_target="tpu_custom_call" | custom-call | tf_op jit(solution)/shard_map/prep/pallas_call | solution.py:360
  10.0 0.6 %collective-permute-done.2.refs_3_ = bf16[128,256]{1,0:T(8,128)(2,1)S(1)} collective-permute-done((bf16[128,256]{1,0:T(8,128)(2,1)S(1)}, bf16[128,256]{1,0:T(8,128)(2,1)S(1)}, u32[]{:S(2)}, u32[]{:S(2)}) %collective-permute-start.2) | collective-permute-done | bytes 65568 | tf_op jit(solution)/shard_map/ppermute | solution.py:330
  10.6 2.5 %collective-permute-done.1.refs_2_ = bf16[128,256]{1,0:T(8,128)(2,1)S(1)} collective-permute-done((bf16[128,256]{1,0:T(8,128)(2,1)S(1)}, bf16[128,256]{1,0:T(8,128)(2,1)S(1)}, u32[]{:S(2)}, u32[]{:S(2)}) %collective-permute-start.1) | collective-permute-done | bytes 65568 | tf_op jit(solution)/shard_map/ppermute | solution.py:330
  13.0 0.1 collective-permute-done.refs_1_
  13.2 7.2 %heat.1 = (bf16[32,384]{1,0:T(8,128)(2,1)S(1)}, bf16[32,384]{1,0:T(8,128)(2,1)S(1)}, bf16[32,384]{1,0:T(8,128)(2,1)S(1)}, bf16[32,384]{1,0:T(8,128)(2,1)S(1)}) custom-call(bf16[128,256]{1,0:T(8,128)(2,1)S(1)} %get-tuple-element.13.refs_0_, bf16[128,256]{1,0:T(8,128)(2,1)S(1)} %collective-permute-done.refs_1_, ...), custom_call_target="tpu_custom_call" | custom-call | tf_op jit(solution)/shard_map/heat/pallas_call | solution.py:373
  20.4 0.8 %collective-permute-start.3 = (bf16[32,384]{1,0:T(8,128)(2,1)S(1)}, bf16[32,384]{1,0:T(8,128)(2,1)S(1)}, u32[]{:S(2)}, u32[]{:S(2)}) collective-permute-start(bf16[32,384]{1,0:T(8,128)(2,1)S(1)} %get-tuple-element.18), channel_id=1, source_target_pairs={{0,4},{4,8},{8,12},{12,0},{1,5},{5,9},{9,13},{13,1},{2,6},{6,10},{... | collective-permute-start | bytes 73736 | tf_op jit(solution)/shard_map/ppermute | solution.py:327
  21.2 2.8 %collective-permute-start.4 = (bf16[32,384]{1,0:T(8,128)(2,1)S(1)}, bf16[32,384]{1,0:T(8,128)(2,1)S(1)}, u32[]{:S(2)}, u32[]{:S(2)}) collective-permute-start(bf16[32,384]{1,0:T(8,128)(2,1)S(1)} %get-tuple-element.19), channel_id=1, source_target_pairs={{0,8},{4,12},{8,0},{12,4},{1,9},{5,13},{9,1},{13,5},{2,10},{6,14},... | collective-permute-start | bytes 73736 | tf_op jit(solution)/shard_map/ppermute | solution.py:327
  24.0 2.0 %collective-permute-start.5 = (bf16[32,384]{1,0:T(8,128)(2,1)S(1)}, bf16[32,384]{1,0:T(8,128)(2,1)S(1)}, u32[]{:S(2)}, u32[]{:S(2)}) collective-permute-start(bf16[32,384]{1,0:T(8,128)(2,1)S(1)} %get-tuple-element.20), channel_id=1, source_target_pairs={{0,12},{4,0},{8,4},{12,8},{1,13},{5,1},{9,5},{13,9},{2,14},{6,2},{... | collective-permute-start | bytes 73736 | tf_op jit(solution)/shard_map/ppermute | solution.py:327
  26.0 0.1 collective-permute-done.3.refs_1_
  26.1 0.3 collective-permute-done.4.refs_2_
  26.4 1.4 %collective-permute-done.5.refs_3_ = bf16[32,384]{1,0:T(8,128)(2,1)S(1)} collective-permute-done((bf16[32,384]{1,0:T(8,128)(2,1)S(1)}, bf16[32,384]{1,0:T(8,128)(2,1)S(1)}, u32[]{:S(2)}, u32[]{:S(2)}) %collective-permute-start.5) | collective-permute-done | bytes 24608 | tf_op jit(solution)/shard_map/ppermute | solution.py:327
  27.8 0.0 copy-done
  27.8 0.0 copy-done.1
  27.8 0.0 copy-done.2
  27.8 0.0 copy-done.4
  27.8 1.5 %mix.1 = f32[3,4,32]{2,1,0:T(4,128)} custom-call(bf16[32,384]{1,0:T(8,128)(2,1)S(1)} %get-tuple-element.17.refs_0_, bf16[32,384]{1,0:T(8,128)(2,1)S(1)} %collective-permute-done.3.refs_1_, bf16[32,384]{1,0:T(8,128)(2,1)S(1)} %collective-permute-done.4.refs_2_, bf16[32,384]{1,0:T(8,128)(2,1)S(1)} %collective-permute-done.5.refs_3_, ...), custom_call_target="tpu_custom_call" | custom-call | tf_op jit(solution)/shard_map/mix/pallas_call | solution.py:398
Async XLA Ops:
  0.0 8.5 %copy-start.6 = (f32[16]{0:T(128)S(1)}, f32[16]{0:T(128)}, u32[]{:S(2)}) copy-start(f32[16]{0:T(128)} %head_ref.1) | copy-start | bytes 196
  0.0 8.5 %copy-start.5 = (f32[16]{0:T(128)S(1)}, f32[16]{0:T(128)}, u32[]{:S(2)}) copy-start(f32[16]{0:T(128)} %bias_ref.1) | copy-start | bytes 196
  0.0 8.5 %copy-start.3 = (f32[16,9]{1,0:T(8,128)S(1)}, f32[16,9]{1,0:T(8,128)}, u32[]{:S(2)}) copy-start(f32[16,9]{1,0:T(8,128)} %weight_ref.1) | copy-start | bytes 1732
  0.0 27.8 %copy-start = (bf16[256,1024]{1,0:T(8,128)(2,1)S(1)}, bf16[256,1024]{1,0:T(8,128)(2,1)}, u32[]{:S(2)}) copy-start(bf16[256,1024]{1,0:T(8,128)(2,1)} %refs_4_.1) | copy-start | bytes 1572868
  0.0 27.8 %copy-start.1 = (f32[3,1024]{1,0:T(4,128)S(1)}, f32[3,1024]{1,0:T(4,128)}, u32[]{:S(2)}) copy-start(f32[3,1024]{1,0:T(4,128)} %refs_5_.1) | copy-start | bytes 36868
  0.0 27.8 %copy-start.2 = (bf16[1024,3]{0,1:T(4,128)(2,1)S(1)}, bf16[1024,3]{0,1:T(4,128)(2,1)}, u32[]{:S(2)}) copy-start(bf16[1024,3]{0,1:T(4,128)(2,1)} %param.23) | copy-start | bytes 18436
  0.0 27.8 %copy-start.4 = (f32[1024]{0:T(1024)S(1)}, f32[1024]{0:T(1024)}, u32[]{:S(2)}) copy-start(f32[1024]{0:T(1024)} %param.22) | copy-start | bytes 12292
  2.7 7.9 %collective-permute-start.2 = (bf16[128,256]{1,0:T(8,128)(2,1)S(1)}, bf16[128,256]{1,0:T(8,128)(2,1)S(1)}, u32[]{:S(2)}, u32[]{:S(2)}) collective-permute-start(bf16[128,256]{1,0:T(8,128)(2,1)S(1)} %get-tuple-element.13.refs_0_), channel_id=1, source_target_pairs={{0,8},{4,12},{8,0},{12,4},{1,9},{5,13},{9,1},{13,5},{2,10},{6,14},... | collective-permute-start | bytes 196616 | tf_op jit(solution)/shard_map/ppermute | solution.py:330
  6.9 6.2 %collective-permute-start.1 = (bf16[128,256]{1,0:T(8,128)(2,1)S(1)}, bf16[128,256]{1,0:T(8,128)(2,1)S(1)}, u32[]{:S(2)}, u32[]{:S(2)}) collective-permute-start(bf16[128,256]{1,0:T(8,128)(2,1)S(1)} %get-tuple-element.13.refs_0_), channel_id=1, source_target_pairs={{0,12},{4,8},{8,4},{12,0},{1,13},{5,9},{9,5},{13,1},{2,14},{6,10},... | collective-permute-start | bytes 196616 | tf_op jit(solution)/shard_map/ppermute | solution.py:330
  8.2 5.0 %collective-permute-start = (bf16[128,256]{1,0:T(8,128)(2,1)S(1)}, bf16[128,256]{1,0:T(8,128)(2,1)S(1)}, u32[]{:S(2)}, u32[]{:S(2)}) collective-permute-start(bf16[128,256]{1,0:T(8,128)(2,1)S(1)} %get-tuple-element.13.refs_0_), channel_id=1, source_target_pairs={{0,4},{4,0},{8,12},{12,8},{1,5},{5,1},{9,13},{13,9},{2,6},{6,2},{1... | collective-permute-start | bytes 196616 | tf_op jit(solution)/shard_map/ppermute | solution.py:330
  20.4 5.8 %collective-permute-start.3 = (bf16[32,384]{1,0:T(8,128)(2,1)S(1)}, bf16[32,384]{1,0:T(8,128)(2,1)S(1)}, u32[]{:S(2)}, u32[]{:S(2)}) collective-permute-start(bf16[32,384]{1,0:T(8,128)(2,1)S(1)} %get-tuple-element.18), channel_id=1, source_target_pairs={{0,4},{4,8},{8,12},{12,0},{1,5},{5,9},{9,13},{13,1},{2,6},{6,10},{... | collective-permute-start | bytes 73736 | tf_op jit(solution)/shard_map/ppermute | solution.py:327
  21.2 5.3 %collective-permute-start.4 = (bf16[32,384]{1,0:T(8,128)(2,1)S(1)}, bf16[32,384]{1,0:T(8,128)(2,1)S(1)}, u32[]{:S(2)}, u32[]{:S(2)}) collective-permute-start(bf16[32,384]{1,0:T(8,128)(2,1)S(1)} %get-tuple-element.19), channel_id=1, source_target_pairs={{0,8},{4,12},{8,0},{12,4},{1,9},{5,13},{9,1},{13,5},{2,10},{6,14},... | collective-permute-start | bytes 73736 | tf_op jit(solution)/shard_map/ppermute | solution.py:327
  24.0 3.8 %collective-permute-start.5 = (bf16[32,384]{1,0:T(8,128)(2,1)S(1)}, bf16[32,384]{1,0:T(8,128)(2,1)S(1)}, u32[]{:S(2)}, u32[]{:S(2)}) collective-permute-start(bf16[32,384]{1,0:T(8,128)(2,1)S(1)} %get-tuple-element.20), channel_id=1, source_target_pairs={{0,12},{4,0},{8,4},{12,8},{1,13},{5,1},{9,5},{13,9},{2,14},{6,2},{... | collective-permute-start | bytes 73736 | tf_op jit(solution)/shard_map/ppermute | solution.py:327

commit v5 on v4

--- a/solution.py
+++ b/solution.py
@@ -14,6 +14,8 @@
 KDIM = 256
 ROWS_PAD = GRID_H + 4
 LANES = 128
+CHUNK = 8
+LOG2E = math.log2(math.e)
 
 VMEM_SPEC = pl.BlockSpec(memory_space=pltpu.VMEM)
 SMEM_SPEC = pl.BlockSpec(memory_space=pltpu.SMEM)
@@ -76,14 +78,16 @@
     flat = found[1:2] * GRID_W + found[2:3]
     flat = jnp.where(found[0:1] == frame_here.astype(F32), flat, -1.0)
     column = jnp.broadcast_to(flat, (slots, slots)).T[:, 0:1].astype(jnp.int32)
-    acc = jnp.zeros((slots, chan), F32)
+    spread = jnp.broadcast_to(column, (slots, step))
+    lane = iota((slots, step), 1)
+    sums = [jnp.zeros((slots, chan), F32)] * 2
     for n in range(chunks):
-        sel = jnp.where(iota((slots, step), 1) + n * step == column, 1.0, 0.0).astype(BF16)
+        sel = jnp.where(spread == lane + n * step, 1.0, 0.0).astype(BF16)
         copies[n].wait()
-        acc = acc + jnp.dot(
+        sums[n % 2] = sums[n % 2] + jnp.dot(
             sel, held_ref[n * step : (n + 1) * step, :], preferred_element_type=F32
         )
-    out_ref[...] = acc.astype(BF16)
+    out_ref[...] = (sums[0] + sums[1]).astype(BF16)
 
 
 def prep_kernel(weight_ref, bias_ref, head_ref, out_ref, coef_ref):
@@ -117,9 +121,9 @@
     const = 0.0
     for h in range(hid):
         coef_ref[h] = jnp.full(coef_ref.shape[1:], -bias_ref[h], F32)
-        coef_ref[hid + h] = jnp.full(coef_ref.shape[1:], head_ref[h], F32)
+        coef_ref[hid + h] = jnp.full(coef_ref.shape[1:], head_ref[h] * LOG2E, F32)
         const = const + head_ref[h] * bias_ref[h]
-    coef_ref[2 * hid] = jnp.full(coef_ref.shape[1:], const, F32)
+    coef_ref[2 * hid] = jnp.full(coef_ref.shape[1:], const * LOG2E, F32)
 
 
 def heat_kernel(
@@ -131,7 +135,7 @@
     maps_ref, weight_ref, coef_ref = refs[queries : queries + 3]
     rest = refs[queries + 3 :]
     out_refs = rest[:pieces]
-    cost_ref, high_ref, low_ref, edge_high, edge_low, logit_ref, full_ref = rest[pieces:]
+    cost_ref, high_ref, low_ref, edge_high, edge_low, logit_ref, peak_ref, full_ref = rest[pieces:]
     pixels, chan = maps_ref.shape
     slots = q_refs[0].shape[0]
     hid = coef_ref.shape[0] // 2
@@ -160,7 +164,7 @@
         low_ref[pl.ds(to, step), :] = (cost - high.astype(F32)).astype(BF16)
         return carry
 
-    lax.fori_loop(0, pixels // step, cost_step, 0, unroll=4)
+    lax.fori_loop(0, pixels // step, cost_step, 0, unroll=8)
 
     cols = GRID_W // TILE
     def window_step(j, best):
@@ -209,38 +213,60 @@
                         best = jnp.maximum(best, acc)
         return best
 
-    best = lax.fori_loop(0, GRID_H // 4, window_step, jnp.full((8, slots), -jnp.inf, F32), unroll=8)
+    def chunk_step(c, carry):
+        best, row_acc, col_acc = carry
+        peak = best
+        for m in range(CHUNK // 4):
+            peak = window_step(c * (CHUNK // 4) + m, peak)
+        peak_ref[c] = peak
+        shrink = jnp.exp2(best - peak)
+        row_acc = row_acc * shrink
+        col_acc = [part * shrink for part in col_acc]
+        for m in range(CHUNK):
+            r = c * CHUNK + m
+            values = []
+            for n in range(GRID_W // 8):
+                at = pl.multiple_of(r * GRID_W + 8 * n, 8)
+                value = jnp.exp2(logit_ref[pl.ds(at, 8), :] - peak)
+                logit_ref[pl.ds(at, 8), :] = value
+                col_acc[n] = col_acc[n] + value
+                values.append(value)
+            while len(values) > 1:
+                values = [x + y for x, y in zip(values[::2], values[1::2])]
+            row_acc = row_acc + values[0] * (jnp.float32(r) * (1.0 / (GRID_H - 1)))
+        return peak, row_acc, col_acc
+
+    zero = jnp.zeros((8, slots), F32)
+    best, row_acc, col_acc = lax.fori_loop(
+        0,
+        GRID_H // CHUNK,
+        chunk_step,
+        (jnp.full((8, slots), -jnp.inf, F32), zero, [zero] * (GRID_W // 8)),
+        unroll=8,
+    )
     top_value = jnp.max(best, axis=0, keepdims=True)
-
-    def exp_step(n, carry):
-        row_acc, col_acc = carry
-        for m in range(4):
-            r = n * 4 + m
-            at = pl.multiple_of(r * GRID_W, GRID_W)
-            value = jnp.exp(logit_ref[pl.ds(at, GRID_W), :] - top_value)
-            logit_ref[pl.ds(at, GRID_W), :] = value
-            col_acc = col_acc + value
-            parts = [value[8 * n : 8 * n + 8] for n in range(GRID_W // 8)]
-            while len(parts) > 1:
-                parts = [a + b for a, b in zip(parts[::2], parts[1::2])]
-            row_acc = row_acc + parts[0] * (r.astype(F32) * (1.0 / (GRID_H - 1)))
-        return row_acc, col_acc
-
-    row_acc, col_acc = lax.fori_loop(
-        0, GRID_H // 4, exp_step, (jnp.zeros((8, slots), F32), jnp.zeros((GRID_W, slots), F32)), unroll=4
-    )
-    total = jnp.sum(col_acc, axis=0, keepdims=True)
-    inverse = 1.0 / total
-    row_est = jnp.sum(row_acc, axis=0, keepdims=True) * inverse
-    col_pos = iota((GRID_W, slots), 0).astype(F32) * (1.0 / (GRID_W - 1))
-    col_est = jnp.sum(col_acc * col_pos, axis=0, keepdims=True) * inverse
-
-    def sample_step(n, acc):
-        at = pl.multiple_of(n * step, step)
-        heat = (logit_ref[pl.ds(at, step), :] * inverse).astype(BF16)
-        return acc + jnp.dot(heat.T, maps_ref[pl.ds(at, step), :], preferred_element_type=F32)
-
-    sampled = lax.fori_loop(0, pixels // step, sample_step, jnp.zeros((slots, chan), F32), unroll=4)
+    shrink = jnp.exp2(best - top_value)
+    total, col_sum = zero, zero
+    for n in range(GRID_W // 8):
+        col_pos = (iota((8, slots), 0) + 8 * n).astype(F32) * (1.0 / (GRID_W - 1))
+        total = total + col_acc[n]
+        col_sum = col_sum + col_acc[n] * col_pos
+    inverse = 1.0 / jnp.sum(total * shrink, axis=0, keepdims=True)
+    row_est = jnp.sum(row_acc * shrink, axis=0, keepdims=True) * inverse
+    col_est = jnp.sum(col_sum * shrink, axis=0, keepdims=True) * inverse
+
+    span = CHUNK * GRID_W
+
+    def sample_step(c, acc):
+        at = pl.multiple_of(c * span, span)
+        factor = jnp.exp2(peak_ref[c] - top_value) * inverse
+        heat = logit_ref[pl.ds(at, span), :].reshape(span // 8, 8, slots) * factor
+        heat = heat.reshape(span, slots).astype(BF16)
+        return acc + jnp.dot(heat.T, maps_ref[pl.ds(at, span), :], preferred_element_type=F32)
+
+    sampled = lax.fori_loop(
+        0, GRID_H // CHUNK, sample_step, jnp.zeros((slots, chan), F32), unroll=8
+    )
     rest = jnp.concatenate([row_est, col_est, jnp.zeros((LANES - 2, slots), F32)], axis=0)
     sub = slots // pieces
     full_ref[:, :, :chan] = sampled.astype(BF16).reshape(pieces, sub, chan)
@@ -340,7 +366,7 @@
         scratch_shapes=[
             pltpu.VMEM((4, 1, total), jnp.int32),
             pltpu.SemaphoreType.DMA((4,)),
-            pltpu.SemaphoreType.DMA((4,)),
+            pltpu.SemaphoreType.DMA((2,)),
         ],
         compiler_params=limits,
     )(
@@ -385,6 +411,7 @@
             pltpu.VMEM((GRID_W // TILE, TILE, tr_dev), BF16),
             pltpu.VMEM((GRID_W // TILE, TILE, tr_dev), BF16),
             pltpu.VMEM((pixels, tr_dev), F32),
+            pltpu.VMEM((GRID_H // CHUNK, 8, tr_dev), F32),
             pltpu.VMEM((frame_count, sub_rows, chan + LANES), BF16),
         ],
         compiler_params=limits,

time: 29.4 us -> 28.4 us (0.966)
  Pallas kernels: 12.8 us -> 11.7 us
    pallas_call x1, Pallas kernels: 7.16 us -> 6.54 us  [on_device(): pl.pallas_call(functools.partial(heat_kernel, frame_count, len(queries)),...]
    pallas_call x1, Pallas kernels: 2.69 us -> 2.22 us  [on_device(): pl.pallas_call(functools.partial(pick_kernel, frame_count, track_count),...]
where the time goes in v5:
time: 28.4 us; the launch traced here: 28.2 us
  Pallas kernels  11.7 us (41%)
  starting transfers between devices  11.4 us (40%)
  waiting for transfers between devices  5.02 us (18%)
    pallas_call x1, Pallas kernels, on_device(): pl.pallas_call(functools.partial(heat_kernel, frame_count, len(queries)),...  6.54 us
    ppermute x3, starting transfers between devices, swap(): return lax.ppermute(x, 'frame', [(i, i ^ m) for i in range(frame_count)])  5.72 us
    ppermute x3, starting transfers between devices, send(): return lax.ppermute(x, 'frame', pairs)  5.65 us
    ppermute x3, waiting for transfers between devices, swap(): return lax.ppermute(x, 'frame', [(i, i ^ m) for i in range(frame_count)])  3.24 us
    pallas_call x1, Pallas kernels, on_device(): pl.pallas_call(functools.partial(pick_kernel, frame_count, track_count),...  2.22 us
    ppermute x3, waiting for transfers between devices, send(): return lax.ppermute(x, 'frame', pairs)  1.77 us
    pallas_call x1, Pallas kernels, on_device(): pl.pallas_call(functools.partial(mix_kernel, frame_count), name='mix', ou...  1.49 us
    pallas_call x1, Pallas kernels, on_device(): pl.pallas_call(prep_kernel, name='prep', out_shape=(pltpu.VMEM((2, hid *...  1.48 us
  transfers between devices with their start and end apart: 6, of which 6 were waited for; matrix products, arithmetic and copies ran while one was open for 0% of the time, Pallas kernels for 5%

profile of v5, /device:TPU:0, one launch (start us, length us, event | category | flops | bytes accessed | tf_op | source)
XLA Modules:
  0.0 28.2 jit_solution(9662091661179729516)
XLA Ops:
  0.0 0.0 copy-start.6
  0.0 0.0 copy-start.5
  0.0 0.0 copy-start.3
  0.0 0.0 copy-start
  0.0 0.0 copy-start.1
  0.0 0.0 copy-start.2
  0.0 0.0 copy-start.4
  0.0 2.2 %pick.1 = (bf16[128,256]{1,0:T(8,128)(2,1)S(1)}, bf16[4096,256]{1,0:T(8,128)(2,1)S(1)}) custom-call(s32[1,512]{1,0:T(1,128)} %bitcast.11, s32[1,512]{1,0:T(1,128)} %bitcast.12, s32[1,512]{1,0:T(1,128)} %bitcast.13, s32[1,512]{1,0:T(1,128)} %bitcast.14, bf16[4096,256]{1,0:T(8,128)(2,1)} %bitcast.10), custom_call_target="tpu_custom_call" | custom-call | tf_op jit(solution)/shard_map/pick/pallas_call | solution.py:360
  2.3 4.1 %collective-permute-start.2 = (bf16[128,256]{1,0:T(8,128)(2,1)S(1)}, bf16[128,256]{1,0:T(8,128)(2,1)S(1)}, u32[]{:S(2)}, u32[]{:S(2)}) collective-permute-start(bf16[128,256]{1,0:T(8,128)(2,1)S(1)} %get-tuple-element.13.refs_0_), channel_id=1, source_target_pairs={{0,8},{4,12},{8,0},{12,4},{1,9},{5,13},{9,1},{13,5},{2,10},{6,14},... | collective-permute-start | bytes 196616 | tf_op jit(solution)/shard_map/ppermute | solution.py:356
  6.4 1.3 %collective-permute-start.1 = (bf16[128,256]{1,0:T(8,128)(2,1)S(1)}, bf16[128,256]{1,0:T(8,128)(2,1)S(1)}, u32[]{:S(2)}, u32[]{:S(2)}) collective-permute-start(bf16[128,256]{1,0:T(8,128)(2,1)S(1)} %get-tuple-element.13.refs_0_), channel_id=1, source_target_pairs={{0,12},{4,8},{8,4},{12,0},{1,13},{5,9},{9,5},{13,1},{2,14},{6,10},... | collective-permute-start | bytes 196616 | tf_op jit(solution)/shard_map/ppermute | solution.py:356
  7.8 0.2 collective-permute-start
  8.0 0.0 copy-done.6
  8.0 0.0 copy-done.5
  8.0 0.0 copy-done.3
  8.0 1.5 %prep.1 = (bf16[2,512,256]{2,1,0:T(8,128)(2,1)S(1)}, f32[33,8,128]{2,1,0:T(8,128)S(1)}) custom-call(f32[16,9]{1,0:T(8,128)S(1)} %copy-done.3, f32[16]{0:T(128)S(1)} %copy-done.5, f32[16]{0:T(128)S(1)} %copy-done.6), custom_call_target="tpu_custom_call" | custom-call | tf_op jit(solution)/shard_map/prep/pallas_call | solution.py:386
  9.5 0.6 %collective-permute-done.2.refs_3_ = bf16[128,256]{1,0:T(8,128)(2,1)S(1)} collective-permute-done((bf16[128,256]{1,0:T(8,128)(2,1)S(1)}, bf16[128,256]{1,0:T(8,128)(2,1)S(1)}, u32[]{:S(2)}, u32[]{:S(2)}) %collective-permute-start.2) | collective-permute-done | bytes 65568 | tf_op jit(solution)/shard_map/ppermute | solution.py:356
  10.1 2.5 %collective-permute-done.1.refs_2_ = bf16[128,256]{1,0:T(8,128)(2,1)S(1)} collective-permute-done((bf16[128,256]{1,0:T(8,128)(2,1)S(1)}, bf16[128,256]{1,0:T(8,128)(2,1)S(1)}, u32[]{:S(2)}, u32[]{:S(2)}) %collective-permute-start.1) | collective-permute-done | bytes 65568 | tf_op jit(solution)/shard_map/ppermute | solution.py:356
  12.6 0.1 collective-permute-done.refs_1_
  12.7 6.5 %heat.1 = (bf16[32,384]{1,0:T(8,128)(2,1)S(1)}, bf16[32,384]{1,0:T(8,128)(2,1)S(1)}, bf16[32,384]{1,0:T(8,128)(2,1)S(1)}, bf16[32,384]{1,0:T(8,128)(2,1)S(1)}) custom-call(bf16[128,256]{1,0:T(8,128)(2,1)S(1)} %get-tuple-element.13.refs_0_, bf16[128,256]{1,0:T(8,128)(2,1)S(1)} %collective-permute-done.refs_1_, ...), custom_call_target="tpu_custom_call" | custom-call | tf_op jit(solution)/shard_map/heat/pallas_call | solution.py:399
  19.3 0.8 %collective-permute-start.3 = (bf16[32,384]{1,0:T(8,128)(2,1)S(1)}, bf16[32,384]{1,0:T(8,128)(2,1)S(1)}, u32[]{:S(2)}, u32[]{:S(2)}) collective-permute-start(bf16[32,384]{1,0:T(8,128)(2,1)S(1)} %get-tuple-element.18), channel_id=1, source_target_pairs={{0,4},{4,8},{8,12},{12,0},{1,5},{5,9},{9,13},{13,1},{2,6},{6,10},{... | collective-permute-start | bytes 73736 | tf_op jit(solution)/shard_map/ppermute | solution.py:353
  20.1 2.8 %collective-permute-start.4 = (bf16[32,384]{1,0:T(8,128)(2,1)S(1)}, bf16[32,384]{1,0:T(8,128)(2,1)S(1)}, u32[]{:S(2)}, u32[]{:S(2)}) collective-permute-start(bf16[32,384]{1,0:T(8,128)(2,1)S(1)} %get-tuple-element.19), channel_id=1, source_target_pairs={{0,8},{4,12},{8,0},{12,4},{1,9},{5,13},{9,1},{13,5},{2,10},{6,14},... | collective-permute-start | bytes 73736 | tf_op jit(solution)/shard_map/ppermute | solution.py:353
  22.9 2.1 %collective-permute-start.5 = (bf16[32,384]{1,0:T(8,128)(2,1)S(1)}, bf16[32,384]{1,0:T(8,128)(2,1)S(1)}, u32[]{:S(2)}, u32[]{:S(2)}) collective-permute-start(bf16[32,384]{1,0:T(8,128)(2,1)S(1)} %get-tuple-element.20), channel_id=1, source_target_pairs={{0,12},{4,0},{8,4},{12,8},{1,13},{5,1},{9,5},{13,9},{2,14},{6,2},{... | collective-permute-start | bytes 73736 | tf_op jit(solution)/shard_map/ppermute | solution.py:353
  24.9 0.1 collective-permute-done.3.refs_1_
  25.1 0.3 collective-permute-done.4.refs_2_
  25.3 1.4 %collective-permute-done.5.refs_3_ = bf16[32,384]{1,0:T(8,128)(2,1)S(1)} collective-permute-done((bf16[32,384]{1,0:T(8,128)(2,1)S(1)}, bf16[32,384]{1,0:T(8,128)(2,1)S(1)}, u32[]{:S(2)}, u32[]{:S(2)}) %collective-permute-start.5) | collective-permute-done | bytes 24608 | tf_op jit(solution)/shard_map/ppermute | solution.py:353
  26.7 0.0 copy-done
  26.7 0.0 copy-done.1
  26.7 0.0 copy-done.2
  26.7 0.0 copy-done.4
  26.7 1.5 %mix.1 = f32[3,4,32]{2,1,0:T(4,128)} custom-call(bf16[32,384]{1,0:T(8,128)(2,1)S(1)} %get-tuple-element.17.refs_0_, bf16[32,384]{1,0:T(8,128)(2,1)S(1)} %collective-permute-done.3.refs_1_, bf16[32,384]{1,0:T(8,128)(2,1)S(1)} %collective-permute-done.4.refs_2_, bf16[32,384]{1,0:T(8,128)(2,1)S(1)} %collective-permute-done.5.refs_3_, ...), custom_call_target="tpu_custom_call" | custom-call | tf_op jit(solution)/shard_map/mix/pallas_call | solution.py:425
Async XLA Ops:
  0.0 8.0 %copy-start.6 = (f32[16]{0:T(128)S(1)}, f32[16]{0:T(128)}, u32[]{:S(2)}) copy-start(f32[16]{0:T(128)} %head_ref.1) | copy-start | bytes 196
  0.0 8.0 %copy-start.5 = (f32[16]{0:T(128)S(1)}, f32[16]{0:T(128)}, u32[]{:S(2)}) copy-start(f32[16]{0:T(128)} %bias_ref.1) | copy-start | bytes 196
  0.0 8.0 %copy-start.3 = (f32[16,9]{1,0:T(8,128)S(1)}, f32[16,9]{1,0:T(8,128)}, u32[]{:S(2)}) copy-start(f32[16,9]{1,0:T(8,128)} %weight_ref.1) | copy-start | bytes 1732
  0.0 26.7 %copy-start = (bf16[256,1024]{1,0:T(8,128)(2,1)S(1)}, bf16[256,1024]{1,0:T(8,128)(2,1)}, u32[]{:S(2)}) copy-start(bf16[256,1024]{1,0:T(8,128)(2,1)} %refs_4_.1) | copy-start | bytes 1572868
  0.0 26.7 %copy-start.1 = (f32[3,1024]{1,0:T(4,128)S(1)}, f32[3,1024]{1,0:T(4,128)}, u32[]{:S(2)}) copy-start(f32[3,1024]{1,0:T(4,128)} %refs_5_.1) | copy-start | bytes 36868
  0.0 26.7 %copy-start.2 = (bf16[1024,3]{0,1:T(4,128)(2,1)S(1)}, bf16[1024,3]{0,1:T(4,128)(2,1)}, u32[]{:S(2)}) copy-start(bf16[1024,3]{0,1:T(4,128)(2,1)} %param.23) | copy-start | bytes 18436
  0.0 26.7 %copy-start.4 = (f32[1024]{0:T(1024)S(1)}, f32[1024]{0:T(1024)}, u32[]{:S(2)}) copy-start(f32[1024]{0:T(1024)} %param.22) | copy-start | bytes 12292
  2.3 7.9 %collective-permute-start.2 = (bf16[128,256]{1,0:T(8,128)(2,1)S(1)}, bf16[128,256]{1,0:T(8,128)(2,1)S(1)}, u32[]{:S(2)}, u32[]{:S(2)}) collective-permute-start(bf16[128,256]{1,0:T(8,128)(2,1)S(1)} %get-tuple-element.13.refs_0_), channel_id=1, source_target_pairs={{0,8},{4,12},{8,0},{12,4},{1,9},{5,13},{9,1},{13,5},{2,10},{6,14},... | collective-permute-start | bytes 196616 | tf_op jit(solution)/shard_map/ppermute | solution.py:356
  6.4 6.2 %collective-permute-start.1 = (bf16[128,256]{1,0:T(8,128)(2,1)S(1)}, bf16[128,256]{1,0:T(8,128)(2,1)S(1)}, u32[]{:S(2)}, u32[]{:S(2)}) collective-permute-start(bf16[128,256]{1,0:T(8,128)(2,1)S(1)} %get-tuple-element.13.refs_0_), channel_id=1, source_target_pairs={{0,12},{4,8},{8,4},{12,0},{1,13},{5,9},{9,5},{13,1},{2,14},{6,10},... | collective-permute-start | bytes 196616 | tf_op jit(solution)/shard_map/ppermute | solution.py:356
  7.8 5.0 %collective-permute-start = (bf16[128,256]{1,0:T(8,128)(2,1)S(1)}, bf16[128,256]{1,0:T(8,128)(2,1)S(1)}, u32[]{:S(2)}, u32[]{:S(2)}) collective-permute-start(bf16[128,256]{1,0:T(8,128)(2,1)S(1)} %get-tuple-element.13.refs_0_), channel_id=1, source_target_pairs={{0,4},{4,0},{8,12},{12,8},{1,5},{5,1},{9,13},{13,9},{2,6},{6,2},{1... | collective-permute-start | bytes 196616 | tf_op jit(solution)/shard_map/ppermute | solution.py:356
  19.3 5.8 %collective-permute-start.3 = (bf16[32,384]{1,0:T(8,128)(2,1)S(1)}, bf16[32,384]{1,0:T(8,128)(2,1)S(1)}, u32[]{:S(2)}, u32[]{:S(2)}) collective-permute-start(bf16[32,384]{1,0:T(8,128)(2,1)S(1)} %get-tuple-element.18), channel_id=1, source_target_pairs={{0,4},{4,8},{8,12},{12,0},{1,5},{5,9},{9,13},{13,1},{2,6},{6,10},{... | collective-permute-start | bytes 73736 | tf_op jit(solution)/shard_map/ppermute | solution.py:353
  20.1 5.3 %collective-permute-start.4 = (bf16[32,384]{1,0:T(8,128)(2,1)S(1)}, bf16[32,384]{1,0:T(8,128)(2,1)S(1)}, u32[]{:S(2)}, u32[]{:S(2)}) collective-permute-start(bf16[32,384]{1,0:T(8,128)(2,1)S(1)} %get-tuple-element.19), channel_id=1, source_target_pairs={{0,8},{4,12},{8,0},{12,4},{1,9},{5,13},{9,1},{13,5},{2,10},{6,14},... | collective-permute-start | bytes 73736 | tf_op jit(solution)/shard_map/ppermute | solution.py:353
  22.9 3.8 %collective-permute-start.5 = (bf16[32,384]{1,0:T(8,128)(2,1)S(1)}, bf16[32,384]{1,0:T(8,128)(2,1)S(1)}, u32[]{:S(2)}, u32[]{:S(2)}) collective-permute-start(bf16[32,384]{1,0:T(8,128)(2,1)S(1)} %get-tuple-element.20), channel_id=1, source_target_pairs={{0,12},{4,0},{8,4},{12,8},{1,13},{5,1},{9,5},{13,9},{2,14},{6,2},{... | collective-permute-start | bytes 73736 | tf_op jit(solution)/shard_map/ppermute | solution.py:353

commit v6 on v5

--- a/solution.py
+++ b/solution.py
@@ -14,7 +14,7 @@
 KDIM = 256
 ROWS_PAD = GRID_H + 4
 LANES = 128
-CHUNK = 8
+CHUNK = 4
 LOG2E = math.log2(math.e)
 
 VMEM_SPEC = pl.BlockSpec(memory_space=pltpu.VMEM)
@@ -189,7 +189,7 @@
             for pair in range(cols // 2):
                 sides = []
                 for k in (2 * pair, 2 * pair + 1):
-                    at = [pl.multiple_of(top + rr * GRID_W + k * TILE, TILE) for rr in range(4)]
+                    at = [top + rr * GRID_W + k * TILE for rr in range(4)]
                     mid_high = [high_ref[pl.ds(a, TILE), :] for a in at]
                     mid_low = [low_ref[pl.ds(a, TILE), :] for a in at]
                     eh, el = edge_high[k], edge_low[k]
@@ -197,7 +197,19 @@
                         jnp.concatenate(mid_high + mid_low + mid_high + [eh, el, eh, eh], axis=0)
                     )
                 window = jnp.concatenate(sides, axis=1)
-                act = jnp.dot(weight_ref[parity], window, preferred_element_type=F32)
+                cuts = 2 if j == GRID_H // 4 - 1 and parity == 1 and pair >= 0 else 1
+                length = hid * part // cuts
+                act = jnp.concatenate(
+                    [
+                        jnp.dot(
+                            weight_ref[parity, n * length : (n + 1) * length],
+                            window,
+                            preferred_element_type=F32,
+                        )
+                        for n in range(cuts)
+                    ],
+                    axis=0,
+                )
                 for side in range(2):
                     k = 2 * pair + side
                     lanes = slice(side * slots, (side + 1) * slots)
@@ -209,7 +221,7 @@
                                 act[at : at + 8, lanes], coef_ref[h]
                             )
                         to = top + (8 * q // TILE) * GRID_W + k * TILE + 8 * q % TILE
-                        logit_ref[pl.ds(pl.multiple_of(to, 8), 8), :] = acc
+                        logit_ref[pl.ds(to, 8), :] = acc
                         best = jnp.maximum(best, acc)
         return best
 
@@ -226,24 +238,21 @@
             r = c * CHUNK + m
             values = []
             for n in range(GRID_W // 8):
-                at = pl.multiple_of(r * GRID_W + 8 * n, 8)
+                at = r * GRID_W + 8 * n
                 value = jnp.exp2(logit_ref[pl.ds(at, 8), :] - peak)
                 logit_ref[pl.ds(at, 8), :] = value
                 col_acc[n] = col_acc[n] + value
                 values.append(value)
             while len(values) > 1:
                 values = [x + y for x, y in zip(values[::2], values[1::2])]
-            row_acc = row_acc + values[0] * (jnp.float32(r) * (1.0 / (GRID_H - 1)))
+            row_acc = row_acc + values[0] * (r * (1.0 / (GRID_H - 1)))
         return peak, row_acc, col_acc
 
     zero = jnp.zeros((8, slots), F32)
-    best, row_acc, col_acc = lax.fori_loop(
-        0,
-        GRID_H // CHUNK,
-        chunk_step,
-        (jnp.full((8, slots), -jnp.inf, F32), zero, [zero] * (GRID_W // 8)),
-        unroll=8,
-    )
+    carry = (jnp.full((8, slots), -jnp.inf, F32), zero, [zero] * (GRID_W // 8))
+    for c in range(GRID_H // CHUNK):
+        carry = chunk_step(c, carry)
+    best, row_acc, col_acc = carry
     top_value = jnp.max(best, axis=0, keepdims=True)
     shrink = jnp.exp2(best - top_value)
     total, col_sum = zero, zero
@@ -257,16 +266,25 @@
 
     span = CHUNK * GRID_W
 
-    def sample_step(c, acc):
-        at = pl.multiple_of(c * span, span)
-        factor = jnp.exp2(peak_ref[c] - top_value) * inverse
-        heat = logit_ref[pl.ds(at, span), :].reshape(span // 8, 8, slots) * factor
-        heat = heat.reshape(span, slots).astype(BF16)
-        return acc + jnp.dot(heat.T, maps_ref[pl.ds(at, span), :], preferred_element_type=F32)
-
-    sampled = lax.fori_loop(
-        0, GRID_H // CHUNK, sample_step, jnp.zeros((slots, chan), F32), unroll=8
-    )
+    each = GRID_H // CHUNK
+
+    def sample_step(n, sums):
+        sums = list(sums)
+        for m in range(each):
+            c = n * each + m
+            at = pl.multiple_of(c * span, span)
+            factor = jnp.exp2(peak_ref[c] - top_value) * inverse
+            heat = logit_ref[pl.ds(at, span), :].reshape(span // 8, 8, slots) * factor
+            heat = heat.reshape(span, slots).astype(BF16)
+            sums[m % 2] = sums[m % 2] + jnp.dot(
+                heat.T, maps_ref[pl.ds(at, span), :], preferred_element_type=F32
+            )
+        return tuple(sums)
+
+    sums = lax.fori_loop(
+        0, lax.min(here, 0) + 1, sample_step, (jnp.zeros((slots, chan), F32),) * 2
+    )
+    sampled = sums[0] + sums[1]
     rest = jnp.concatenate([row_est, col_est, jnp.zeros((LANES - 2, slots), F32)], axis=0)
     sub = slots // pieces
     full_ref[:, :, :chan] = sampled.astype(BF16).reshape(pieces, sub, chan)

time: 28.4 us -> 28 us (0.986)
  Pallas kernels: 11.7 us -> 11.4 us
    pallas_call x1, Pallas kernels: 6.54 us -> 6.23 us  [on_device(): pl.pallas_call(functools.partial(heat_kernel, frame_count, len(queries)),...]
where the time goes in v6:
time: 28 us; the launch traced here: 27.9 us
  Pallas kernels  11.4 us (41%)
  starting transfers between devices  11.4 us (41%)
  waiting for transfers between devices  5.02 us (18%)
    pallas_call x1, Pallas kernels, on_device(): pl.pallas_call(functools.partial(heat_kernel, frame_count, len(queries)),...  6.23 us
    ppermute x3, starting transfers between devices, swap(): return lax.ppermute(x, 'frame', [(i, i ^ m) for i in range(frame_count)])  5.72 us
    ppermute x3, starting transfers between devices, send(): return lax.ppermute(x, 'frame', pairs)  5.65 us
    ppermute x3, waiting for transfers between devices, swap(): return lax.ppermute(x, 'frame', [(i, i ^ m) for i in range(frame_count)])  3.24 us
    pallas_call x1, Pallas kernels, on_device(): pl.pallas_call(functools.partial(pick_kernel, frame_count, track_count),...  2.22 us
    ppermute x3, waiting for transfers between devices, send(): return lax.ppermute(x, 'frame', pairs)  1.77 us
    pallas_call x1, Pallas kernels, on_device(): pl.pallas_call(functools.partial(mix_kernel, frame_count), name='mix', ou...  1.49 us
    pallas_call x1, Pallas kernels, on_device(): pl.pallas_call(prep_kernel, name='prep', out_shape=(pltpu.VMEM((2, hid *...  1.48 us
  transfers between devices with their start and end apart: 6, of which 6 were waited for; matrix products, arithmetic and copies ran while one was open for 0% of the time, Pallas kernels for 5%

profile of v6, /device:TPU:0, one launch (start us, length us, event | category | flops | bytes accessed | tf_op | source)
XLA Modules:
  0.0 27.9 jit_solution(12027102396111132061)
XLA Ops:
  0.0 0.0 copy-start.6
  0.0 0.0 copy-start.5
  0.0 0.0 copy-start.3
  0.0 0.0 copy-start
  0.0 0.0 copy-start.1
  0.0 0.0 copy-start.2
  0.0 0.0 copy-start.4
  0.0 2.2 %pick.1 = (bf16[128,256]{1,0:T(8,128)(2,1)S(1)}, bf16[4096,256]{1,0:T(8,128)(2,1)S(1)}) custom-call(s32[1,512]{1,0:T(1,128)} %bitcast.11, s32[1,512]{1,0:T(1,128)} %bitcast.12, s32[1,512]{1,0:T(1,128)} %bitcast.13, s32[1,512]{1,0:T(1,128)} %bitcast.14, bf16[4096,256]{1,0:T(8,128)(2,1)} %bitcast.10), custom_call_target="tpu_custom_call" | custom-call | tf_op jit(solution)/shard_map/pick/pallas_call | solution.py:378
  2.3 4.1 %collective-permute-start.2 = (bf16[128,256]{1,0:T(8,128)(2,1)S(1)}, bf16[128,256]{1,0:T(8,128)(2,1)S(1)}, u32[]{:S(2)}, u32[]{:S(2)}) collective-permute-start(bf16[128,256]{1,0:T(8,128)(2,1)S(1)} %get-tuple-element.13.refs_0_), channel_id=1, source_target_pairs={{0,8},{4,12},{8,0},{12,4},{1,9},{5,13},{9,1},{13,5},{2,10},{6,14},... | collective-permute-start | bytes 196616 | tf_op jit(solution)/shard_map/ppermute | solution.py:374
  6.4 1.3 %collective-permute-start.1 = (bf16[128,256]{1,0:T(8,128)(2,1)S(1)}, bf16[128,256]{1,0:T(8,128)(2,1)S(1)}, u32[]{:S(2)}, u32[]{:S(2)}) collective-permute-start(bf16[128,256]{1,0:T(8,128)(2,1)S(1)} %get-tuple-element.13.refs_0_), channel_id=1, source_target_pairs={{0,12},{4,8},{8,4},{12,0},{1,13},{5,9},{9,5},{13,1},{2,14},{6,10},... | collective-permute-start | bytes 196616 | tf_op jit(solution)/shard_map/ppermute | solution.py:374
  7.8 0.2 collective-permute-start
  8.0 0.0 copy-done.6
  8.0 0.0 copy-done.5
  8.0 0.0 copy-done.3
  8.0 1.5 %prep.1 = (bf16[2,512,256]{2,1,0:T(8,128)(2,1)S(1)}, f32[33,8,128]{2,1,0:T(8,128)S(1)}) custom-call(f32[16,9]{1,0:T(8,128)S(1)} %copy-done.3, f32[16]{0:T(128)S(1)} %copy-done.5, f32[16]{0:T(128)S(1)} %copy-done.6), custom_call_target="tpu_custom_call" | custom-call | tf_op jit(solution)/shard_map/prep/pallas_call | solution.py:404
  9.5 0.6 %collective-permute-done.2.refs_3_ = bf16[128,256]{1,0:T(8,128)(2,1)S(1)} collective-permute-done((bf16[128,256]{1,0:T(8,128)(2,1)S(1)}, bf16[128,256]{1,0:T(8,128)(2,1)S(1)}, u32[]{:S(2)}, u32[]{:S(2)}) %collective-permute-start.2) | collective-permute-done | bytes 65568 | tf_op jit(solution)/shard_map/ppermute | solution.py:374
  10.1 2.5 %collective-permute-done.1.refs_2_ = bf16[128,256]{1,0:T(8,128)(2,1)S(1)} collective-permute-done((bf16[128,256]{1,0:T(8,128)(2,1)S(1)}, bf16[128,256]{1,0:T(8,128)(2,1)S(1)}, u32[]{:S(2)}, u32[]{:S(2)}) %collective-permute-start.1) | collective-permute-done | bytes 65568 | tf_op jit(solution)/shard_map/ppermute | solution.py:374
  12.6 0.1 collective-permute-done.refs_1_
  12.7 6.2 %heat.1 = (bf16[32,384]{1,0:T(8,128)(2,1)S(1)}, bf16[32,384]{1,0:T(8,128)(2,1)S(1)}, bf16[32,384]{1,0:T(8,128)(2,1)S(1)}, bf16[32,384]{1,0:T(8,128)(2,1)S(1)}) custom-call(bf16[128,256]{1,0:T(8,128)(2,1)S(1)} %get-tuple-element.13.refs_0_, bf16[128,256]{1,0:T(8,128)(2,1)S(1)} %collective-permute-done.refs_1_, ...), custom_call_target="tpu_custom_call" | custom-call | tf_op jit(solution)/shard_map/heat/pallas_call | solution.py:417
  19.0 0.8 %collective-permute-start.3 = (bf16[32,384]{1,0:T(8,128)(2,1)S(1)}, bf16[32,384]{1,0:T(8,128)(2,1)S(1)}, u32[]{:S(2)}, u32[]{:S(2)}) collective-permute-start(bf16[32,384]{1,0:T(8,128)(2,1)S(1)} %get-tuple-element.18), channel_id=1, source_target_pairs={{0,4},{4,8},{8,12},{12,0},{1,5},{5,9},{9,13},{13,1},{2,6},{6,10},{... | collective-permute-start | bytes 73736 | tf_op jit(solution)/shard_map/ppermute | solution.py:371
  19.8 2.8 %collective-permute-start.4 = (bf16[32,384]{1,0:T(8,128)(2,1)S(1)}, bf16[32,384]{1,0:T(8,128)(2,1)S(1)}, u32[]{:S(2)}, u32[]{:S(2)}) collective-permute-start(bf16[32,384]{1,0:T(8,128)(2,1)S(1)} %get-tuple-element.19), channel_id=1, source_target_pairs={{0,8},{4,12},{8,0},{12,4},{1,9},{5,13},{9,1},{13,5},{2,10},{6,14},... | collective-permute-start | bytes 73736 | tf_op jit(solution)/shard_map/ppermute | solution.py:371
  22.6 2.1 %collective-permute-start.5 = (bf16[32,384]{1,0:T(8,128)(2,1)S(1)}, bf16[32,384]{1,0:T(8,128)(2,1)S(1)}, u32[]{:S(2)}, u32[]{:S(2)}) collective-permute-start(bf16[32,384]{1,0:T(8,128)(2,1)S(1)} %get-tuple-element.20), channel_id=1, source_target_pairs={{0,12},{4,0},{8,4},{12,8},{1,13},{5,1},{9,5},{13,9},{2,14},{6,2},{... | collective-permute-start | bytes 73736 | tf_op jit(solution)/shard_map/ppermute | solution.py:371
  24.6 0.1 collective-permute-done.3.refs_1_
  24.8 0.3 collective-permute-done.4.refs_2_
  25.0 1.4 %collective-permute-done.5.refs_3_ = bf16[32,384]{1,0:T(8,128)(2,1)S(1)} collective-permute-done((bf16[32,384]{1,0:T(8,128)(2,1)S(1)}, bf16[32,384]{1,0:T(8,128)(2,1)S(1)}, u32[]{:S(2)}, u32[]{:S(2)}) %collective-permute-start.5) | collective-permute-done | bytes 24608 | tf_op jit(solution)/shard_map/ppermute | solution.py:371
  26.4 0.0 copy-done
  26.4 0.0 copy-done.1
  26.4 0.0 copy-done.2
  26.4 0.0 copy-done.4
  26.4 1.5 %mix.1 = f32[3,4,32]{2,1,0:T(4,128)} custom-call(bf16[32,384]{1,0:T(8,128)(2,1)S(1)} %get-tuple-element.17.refs_0_, bf16[32,384]{1,0:T(8,128)(2,1)S(1)} %collective-permute-done.3.refs_1_, bf16[32,384]{1,0:T(8,128)(2,1)S(1)} %collective-permute-done.4.refs_2_, bf16[32,384]{1,0:T(8,128)(2,1)S(1)} %collective-permute-done.5.refs_3_, ...), custom_call_target="tpu_custom_call" | custom-call | tf_op jit(solution)/shard_map/mix/pallas_call | solution.py:443
Async XLA Ops:
  0.0 8.0 %copy-start.6 = (f32[16]{0:T(128)S(1)}, f32[16]{0:T(128)}, u32[]{:S(2)}) copy-start(f32[16]{0:T(128)} %head_ref.1) | copy-start | bytes 196
  0.0 8.0 %copy-start.5 = (f32[16]{0:T(128)S(1)}, f32[16]{0:T(128)}, u32[]{:S(2)}) copy-start(f32[16]{0:T(128)} %bias_ref.1) | copy-start | bytes 196
  0.0 8.0 %copy-start.3 = (f32[16,9]{1,0:T(8,128)S(1)}, f32[16,9]{1,0:T(8,128)}, u32[]{:S(2)}) copy-start(f32[16,9]{1,0:T(8,128)} %weight_ref.1) | copy-start | bytes 1732
  0.0 26.4 %copy-start = (bf16[256,1024]{1,0:T(8,128)(2,1)S(1)}, bf16[256,1024]{1,0:T(8,128)(2,1)}, u32[]{:S(2)}) copy-start(bf16[256,1024]{1,0:T(8,128)(2,1)} %refs_4_.1) | copy-start | bytes 1572868
  0.0 26.4 %copy-start.1 = (f32[3,1024]{1,0:T(4,128)S(1)}, f32[3,1024]{1,0:T(4,128)}, u32[]{:S(2)}) copy-start(f32[3,1024]{1,0:T(4,128)} %refs_5_.1) | copy-start | bytes 36868
  0.0 26.4 %copy-start.2 = (bf16[1024,3]{0,1:T(4,128)(2,1)S(1)}, bf16[1024,3]{0,1:T(4,128)(2,1)}, u32[]{:S(2)}) copy-start(bf16[1024,3]{0,1:T(4,128)(2,1)} %param.23) | copy-start | bytes 18436
  0.0 26.4 %copy-start.4 = (f32[1024]{0:T(1024)S(1)}, f32[1024]{0:T(1024)}, u32[]{:S(2)}) copy-start(f32[1024]{0:T(1024)} %param.22) | copy-start | bytes 12292
  2.3 7.9 %collective-permute-start.2 = (bf16[128,256]{1,0:T(8,128)(2,1)S(1)}, bf16[128,256]{1,0:T(8,128)(2,1)S(1)}, u32[]{:S(2)}, u32[]{:S(2)}) collective-permute-start(bf16[128,256]{1,0:T(8,128)(2,1)S(1)} %get-tuple-element.13.refs_0_), channel_id=1, source_target_pairs={{0,8},{4,12},{8,0},{12,4},{1,9},{5,13},{9,1},{13,5},{2,10},{6,14},... | collective-permute-start | bytes 196616 | tf_op jit(solution)/shard_map/ppermute | solution.py:374
  6.4 6.2 %collective-permute-start.1 = (bf16[128,256]{1,0:T(8,128)(2,1)S(1)}, bf16[128,256]{1,0:T(8,128)(2,1)S(1)}, u32[]{:S(2)}, u32[]{:S(2)}) collective-permute-start(bf16[128,256]{1,0:T(8,128)(2,1)S(1)} %get-tuple-element.13.refs_0_), channel_id=1, source_target_pairs={{0,12},{4,8},{8,4},{12,0},{1,13},{5,9},{9,5},{13,1},{2,14},{6,10},... | collective-permute-start | bytes 196616 | tf_op jit(solution)/shard_map/ppermute | solution.py:374
  7.8 5.0 %collective-permute-start = (bf16[128,256]{1,0:T(8,128)(2,1)S(1)}, bf16[128,256]{1,0:T(8,128)(2,1)S(1)}, u32[]{:S(2)}, u32[]{:S(2)}) collective-permute-start(bf16[128,256]{1,0:T(8,128)(2,1)S(1)} %get-tuple-element.13.refs_0_), channel_id=1, source_target_pairs={{0,4},{4,0},{8,12},{12,8},{1,5},{5,1},{9,13},{13,9},{2,6},{6,2},{1... | collective-permute-start | bytes 196616 | tf_op jit(solution)/shard_map/ppermute | solution.py:374
  19.0 5.8 %collective-permute-start.3 = (bf16[32,384]{1,0:T(8,128)(2,1)S(1)}, bf16[32,384]{1,0:T(8,128)(2,1)S(1)}, u32[]{:S(2)}, u32[]{:S(2)}) collective-permute-start(bf16[32,384]{1,0:T(8,128)(2,1)S(1)} %get-tuple-element.18), channel_id=1, source_target_pairs={{0,4},{4,8},{8,12},{12,0},{1,5},{5,9},{9,13},{13,1},{2,6},{6,10},{... | collective-permute-start | bytes 73736 | tf_op jit(solution)/shard_map/ppermute | solution.py:371
  19.8 5.3 %collective-permute-start.4 = (bf16[32,384]{1,0:T(8,128)(2,1)S(1)}, bf16[32,384]{1,0:T(8,128)(2,1)S(1)}, u32[]{:S(2)}, u32[]{:S(2)}) collective-permute-start(bf16[32,384]{1,0:T(8,128)(2,1)S(1)} %get-tuple-element.19), channel_id=1, source_target_pairs={{0,8},{4,12},{8,0},{12,4},{1,9},{5,13},{9,1},{13,5},{2,10},{6,14},... | collective-permute-start | bytes 73736 | tf_op jit(solution)/shard_map/ppermute | solution.py:371
  22.6 3.8 %collective-permute-start.5 = (bf16[32,384]{1,0:T(8,128)(2,1)S(1)}, bf16[32,384]{1,0:T(8,128)(2,1)S(1)}, u32[]{:S(2)}, u32[]{:S(2)}) collective-permute-start(bf16[32,384]{1,0:T(8,128)(2,1)S(1)} %get-tuple-element.20), channel_id=1, source_target_pairs={{0,12},{4,0},{8,4},{12,8},{1,13},{5,1},{9,5},{13,9},{2,14},{6,2},{... | collective-permute-start | bytes 73736 | tf_op jit(solution)/shard_map/ppermute | solution.py:371

commit v7 on v6

--- a/solution.py
+++ b/solution.py
@@ -78,15 +78,18 @@
     flat = found[1:2] * GRID_W + found[2:3]
     flat = jnp.where(found[0:1] == frame_here.astype(F32), flat, -1.0)
     column = jnp.broadcast_to(flat, (slots, slots)).T[:, 0:1].astype(jnp.int32)
-    spread = jnp.broadcast_to(column, (slots, step))
-    lane = iota((slots, step), 1)
+    half = step // 2
+    spread = jnp.broadcast_to(column, (slots, half))
+    lane = iota((slots, half), 1)
     sums = [jnp.zeros((slots, chan), F32)] * 2
     for n in range(chunks):
-        sel = jnp.where(spread == lane + n * step, 1.0, 0.0).astype(BF16)
         copies[n].wait()
-        sums[n % 2] = sums[n % 2] + jnp.dot(
-            sel, held_ref[n * step : (n + 1) * step, :], preferred_element_type=F32
-        )
+        for m in range(2):
+            at = n * step + m * half
+            sel = jnp.where(spread == lane + at, 1.0, 0.0).astype(BF16)
+            sums[m] = sums[m] + jnp.dot(
+                sel, held_ref[at : at + half, :], preferred_element_type=F32
+            )
     out_ref[...] = (sums[0] + sums[1]).astype(BF16)
 
 
@@ -141,10 +144,10 @@
     hid = coef_ref.shape[0] // 2
     part = 2 * TILE
     here = lax.axis_index("frame").astype(jnp.int32)
-    query = q_refs[0][...].astype(F32)
+    query = q_refs[0][...]
     for ref in q_refs[1:]:
-        query = query + ref[...].astype(F32)
-    turned_q = query.T.astype(BF16)
+        query = query + ref[...]
+    turned_q = query.T
     scale = 1.0 / math.sqrt(chan)
 
     for lo, hi in ((0, GRID_W), (GRID_W + pixels, ROWS_PAD * GRID_W)):
@@ -295,17 +298,18 @@
 
 def mix_kernel(frames, *refs):
     got_refs = refs[:frames]
-    mix_in_ref, taps_ref, gain_ref, mix_out_ref, out_ref, z_ref, place_ref = refs[frames:]
+    mix_in_ref, taps_ref, gain_ref, mix_out_ref, out_ref, z_ref, join_ref = refs[frames:]
     chan = mix_in_ref.shape[0]
     rows = got_refs[0].shape[0]
     here = lax.axis_index("frame").astype(jnp.int32)
-    joined = jnp.concatenate([ref[...] for ref in got_refs], axis=0)
-    z = jnp.dot(joined[:, :chan], mix_in_ref[...], preferred_element_type=F32)
     for m in range(frames):
-        source = ahead(here, -m, frames)
-        z_ref[source] = z[m * rows : (m + 1) * rows]
-        place_ref[source] = got_refs[m][:, chan:]
-    place = place_ref[...].astype(F32).reshape(frames * rows, LANES).T[:8]
+        join_ref[ahead(here, -m, frames)] = got_refs[m][...]
+    joined = join_ref[...].reshape(frames * rows, join_ref.shape[2])
+    place = joined[:, chan:].astype(F32).T[:8]
+    z_ref[...] = jnp.dot(
+        joined[:, :chan], mix_in_ref[...], preferred_element_type=F32
+    ).reshape(z_ref.shape)
+    rate = math.sqrt(2.0 / math.pi)
     hidden = []
     for t in range(frames):
         mixed = taps_ref[1:2, :] * z_ref[t]
@@ -315,7 +319,9 @@
             mixed = mixed + taps_ref[2:3, :] * z_ref[t + 1]
         power = jnp.mean(mixed * mixed, axis=-1, keepdims=True)
         normed = mixed * lax.rsqrt(power + 1e-06) * gain_ref[...]
-        hidden.append(jax.nn.gelu(normed).astype(BF16))
+        curve = jnp.tanh(normed * (normed * normed * (0.044715 * rate) + rate))
+        half = 0.5 * normed
+        hidden.append((half * curve + half).astype(BF16))
     delta = lax.dot_general(
         mix_out_ref[...],
         jnp.concatenate(hidden, axis=0),
@@ -448,7 +454,7 @@
         out_specs=VMEM_SPEC,
         scratch_shapes=[
             pltpu.VMEM((frame_count, sub_rows, mixw), F32),
-            pltpu.VMEM((frame_count, sub_rows, LANES), BF16),
+            pltpu.VMEM((frame_count, sub_rows, chan + LANES), BF16),
         ],
         compiler_params=limits,
     )(

time: 28 us -> 27.7 us (0.989)
  Pallas kernels: 11.4 us -> 11.1 us
where the time goes in v7:
time: 27.7 us; the launch traced here: 27.6 us
  starting transfers between devices  11.4 us (41%)
  Pallas kernels  11.1 us (40%)
  waiting for transfers between devices  5.03 us (18%)
    pallas_call x1, Pallas kernels, on_device(): pl.pallas_call(functools.partial(heat_kernel, frame_count, len(queries)),...  6.13 us
    ppermute x3, starting transfers between devices, swap(): return lax.ppermute(x, 'frame', [(i, i ^ m) for i in range(frame_count)])  5.72 us
    ppermute x3, starting transfers between devices, send(): return lax.ppermute(x, 'frame', pairs)  5.64 us
    ppermute x3, waiting for transfers between devices, swap(): return lax.ppermute(x, 'frame', [(i, i ^ m) for i in range(frame_count)])  3.24 us
    pallas_call x1, Pallas kernels, on_device(): pl.pallas_call(functools.partial(pick_kernel, frame_count, track_count),...  2.16 us
    ppermute x3, waiting for transfers between devices, send(): return lax.ppermute(x, 'frame', pairs)  1.79 us
    pallas_call x1, Pallas kernels, on_device(): pl.pallas_call(prep_kernel, name='prep', out_shape=(pltpu.VMEM((2, hid *...  1.48 us
    pallas_call x1, Pallas kernels, on_device(): pl.pallas_call(functools.partial(mix_kernel, frame_count), name='mix', ou...  1.34 us
  transfers between devices with their start and end apart: 6, of which 6 were waited for; matrix products, arithmetic and copies ran while one was open for 0% of the time, Pallas kernels for 5%

profile of v7, /device:TPU:0, one launch (start us, length us, event | category | flops | bytes accessed | tf_op | source)
XLA Modules:
  0.0 27.6 jit_solution(686598849424007427)
XLA Ops:
  0.0 0.0 copy-start.6
  0.0 0.0 copy-start.5
  0.0 0.0 copy-start.3
  0.0 0.0 copy-start
  0.0 0.0 copy-start.1
  0.0 0.0 copy-start.2
  0.0 0.0 copy-start.4
  0.0 2.2 %pick.1 = (bf16[128,256]{1,0:T(8,128)(2,1)S(1)}, bf16[4096,256]{1,0:T(8,128)(2,1)S(1)}) custom-call(s32[1,512]{1,0:T(1,128)} %bitcast.11, s32[1,512]{1,0:T(1,128)} %bitcast.12, s32[1,512]{1,0:T(1,128)} %bitcast.13, s32[1,512]{1,0:T(1,128)} %bitcast.14, bf16[4096,256]{1,0:T(8,128)(2,1)} %bitcast.10), custom_call_target="tpu_custom_call" | custom-call | tf_op jit(solution)/shard_map/pick/pallas_call | solution.py:384
  2.2 4.1 %collective-permute-start.2 = (bf16[128,256]{1,0:T(8,128)(2,1)S(1)}, bf16[128,256]{1,0:T(8,128)(2,1)S(1)}, u32[]{:S(2)}, u32[]{:S(2)}) collective-permute-start(bf16[128,256]{1,0:T(8,128)(2,1)S(1)} %get-tuple-element.13.refs_0_), channel_id=1, source_target_pairs={{0,8},{4,12},{8,0},{12,4},{1,9},{5,13},{9,1},{13,5},{2,10},{6,14},... | collective-permute-start | bytes 196616 | tf_op jit(solution)/shard_map/ppermute | solution.py:380
  6.3 1.3 %collective-permute-start.1 = (bf16[128,256]{1,0:T(8,128)(2,1)S(1)}, bf16[128,256]{1,0:T(8,128)(2,1)S(1)}, u32[]{:S(2)}, u32[]{:S(2)}) collective-permute-start(bf16[128,256]{1,0:T(8,128)(2,1)S(1)} %get-tuple-element.13.refs_0_), channel_id=1, source_target_pairs={{0,12},{4,8},{8,4},{12,0},{1,13},{5,9},{9,5},{13,1},{2,14},{6,10},... | collective-permute-start | bytes 196616 | tf_op jit(solution)/shard_map/ppermute | solution.py:380
  7.7 0.2 collective-permute-start
  7.9 0.0 copy-done.6
  7.9 0.0 copy-done.5
  7.9 0.0 copy-done.3
  7.9 1.5 %prep.1 = (bf16[2,512,256]{2,1,0:T(8,128)(2,1)S(1)}, f32[33,8,128]{2,1,0:T(8,128)S(1)}) custom-call(f32[16,9]{1,0:T(8,128)S(1)} %copy-done.3, f32[16]{0:T(128)S(1)} %copy-done.5, f32[16]{0:T(128)S(1)} %copy-done.6), custom_call_target="tpu_custom_call" | custom-call | tf_op jit(solution)/shard_map/prep/pallas_call | solution.py:410
  9.4 0.6 %collective-permute-done.2.refs_3_ = bf16[128,256]{1,0:T(8,128)(2,1)S(1)} collective-permute-done((bf16[128,256]{1,0:T(8,128)(2,1)S(1)}, bf16[128,256]{1,0:T(8,128)(2,1)S(1)}, u32[]{:S(2)}, u32[]{:S(2)}) %collective-permute-start.2) | collective-permute-done | bytes 65568 | tf_op jit(solution)/shard_map/ppermute | solution.py:380
  10.1 2.5 %collective-permute-done.1.refs_2_ = bf16[128,256]{1,0:T(8,128)(2,1)S(1)} collective-permute-done((bf16[128,256]{1,0:T(8,128)(2,1)S(1)}, bf16[128,256]{1,0:T(8,128)(2,1)S(1)}, u32[]{:S(2)}, u32[]{:S(2)}) %collective-permute-start.1) | collective-permute-done | bytes 65568 | tf_op jit(solution)/shard_map/ppermute | solution.py:380
  12.5 0.1 collective-permute-done.refs_1_
  12.7 6.1 %heat.1 = (bf16[32,384]{1,0:T(8,128)(2,1)S(1)}, bf16[32,384]{1,0:T(8,128)(2,1)S(1)}, bf16[32,384]{1,0:T(8,128)(2,1)S(1)}, bf16[32,384]{1,0:T(8,128)(2,1)S(1)}) custom-call(bf16[128,256]{1,0:T(8,128)(2,1)S(1)} %get-tuple-element.13.refs_0_, bf16[128,256]{1,0:T(8,128)(2,1)S(1)} %collective-permute-done.refs_1_, ...), custom_call_target="tpu_custom_call" | custom-call | tf_op jit(solution)/shard_map/heat/pallas_call | solution.py:423
  18.8 0.8 %collective-permute-start.3 = (bf16[32,384]{1,0:T(8,128)(2,1)S(1)}, bf16[32,384]{1,0:T(8,128)(2,1)S(1)}, u32[]{:S(2)}, u32[]{:S(2)}) collective-permute-start(bf16[32,384]{1,0:T(8,128)(2,1)S(1)} %get-tuple-element.18), channel_id=1, source_target_pairs={{0,4},{4,8},{8,12},{12,0},{1,5},{5,9},{9,13},{13,1},{2,6},{6,10},{... | collective-permute-start | bytes 73736 | tf_op jit(solution)/shard_map/ppermute | solution.py:377
  19.6 2.8 %collective-permute-start.4 = (bf16[32,384]{1,0:T(8,128)(2,1)S(1)}, bf16[32,384]{1,0:T(8,128)(2,1)S(1)}, u32[]{:S(2)}, u32[]{:S(2)}) collective-permute-start(bf16[32,384]{1,0:T(8,128)(2,1)S(1)} %get-tuple-element.19), channel_id=1, source_target_pairs={{0,8},{4,12},{8,0},{12,4},{1,9},{5,13},{9,1},{13,5},{2,10},{6,14},... | collective-permute-start | bytes 73736 | tf_op jit(solution)/shard_map/ppermute | solution.py:377
  22.4 2.0 %collective-permute-start.5 = (bf16[32,384]{1,0:T(8,128)(2,1)S(1)}, bf16[32,384]{1,0:T(8,128)(2,1)S(1)}, u32[]{:S(2)}, u32[]{:S(2)}) collective-permute-start(bf16[32,384]{1,0:T(8,128)(2,1)S(1)} %get-tuple-element.20), channel_id=1, source_target_pairs={{0,12},{4,0},{8,4},{12,8},{1,13},{5,1},{9,5},{13,9},{2,14},{6,2},{... | collective-permute-start | bytes 73736 | tf_op jit(solution)/shard_map/ppermute | solution.py:377
  24.4 0.1 collective-permute-done.3.refs_1_
  24.6 0.3 %collective-permute-done.4.refs_2_ = bf16[32,384]{1,0:T(8,128)(2,1)S(1)} collective-permute-done((bf16[32,384]{1,0:T(8,128)(2,1)S(1)}, bf16[32,384]{1,0:T(8,128)(2,1)S(1)}, u32[]{:S(2)}, u32[]{:S(2)}) %collective-permute-start.4) | collective-permute-done | bytes 24608 | tf_op jit(solution)/shard_map/ppermute | solution.py:377
  24.9 1.4 %collective-permute-done.5.refs_3_ = bf16[32,384]{1,0:T(8,128)(2,1)S(1)} collective-permute-done((bf16[32,384]{1,0:T(8,128)(2,1)S(1)}, bf16[32,384]{1,0:T(8,128)(2,1)S(1)}, u32[]{:S(2)}, u32[]{:S(2)}) %collective-permute-start.5) | collective-permute-done | bytes 24608 | tf_op jit(solution)/shard_map/ppermute | solution.py:377
  26.2 0.0 copy-done
  26.2 0.0 copy-done.1
  26.2 0.0 copy-done.2
  26.2 0.0 copy-done.4
  26.3 1.3 %mix.1 = f32[3,4,32]{2,1,0:T(4,128)} custom-call(bf16[32,384]{1,0:T(8,128)(2,1)S(1)} %get-tuple-element.17.refs_0_, bf16[32,384]{1,0:T(8,128)(2,1)S(1)} %collective-permute-done.3.refs_1_, bf16[32,384]{1,0:T(8,128)(2,1)S(1)} %collective-permute-done.4.refs_2_, bf16[32,384]{1,0:T(8,128)(2,1)S(1)} %collective-permute-done.5.refs_3_, ...), custom_call_target="tpu_custom_call" | custom-call | tf_op jit(solution)/shard_map/mix/pallas_call | solution.py:449
Async XLA Ops:
  0.0 7.9 %copy-start.6 = (f32[16]{0:T(128)S(1)}, f32[16]{0:T(128)}, u32[]{:S(2)}) copy-start(f32[16]{0:T(128)} %head_ref.1) | copy-start | bytes 196
  0.0 7.9 %copy-start.5 = (f32[16]{0:T(128)S(1)}, f32[16]{0:T(128)}, u32[]{:S(2)}) copy-start(f32[16]{0:T(128)} %bias_ref.1) | copy-start | bytes 196
  0.0 7.9 %copy-start.3 = (f32[16,9]{1,0:T(8,128)S(1)}, f32[16,9]{1,0:T(8,128)}, u32[]{:S(2)}) copy-start(f32[16,9]{1,0:T(8,128)} %weight_ref.1) | copy-start | bytes 1732
  0.0 26.2 %copy-start = (bf16[256,1024]{1,0:T(8,128)(2,1)S(1)}, bf16[256,1024]{1,0:T(8,128)(2,1)}, u32[]{:S(2)}) copy-start(bf16[256,1024]{1,0:T(8,128)(2,1)} %refs_4_.1) | copy-start | bytes 1572868
  0.0 26.2 %copy-start.1 = (f32[3,1024]{1,0:T(4,128)S(1)}, f32[3,1024]{1,0:T(4,128)}, u32[]{:S(2)}) copy-start(f32[3,1024]{1,0:T(4,128)} %refs_5_.1) | copy-start | bytes 36868
  0.0 26.2 %copy-start.2 = (bf16[1024,3]{0,1:T(4,128)(2,1)S(1)}, bf16[1024,3]{0,1:T(4,128)(2,1)}, u32[]{:S(2)}) copy-start(bf16[1024,3]{0,1:T(4,128)(2,1)} %param.23) | copy-start | bytes 18436
  0.0 26.2 %copy-start.4 = (f32[1024]{0:T(1024)S(1)}, f32[1024]{0:T(1024)}, u32[]{:S(2)}) copy-start(f32[1024]{0:T(1024)} %param.22) | copy-start | bytes 12292
  2.2 7.9 %collective-permute-start.2 = (bf16[128,256]{1,0:T(8,128)(2,1)S(1)}, bf16[128,256]{1,0:T(8,128)(2,1)S(1)}, u32[]{:S(2)}, u32[]{:S(2)}) collective-permute-start(bf16[128,256]{1,0:T(8,128)(2,1)S(1)} %get-tuple-element.13.refs_0_), channel_id=1, source_target_pairs={{0,8},{4,12},{8,0},{12,4},{1,9},{5,13},{9,1},{13,5},{2,10},{6,14},... | collective-permute-start | bytes 196616 | tf_op jit(solution)/shard_map/ppermute | solution.py:380
  6.3 6.2 %collective-permute-start.1 = (bf16[128,256]{1,0:T(8,128)(2,1)S(1)}, bf16[128,256]{1,0:T(8,128)(2,1)S(1)}, u32[]{:S(2)}, u32[]{:S(2)}) collective-permute-start(bf16[128,256]{1,0:T(8,128)(2,1)S(1)} %get-tuple-element.13.refs_0_), channel_id=1, source_target_pairs={{0,12},{4,8},{8,4},{12,0},{1,13},{5,9},{9,5},{13,1},{2,14},{6,10},... | collective-permute-start | bytes 196616 | tf_op jit(solution)/shard_map/ppermute | solution.py:380
  7.7 5.0 %collective-permute-start = (bf16[128,256]{1,0:T(8,128)(2,1)S(1)}, bf16[128,256]{1,0:T(8,128)(2,1)S(1)}, u32[]{:S(2)}, u32[]{:S(2)}) collective-permute-start(bf16[128,256]{1,0:T(8,128)(2,1)S(1)} %get-tuple-element.13.refs_0_), channel_id=1, source_target_pairs={{0,4},{4,0},{8,12},{12,8},{1,5},{5,1},{9,13},{13,9},{2,6},{6,2},{1... | collective-permute-start | bytes 196616 | tf_op jit(solution)/shard_map/ppermute | solution.py:380
  18.8 5.8 %collective-permute-start.3 = (bf16[32,384]{1,0:T(8,128)(2,1)S(1)}, bf16[32,384]{1,0:T(8,128)(2,1)S(1)}, u32[]{:S(2)}, u32[]{:S(2)}) collective-permute-start(bf16[32,384]{1,0:T(8,128)(2,1)S(1)} %get-tuple-element.18), channel_id=1, source_target_pairs={{0,4},{4,8},{8,12},{12,0},{1,5},{5,9},{9,13},{13,1},{2,6},{6,10},{... | collective-permute-start | bytes 73736 | tf_op jit(solution)/shard_map/ppermute | solution.py:377
  19.6 5.3 %collective-permute-start.4 = (bf16[32,384]{1,0:T(8,128)(2,1)S(1)}, bf16[32,384]{1,0:T(8,128)(2,1)S(1)}, u32[]{:S(2)}, u32[]{:S(2)}) collective-permute-start(bf16[32,384]{1,0:T(8,128)(2,1)S(1)} %get-tuple-element.19), channel_id=1, source_target_pairs={{0,8},{4,12},{8,0},{12,4},{1,9},{5,13},{9,1},{13,5},{2,10},{6,14},... | collective-permute-start | bytes 73736 | tf_op jit(solution)/shard_map/ppermute | solution.py:377
  22.4 3.8 %collective-permute-start.5 = (bf16[32,384]{1,0:T(8,128)(2,1)S(1)}, bf16[32,384]{1,0:T(8,128)(2,1)S(1)}, u32[]{:S(2)}, u32[]{:S(2)}) collective-permute-start(bf16[32,384]{1,0:T(8,128)(2,1)S(1)} %get-tuple-element.20), channel_id=1, source_target_pairs={{0,12},{4,0},{8,4},{12,8},{1,13},{5,1},{9,5},{13,9},{2,14},{6,2},{... | collective-permute-start | bytes 73736 | tf_op jit(solution)/shard_map/ppermute | solution.py:377

commit v8 on v7

--- a/solution.py
+++ b/solution.py
@@ -157,17 +157,21 @@
 
     step = 512
 
-    def cost_step(n, carry):
-        at = pl.multiple_of(n * step, step)
-        cost = jnp.dot(maps_ref[pl.ds(at, step), :], turned_q, preferred_element_type=F32) * scale
-        to = pl.multiple_of(at + GRID_W, GRID_W)
+    def cost_step(n):
+        at = n * step
+        block = maps_ref[pl.ds(at, step), :]
+        if n < 2:
+            cost = jnp.dot(block, turned_q, preferred_element_type=F32) * scale
+        else:
+            cost = lax.dot_general(
+                query, block, (((1,), (1,)), ((), ())), preferred_element_type=F32
+            )
+            cost = cost.T * scale
+        to = at + GRID_W
         high = cost.astype(BF16)
         cost_ref[pl.ds(to, step), :] = cost
         high_ref[pl.ds(to, step), :] = high
         low_ref[pl.ds(to, step), :] = (cost - high.astype(F32)).astype(BF16)
-        return carry
-
-    lax.fori_loop(0, pixels // step, cost_step, 0, unroll=8)
 
     cols = GRID_W // TILE
     def window_step(j, best):
@@ -253,8 +257,13 @@
 
     zero = jnp.zeros((8, slots), F32)
     carry = (jnp.full((8, slots), -jnp.inf, F32), zero, [zero] * (GRID_W // 8))
+    cost_step(0)
+    cost_step(1)
     for c in range(GRID_H // CHUNK):
         carry = chunk_step(c, carry)
+        ahead_at = c // 2 + 2
+        if c % 2 == 0 and ahead_at < pixels // step:
+            cost_step(ahead_at)
     best, row_acc, col_acc = carry
     top_value = jnp.max(best, axis=0, keepdims=True)
     shrink = jnp.exp2(best - top_value)

time: 27.7 us -> 27.7 us (level)
  no operation moved by 1% of the time
where the time goes in v8:
time: 27.7 us; the launch traced here: 27.5 us
  starting transfers between devices  11.4 us (41%)
  Pallas kernels  11 us (40%)
  waiting for transfers between devices  5.02 us (18%)
    pallas_call x1, Pallas kernels, on_device(): pl.pallas_call(functools.partial(heat_kernel, frame_count, len(queries)),...  6.06 us
    ppermute x3, starting transfers between devices, swap(): return lax.ppermute(x, 'frame', [(i, i ^ m) for i in range(frame_count)])  5.72 us
    ppermute x3, starting transfers between devices, send(): return lax.ppermute(x, 'frame', pairs)  5.65 us
    ppermute x3, waiting for transfers between devices, swap(): return lax.ppermute(x, 'frame', [(i, i ^ m) for i in range(frame_count)])  3.24 us
    pallas_call x1, Pallas kernels, on_device(): pl.pallas_call(functools.partial(pick_kernel, frame_count, track_count),...  2.16 us
    ppermute x3, waiting for transfers between devices, send(): return lax.ppermute(x, 'frame', pairs)  1.78 us
    pallas_call x1, Pallas kernels, on_device(): pl.pallas_call(prep_kernel, name='prep', out_shape=(pltpu.VMEM((2, hid *...  1.48 us
    pallas_call x1, Pallas kernels, on_device(): pl.pallas_call(functools.partial(mix_kernel, frame_count), name='mix', ou...  1.34 us
  transfers between devices with their start and end apart: 6, of which 6 were waited for; matrix products, arithmetic and copies ran while one was open for 0% of the time, Pallas kernels for 5%

profile of v8, /device:TPU:0, one launch (start us, length us, event | category | flops | bytes accessed | tf_op | source)
XLA Modules:
  0.0 27.5 jit_solution(1848560489661751360)
XLA Ops:
  0.0 0.0 copy-start.6
  0.0 0.0 copy-start.5
  0.0 0.0 copy-start.3
  0.0 0.0 copy-start
  0.0 0.0 copy-start.1
  0.0 0.0 copy-start.2
  0.0 0.0 copy-start.4
  0.0 2.2 %pick.1 = (bf16[128,256]{1,0:T(8,128)(2,1)S(1)}, bf16[4096,256]{1,0:T(8,128)(2,1)S(1)}) custom-call(s32[1,512]{1,0:T(1,128)} %bitcast.11, s32[1,512]{1,0:T(1,128)} %bitcast.12, s32[1,512]{1,0:T(1,128)} %bitcast.13, s32[1,512]{1,0:T(1,128)} %bitcast.14, bf16[4096,256]{1,0:T(8,128)(2,1)} %bitcast.10), custom_call_target="tpu_custom_call" | custom-call | tf_op jit(solution)/shard_map/pick/pallas_call | solution.py:393
  2.2 4.1 %collective-permute-start.2 = (bf16[128,256]{1,0:T(8,128)(2,1)S(1)}, bf16[128,256]{1,0:T(8,128)(2,1)S(1)}, u32[]{:S(2)}, u32[]{:S(2)}) collective-permute-start(bf16[128,256]{1,0:T(8,128)(2,1)S(1)} %get-tuple-element.13.refs_0_), channel_id=1, source_target_pairs={{0,8},{4,12},{8,0},{12,4},{1,9},{5,13},{9,1},{13,5},{2,10},{6,14},... | collective-permute-start | bytes 196616 | tf_op jit(solution)/shard_map/ppermute | solution.py:389
  6.3 1.3 %collective-permute-start.1 = (bf16[128,256]{1,0:T(8,128)(2,1)S(1)}, bf16[128,256]{1,0:T(8,128)(2,1)S(1)}, u32[]{:S(2)}, u32[]{:S(2)}) collective-permute-start(bf16[128,256]{1,0:T(8,128)(2,1)S(1)} %get-tuple-element.13.refs_0_), channel_id=1, source_target_pairs={{0,12},{4,8},{8,4},{12,0},{1,13},{5,9},{9,5},{13,1},{2,14},{6,10},... | collective-permute-start | bytes 196616 | tf_op jit(solution)/shard_map/ppermute | solution.py:389
  7.7 0.2 collective-permute-start
  7.9 0.0 copy-done.6
  7.9 0.0 copy-done.5
  7.9 0.0 copy-done.3
  7.9 1.5 %prep.1 = (bf16[2,512,256]{2,1,0:T(8,128)(2,1)S(1)}, f32[33,8,128]{2,1,0:T(8,128)S(1)}) custom-call(f32[16,9]{1,0:T(8,128)S(1)} %copy-done.3, f32[16]{0:T(128)S(1)} %copy-done.5, f32[16]{0:T(128)S(1)} %copy-done.6), custom_call_target="tpu_custom_call" | custom-call | tf_op jit(solution)/shard_map/prep/pallas_call | solution.py:419
  9.4 0.6 %collective-permute-done.2.refs_3_ = bf16[128,256]{1,0:T(8,128)(2,1)S(1)} collective-permute-done((bf16[128,256]{1,0:T(8,128)(2,1)S(1)}, bf16[128,256]{1,0:T(8,128)(2,1)S(1)}, u32[]{:S(2)}, u32[]{:S(2)}) %collective-permute-start.2) | collective-permute-done | bytes 65568 | tf_op jit(solution)/shard_map/ppermute | solution.py:389
  10.1 2.5 %collective-permute-done.1.refs_2_ = bf16[128,256]{1,0:T(8,128)(2,1)S(1)} collective-permute-done((bf16[128,256]{1,0:T(8,128)(2,1)S(1)}, bf16[128,256]{1,0:T(8,128)(2,1)S(1)}, u32[]{:S(2)}, u32[]{:S(2)}) %collective-permute-start.1) | collective-permute-done | bytes 65568 | tf_op jit(solution)/shard_map/ppermute | solution.py:389
  12.5 0.1 collective-permute-done.refs_1_
  12.7 6.1 %heat.1 = (bf16[32,384]{1,0:T(8,128)(2,1)S(1)}, bf16[32,384]{1,0:T(8,128)(2,1)S(1)}, bf16[32,384]{1,0:T(8,128)(2,1)S(1)}, bf16[32,384]{1,0:T(8,128)(2,1)S(1)}) custom-call(bf16[128,256]{1,0:T(8,128)(2,1)S(1)} %get-tuple-element.13.refs_0_, bf16[128,256]{1,0:T(8,128)(2,1)S(1)} %collective-permute-done.refs_1_, ...), custom_call_target="tpu_custom_call" | custom-call | tf_op jit(solution)/shard_map/heat/pallas_call | solution.py:432
  18.7 0.8 %collective-permute-start.3 = (bf16[32,384]{1,0:T(8,128)(2,1)S(1)}, bf16[32,384]{1,0:T(8,128)(2,1)S(1)}, u32[]{:S(2)}, u32[]{:S(2)}) collective-permute-start(bf16[32,384]{1,0:T(8,128)(2,1)S(1)} %get-tuple-element.18), channel_id=1, source_target_pairs={{0,4},{4,8},{8,12},{12,0},{1,5},{5,9},{9,13},{13,1},{2,6},{6,10},{... | collective-permute-start | bytes 73736 | tf_op jit(solution)/shard_map/ppermute | solution.py:386
  19.5 2.8 %collective-permute-start.4 = (bf16[32,384]{1,0:T(8,128)(2,1)S(1)}, bf16[32,384]{1,0:T(8,128)(2,1)S(1)}, u32[]{:S(2)}, u32[]{:S(2)}) collective-permute-start(bf16[32,384]{1,0:T(8,128)(2,1)S(1)} %get-tuple-element.19), channel_id=1, source_target_pairs={{0,8},{4,12},{8,0},{12,4},{1,9},{5,13},{9,1},{13,5},{2,10},{6,14},... | collective-permute-start | bytes 73736 | tf_op jit(solution)/shard_map/ppermute | solution.py:386
  22.3 2.0 %collective-permute-start.5 = (bf16[32,384]{1,0:T(8,128)(2,1)S(1)}, bf16[32,384]{1,0:T(8,128)(2,1)S(1)}, u32[]{:S(2)}, u32[]{:S(2)}) collective-permute-start(bf16[32,384]{1,0:T(8,128)(2,1)S(1)} %get-tuple-element.20), channel_id=1, source_target_pairs={{0,12},{4,0},{8,4},{12,8},{1,13},{5,1},{9,5},{13,9},{2,14},{6,2},{... | collective-permute-start | bytes 73736 | tf_op jit(solution)/shard_map/ppermute | solution.py:386
  24.4 0.1 collective-permute-done.3.refs_1_
  24.5 0.3 collective-permute-done.4.refs_2_
  24.8 1.4 %collective-permute-done.5.refs_3_ = bf16[32,384]{1,0:T(8,128)(2,1)S(1)} collective-permute-done((bf16[32,384]{1,0:T(8,128)(2,1)S(1)}, bf16[32,384]{1,0:T(8,128)(2,1)S(1)}, u32[]{:S(2)}, u32[]{:S(2)}) %collective-permute-start.5) | collective-permute-done | bytes 24608 | tf_op jit(solution)/shard_map/ppermute | solution.py:386
  26.2 0.0 copy-done
  26.2 0.0 copy-done.1
  26.2 0.0 copy-done.2
  26.2 0.0 copy-done.4
  26.2 1.3 %mix.1 = f32[3,4,32]{2,1,0:T(4,128)} custom-call(bf16[32,384]{1,0:T(8,128)(2,1)S(1)} %get-tuple-element.17.refs_0_, bf16[32,384]{1,0:T(8,128)(2,1)S(1)} %collective-permute-done.3.refs_1_, bf16[32,384]{1,0:T(8,128)(2,1)S(1)} %collective-permute-done.4.refs_2_, bf16[32,384]{1,0:T(8,128)(2,1)S(1)} %collective-permute-done.5.refs_3_, ...), custom_call_target="tpu_custom_call" | custom-call | tf_op jit(solution)/shard_map/mix/pallas_call | solution.py:458
Async XLA Ops:
  0.0 7.9 %copy-start.6 = (f32[16]{0:T(128)S(1)}, f32[16]{0:T(128)}, u32[]{:S(2)}) copy-start(f32[16]{0:T(128)} %head_ref.1) | copy-start | bytes 196
  0.0 7.9 %copy-start.5 = (f32[16]{0:T(128)S(1)}, f32[16]{0:T(128)}, u32[]{:S(2)}) copy-start(f32[16]{0:T(128)} %bias_ref.1) | copy-start | bytes 196
  0.0 7.9 %copy-start.3 = (f32[16,9]{1,0:T(8,128)S(1)}, f32[16,9]{1,0:T(8,128)}, u32[]{:S(2)}) copy-start(f32[16,9]{1,0:T(8,128)} %weight_ref.1) | copy-start | bytes 1732
  0.0 26.2 %copy-start = (bf16[256,1024]{1,0:T(8,128)(2,1)S(1)}, bf16[256,1024]{1,0:T(8,128)(2,1)}, u32[]{:S(2)}) copy-start(bf16[256,1024]{1,0:T(8,128)(2,1)} %refs_4_.1) | copy-start | bytes 1572868
  0.0 26.2 %copy-start.1 = (f32[3,1024]{1,0:T(4,128)S(1)}, f32[3,1024]{1,0:T(4,128)}, u32[]{:S(2)}) copy-start(f32[3,1024]{1,0:T(4,128)} %refs_5_.1) | copy-start | bytes 36868
  0.0 26.2 %copy-start.2 = (bf16[1024,3]{0,1:T(4,128)(2,1)S(1)}, bf16[1024,3]{0,1:T(4,128)(2,1)}, u32[]{:S(2)}) copy-start(bf16[1024,3]{0,1:T(4,128)(2,1)} %param.23) | copy-start | bytes 18436
  0.0 26.2 %copy-start.4 = (f32[1024]{0:T(1024)S(1)}, f32[1024]{0:T(1024)}, u32[]{:S(2)}) copy-start(f32[1024]{0:T(1024)} %param.22) | copy-start | bytes 12292
  2.2 7.9 %collective-permute-start.2 = (bf16[128,256]{1,0:T(8,128)(2,1)S(1)}, bf16[128,256]{1,0:T(8,128)(2,1)S(1)}, u32[]{:S(2)}, u32[]{:S(2)}) collective-permute-start(bf16[128,256]{1,0:T(8,128)(2,1)S(1)} %get-tuple-element.13.refs_0_), channel_id=1, source_target_pairs={{0,8},{4,12},{8,0},{12,4},{1,9},{5,13},{9,1},{13,5},{2,10},{6,14},... | collective-permute-start | bytes 196616 | tf_op jit(solution)/shard_map/ppermute | solution.py:389
  6.3 6.2 %collective-permute-start.1 = (bf16[128,256]{1,0:T(8,128)(2,1)S(1)}, bf16[128,256]{1,0:T(8,128)(2,1)S(1)}, u32[]{:S(2)}, u32[]{:S(2)}) collective-permute-start(bf16[128,256]{1,0:T(8,128)(2,1)S(1)} %get-tuple-element.13.refs_0_), channel_id=1, source_target_pairs={{0,12},{4,8},{8,4},{12,0},{1,13},{5,9},{9,5},{13,1},{2,14},{6,10},... | collective-permute-start | bytes 196616 | tf_op jit(solution)/shard_map/ppermute | solution.py:389
  7.7 5.0 %collective-permute-start = (bf16[128,256]{1,0:T(8,128)(2,1)S(1)}, bf16[128,256]{1,0:T(8,128)(2,1)S(1)}, u32[]{:S(2)}, u32[]{:S(2)}) collective-permute-start(bf16[128,256]{1,0:T(8,128)(2,1)S(1)} %get-tuple-element.13.refs_0_), channel_id=1, source_target_pairs={{0,4},{4,0},{8,12},{12,8},{1,5},{5,1},{9,13},{13,9},{2,6},{6,2},{1... | collective-permute-start | bytes 196616 | tf_op jit(solution)/shard_map/ppermute | solution.py:389
  18.7 5.8 %collective-permute-start.3 = (bf16[32,384]{1,0:T(8,128)(2,1)S(1)}, bf16[32,384]{1,0:T(8,128)(2,1)S(1)}, u32[]{:S(2)}, u32[]{:S(2)}) collective-permute-start(bf16[32,384]{1,0:T(8,128)(2,1)S(1)} %get-tuple-element.18), channel_id=1, source_target_pairs={{0,4},{4,8},{8,12},{12,0},{1,5},{5,9},{9,13},{13,1},{2,6},{6,10},{... | collective-permute-start | bytes 73736 | tf_op jit(solution)/shard_map/ppermute | solution.py:386
  19.5 5.3 %collective-permute-start.4 = (bf16[32,384]{1,0:T(8,128)(2,1)S(1)}, bf16[32,384]{1,0:T(8,128)(2,1)S(1)}, u32[]{:S(2)}, u32[]{:S(2)}) collective-permute-start(bf16[32,384]{1,0:T(8,128)(2,1)S(1)} %get-tuple-element.19), channel_id=1, source_target_pairs={{0,8},{4,12},{8,0},{12,4},{1,9},{5,13},{9,1},{13,5},{2,10},{6,14},... | collective-permute-start | bytes 73736 | tf_op jit(solution)/shard_map/ppermute | solution.py:386
  22.3 3.8 %collective-permute-start.5 = (bf16[32,384]{1,0:T(8,128)(2,1)S(1)}, bf16[32,384]{1,0:T(8,128)(2,1)S(1)}, u32[]{:S(2)}, u32[]{:S(2)}) collective-permute-start(bf16[32,384]{1,0:T(8,128)(2,1)S(1)} %get-tuple-element.20), channel_id=1, source_target_pairs={{0,12},{4,0},{8,4},{12,8},{1,13},{5,1},{9,5},{13,9},{2,14},{6,2},{... | collective-permute-start | bytes 73736 | tf_op jit(solution)/shard_map/ppermute | solution.py:386

commit v9 on v8

--- a/solution.py
+++ b/solution.py
@@ -258,9 +258,10 @@
     zero = jnp.zeros((8, slots), F32)
     carry = (jnp.full((8, slots), -jnp.inf, F32), zero, [zero] * (GRID_W // 8))
     cost_step(0)
-    cost_step(1)
     for c in range(GRID_H // CHUNK):
         carry = chunk_step(c, carry)
+        if c == 0:
+            cost_step(1)
         ahead_at = c // 2 + 2
         if c % 2 == 0 and ahead_at < pixels // step:
             cost_step(ahead_at)

time: 27.7 us -> 27.8 us (level)
  no operation moved by 1% of the time
where the time goes in v9:
time: 27.8 us; the launch traced here: 27.7 us
  starting transfers between devices  11.4 us (41%)
  Pallas kernels  11.2 us (40%)
  waiting for transfers between devices  5.02 us (18%)
    pallas_call x1, Pallas kernels, on_device(): pl.pallas_call(functools.partial(heat_kernel, frame_count, len(queries)),...  6.19 us
    ppermute x3, starting transfers between devices, swap(): return lax.ppermute(x, 'frame', [(i, i ^ m) for i in range(frame_count)])  5.72 us
    ppermute x3, starting transfers between devices, send(): return lax.ppermute(x, 'frame', pairs)  5.65 us
    ppermute x3, waiting for transfers between devices, swap(): return lax.ppermute(x, 'frame', [(i, i ^ m) for i in range(frame_count)])  3.24 us
    pallas_call x1, Pallas kernels, on_device(): pl.pallas_call(functools.partial(pick_kernel, frame_count, track_count),...  2.16 us
    ppermute x3, waiting for transfers between devices, send(): return lax.ppermute(x, 'frame', pairs)  1.78 us
    pallas_call x1, Pallas kernels, on_device(): pl.pallas_call(prep_kernel, name='prep', out_shape=(pltpu.VMEM((2, hid *...  1.48 us
    pallas_call x1, Pallas kernels, on_device(): pl.pallas_call(functools.partial(mix_kernel, frame_count), name='mix', ou...  1.34 us
  transfers between devices with their start and end apart: 6, of which 6 were waited for; matrix products, arithmetic and copies ran while one was open for 0% of the time, Pallas kernels for 5%

profile of v9, /device:TPU:0, one launch (start us, length us, event | category | flops | bytes accessed | tf_op | source)
XLA Modules:
  0.0 27.7 jit_solution(6166626748928575188)
XLA Ops:
  0.0 0.0 copy-start.6
  0.0 0.0 copy-start.5
  0.0 0.0 copy-start.3
  0.0 0.0 copy-start
  0.0 0.0 copy-start.1
  0.0 0.0 copy-start.2
  0.0 0.0 copy-start.4
  0.0 2.2 %pick.1 = (bf16[128,256]{1,0:T(8,128)(2,1)S(1)}, bf16[4096,256]{1,0:T(8,128)(2,1)S(1)}) custom-call(s32[1,512]{1,0:T(1,128)} %bitcast.11, s32[1,512]{1,0:T(1,128)} %bitcast.12, s32[1,512]{1,0:T(1,128)} %bitcast.13, s32[1,512]{1,0:T(1,128)} %bitcast.14, bf16[4096,256]{1,0:T(8,128)(2,1)} %bitcast.10), custom_call_target="tpu_custom_call" | custom-call | tf_op jit(solution)/shard_map/pick/pallas_call | solution.py:394
  2.2 4.1 %collective-permute-start.2 = (bf16[128,256]{1,0:T(8,128)(2,1)S(1)}, bf16[128,256]{1,0:T(8,128)(2,1)S(1)}, u32[]{:S(2)}, u32[]{:S(2)}) collective-permute-start(bf16[128,256]{1,0:T(8,128)(2,1)S(1)} %get-tuple-element.13.refs_0_), channel_id=1, source_target_pairs={{0,8},{4,12},{8,0},{12,4},{1,9},{5,13},{9,1},{13,5},{2,10},{6,14},... | collective-permute-start | bytes 196616 | tf_op jit(solution)/shard_map/ppermute | solution.py:390
  6.3 1.3 %collective-permute-start.1 = (bf16[128,256]{1,0:T(8,128)(2,1)S(1)}, bf16[128,256]{1,0:T(8,128)(2,1)S(1)}, u32[]{:S(2)}, u32[]{:S(2)}) collective-permute-start(bf16[128,256]{1,0:T(8,128)(2,1)S(1)} %get-tuple-element.13.refs_0_), channel_id=1, source_target_pairs={{0,12},{4,8},{8,4},{12,0},{1,13},{5,9},{9,5},{13,1},{2,14},{6,10},... | collective-permute-start | bytes 196616 | tf_op jit(solution)/shard_map/ppermute | solution.py:390
  7.7 0.2 collective-permute-start
  7.9 0.0 copy-done.6
  7.9 0.0 copy-done.5
  7.9 0.0 copy-done.3
  7.9 1.5 %prep.1 = (bf16[2,512,256]{2,1,0:T(8,128)(2,1)S(1)}, f32[33,8,128]{2,1,0:T(8,128)S(1)}) custom-call(f32[16,9]{1,0:T(8,128)S(1)} %copy-done.3, f32[16]{0:T(128)S(1)} %copy-done.5, f32[16]{0:T(128)S(1)} %copy-done.6), custom_call_target="tpu_custom_call" | custom-call | tf_op jit(solution)/shard_map/prep/pallas_call | solution.py:420
  9.4 0.6 %collective-permute-done.2.refs_3_ = bf16[128,256]{1,0:T(8,128)(2,1)S(1)} collective-permute-done((bf16[128,256]{1,0:T(8,128)(2,1)S(1)}, bf16[128,256]{1,0:T(8,128)(2,1)S(1)}, u32[]{:S(2)}, u32[]{:S(2)}) %collective-permute-start.2) | collective-permute-done | bytes 65568 | tf_op jit(solution)/shard_map/ppermute | solution.py:390
  10.1 2.5 %collective-permute-done.1.refs_2_ = bf16[128,256]{1,0:T(8,128)(2,1)S(1)} collective-permute-done((bf16[128,256]{1,0:T(8,128)(2,1)S(1)}, bf16[128,256]{1,0:T(8,128)(2,1)S(1)}, u32[]{:S(2)}, u32[]{:S(2)}) %collective-permute-start.1) | collective-permute-done | bytes 65568 | tf_op jit(solution)/shard_map/ppermute | solution.py:390
  12.5 0.1 collective-permute-done.refs_1_
  12.7 6.2 %heat.1 = (bf16[32,384]{1,0:T(8,128)(2,1)S(1)}, bf16[32,384]{1,0:T(8,128)(2,1)S(1)}, bf16[32,384]{1,0:T(8,128)(2,1)S(1)}, bf16[32,384]{1,0:T(8,128)(2,1)S(1)}) custom-call(bf16[128,256]{1,0:T(8,128)(2,1)S(1)} %get-tuple-element.13.refs_0_, bf16[128,256]{1,0:T(8,128)(2,1)S(1)} %collective-permute-done.refs_1_, ...), custom_call_target="tpu_custom_call" | custom-call | tf_op jit(solution)/shard_map/heat/pallas_call | solution.py:433
  18.9 0.8 %collective-permute-start.3 = (bf16[32,384]{1,0:T(8,128)(2,1)S(1)}, bf16[32,384]{1,0:T(8,128)(2,1)S(1)}, u32[]{:S(2)}, u32[]{:S(2)}) collective-permute-start(bf16[32,384]{1,0:T(8,128)(2,1)S(1)} %get-tuple-element.18), channel_id=1, source_target_pairs={{0,4},{4,8},{8,12},{12,0},{1,5},{5,9},{9,13},{13,1},{2,6},{6,10},{... | collective-permute-start | bytes 73736 | tf_op jit(solution)/shard_map/ppermute | solution.py:387
  19.7 2.8 %collective-permute-start.4 = (bf16[32,384]{1,0:T(8,128)(2,1)S(1)}, bf16[32,384]{1,0:T(8,128)(2,1)S(1)}, u32[]{:S(2)}, u32[]{:S(2)}) collective-permute-start(bf16[32,384]{1,0:T(8,128)(2,1)S(1)} %get-tuple-element.19), channel_id=1, source_target_pairs={{0,8},{4,12},{8,0},{12,4},{1,9},{5,13},{9,1},{13,5},{2,10},{6,14},... | collective-permute-start | bytes 73736 | tf_op jit(solution)/shard_map/ppermute | solution.py:387
  22.5 2.0 %collective-permute-start.5 = (bf16[32,384]{1,0:T(8,128)(2,1)S(1)}, bf16[32,384]{1,0:T(8,128)(2,1)S(1)}, u32[]{:S(2)}, u32[]{:S(2)}) collective-permute-start(bf16[32,384]{1,0:T(8,128)(2,1)S(1)} %get-tuple-element.20), channel_id=1, source_target_pairs={{0,12},{4,0},{8,4},{12,8},{1,13},{5,1},{9,5},{13,9},{2,14},{6,2},{... | collective-permute-start | bytes 73736 | tf_op jit(solution)/shard_map/ppermute | solution.py:387
  24.5 0.1 collective-permute-done.3.refs_1_
  24.6 0.3 collective-permute-done.4.refs_2_
  24.9 1.4 %collective-permute-done.5.refs_3_ = bf16[32,384]{1,0:T(8,128)(2,1)S(1)} collective-permute-done((bf16[32,384]{1,0:T(8,128)(2,1)S(1)}, bf16[32,384]{1,0:T(8,128)(2,1)S(1)}, u32[]{:S(2)}, u32[]{:S(2)}) %collective-permute-start.5) | collective-permute-done | bytes 24608 | tf_op jit(solution)/shard_map/ppermute | solution.py:387
  26.3 0.0 copy-done
  26.3 0.0 copy-done.1
  26.3 0.0 copy-done.2
  26.3 0.0 copy-done.4
  26.3 1.3 %mix.1 = f32[3,4,32]{2,1,0:T(4,128)} custom-call(bf16[32,384]{1,0:T(8,128)(2,1)S(1)} %get-tuple-element.17.refs_0_, bf16[32,384]{1,0:T(8,128)(2,1)S(1)} %collective-permute-done.3.refs_1_, bf16[32,384]{1,0:T(8,128)(2,1)S(1)} %collective-permute-done.4.refs_2_, bf16[32,384]{1,0:T(8,128)(2,1)S(1)} %collective-permute-done.5.refs_3_, ...), custom_call_target="tpu_custom_call" | custom-call | tf_op jit(solution)/shard_map/mix/pallas_call | solution.py:459
Async XLA Ops:
  0.0 7.9 %copy-start.6 = (f32[16]{0:T(128)S(1)}, f32[16]{0:T(128)}, u32[]{:S(2)}) copy-start(f32[16]{0:T(128)} %head_ref.1) | copy-start | bytes 196
  0.0 7.9 %copy-start.5 = (f32[16]{0:T(128)S(1)}, f32[16]{0:T(128)}, u32[]{:S(2)}) copy-start(f32[16]{0:T(128)} %bias_ref.1) | copy-start | bytes 196
  0.0 7.9 %copy-start.3 = (f32[16,9]{1,0:T(8,128)S(1)}, f32[16,9]{1,0:T(8,128)}, u32[]{:S(2)}) copy-start(f32[16,9]{1,0:T(8,128)} %weight_ref.1) | copy-start | bytes 1732
  0.0 26.3 %copy-start = (bf16[256,1024]{1,0:T(8,128)(2,1)S(1)}, bf16[256,1024]{1,0:T(8,128)(2,1)}, u32[]{:S(2)}) copy-start(bf16[256,1024]{1,0:T(8,128)(2,1)} %refs_4_.1) | copy-start | bytes 1572868
  0.0 26.3 %copy-start.1 = (f32[3,1024]{1,0:T(4,128)S(1)}, f32[3,1024]{1,0:T(4,128)}, u32[]{:S(2)}) copy-start(f32[3,1024]{1,0:T(4,128)} %refs_5_.1) | copy-start | bytes 36868
  0.0 26.3 %copy-start.2 = (bf16[1024,3]{0,1:T(4,128)(2,1)S(1)}, bf16[1024,3]{0,1:T(4,128)(2,1)}, u32[]{:S(2)}) copy-start(bf16[1024,3]{0,1:T(4,128)(2,1)} %param.23) | copy-start | bytes 18436
  0.0 26.3 %copy-start.4 = (f32[1024]{0:T(1024)S(1)}, f32[1024]{0:T(1024)}, u32[]{:S(2)}) copy-start(f32[1024]{0:T(1024)} %param.22) | copy-start | bytes 12292
  2.2 7.9 %collective-permute-start.2 = (bf16[128,256]{1,0:T(8,128)(2,1)S(1)}, bf16[128,256]{1,0:T(8,128)(2,1)S(1)}, u32[]{:S(2)}, u32[]{:S(2)}) collective-permute-start(bf16[128,256]{1,0:T(8,128)(2,1)S(1)} %get-tuple-element.13.refs_0_), channel_id=1, source_target_pairs={{0,8},{4,12},{8,0},{12,4},{1,9},{5,13},{9,1},{13,5},{2,10},{6,14},... | collective-permute-start | bytes 196616 | tf_op jit(solution)/shard_map/ppermute | solution.py:390
  6.3 6.2 %collective-permute-start.1 = (bf16[128,256]{1,0:T(8,128)(2,1)S(1)}, bf16[128,256]{1,0:T(8,128)(2,1)S(1)}, u32[]{:S(2)}, u32[]{:S(2)}) collective-permute-start(bf16[128,256]{1,0:T(8,128)(2,1)S(1)} %get-tuple-element.13.refs_0_), channel_id=1, source_target_pairs={{0,12},{4,8},{8,4},{12,0},{1,13},{5,9},{9,5},{13,1},{2,14},{6,10},... | collective-permute-start | bytes 196616 | tf_op jit(solution)/shard_map/ppermute | solution.py:390
  7.7 5.0 %collective-permute-start = (bf16[128,256]{1,0:T(8,128)(2,1)S(1)}, bf16[128,256]{1,0:T(8,128)(2,1)S(1)}, u32[]{:S(2)}, u32[]{:S(2)}) collective-permute-start(bf16[128,256]{1,0:T(8,128)(2,1)S(1)} %get-tuple-element.13.refs_0_), channel_id=1, source_target_pairs={{0,4},{4,0},{8,12},{12,8},{1,5},{5,1},{9,13},{13,9},{2,6},{6,2},{1... | collective-permute-start | bytes 196616 | tf_op jit(solution)/shard_map/ppermute | solution.py:390
  18.9 5.8 %collective-permute-start.3 = (bf16[32,384]{1,0:T(8,128)(2,1)S(1)}, bf16[32,384]{1,0:T(8,128)(2,1)S(1)}, u32[]{:S(2)}, u32[]{:S(2)}) collective-permute-start(bf16[32,384]{1,0:T(8,128)(2,1)S(1)} %get-tuple-element.18), channel_id=1, source_target_pairs={{0,4},{4,8},{8,12},{12,0},{1,5},{5,9},{9,13},{13,1},{2,6},{6,10},{... | collective-permute-start | bytes 73736 | tf_op jit(solution)/shard_map/ppermute | solution.py:387
  19.7 5.3 %collective-permute-start.4 = (bf16[32,384]{1,0:T(8,128)(2,1)S(1)}, bf16[32,384]{1,0:T(8,128)(2,1)S(1)}, u32[]{:S(2)}, u32[]{:S(2)}) collective-permute-start(bf16[32,384]{1,0:T(8,128)(2,1)S(1)} %get-tuple-element.19), channel_id=1, source_target_pairs={{0,8},{4,12},{8,0},{12,4},{1,9},{5,13},{9,1},{13,5},{2,10},{6,14},... | collective-permute-start | bytes 73736 | tf_op jit(solution)/shard_map/ppermute | solution.py:387
  22.5 3.8 %collective-permute-start.5 = (bf16[32,384]{1,0:T(8,128)(2,1)S(1)}, bf16[32,384]{1,0:T(8,128)(2,1)S(1)}, u32[]{:S(2)}, u32[]{:S(2)}) collective-permute-start(bf16[32,384]{1,0:T(8,128)(2,1)S(1)} %get-tuple-element.20), channel_id=1, source_target_pairs={{0,12},{4,0},{8,4},{12,8},{1,13},{5,1},{9,5},{13,9},{2,14},{6,2},{... | collective-permute-start | bytes 73736 | tf_op jit(solution)/shard_map/ppermute | solution.py:387
